TPU v7x, 32 devices: a whole 2x2x4 slice. The times are simulated.
32 devices in a mesh: tm: 4 (over z), sx: 4 (over y, x), sy: 2 (over core).
Axes of the slice: x: 2, y: 2, z: 4, core: 2. Of those that a mesh axis runs over, the one named last changes fastest.
Arguments:
- state_guess: float32 [4, 2, 256, 512], P('tm', None, 'sx', 'sy'), may hold values from -6 to 6
- adjoint_guess: float32 [4, 2, 256, 512], P('tm', None, 'sx', 'sy'), may hold values from -6 to 6
- diffusivity: float32 [256, 512], P('sx', 'sy'), may hold values from 0.25 to 2
- decay_rate: float32 [256, 512], P('sx', 'sy'), may hold values from 0.003 to 0.1
- coupling: float32 [256, 512], P('sx', 'sy'), may hold values from -0.7 to 0.7
- control: float32 [2, 256, 512], P(None, 'sx', 'sy'), may hold values from -6 to 6
- target: float32 [2, 256, 512], P(None, 'sx', 'sy'), may hold values from -6 to 6
Outputs:
- state_points: float32 [4, 2, 256, 512], P('tm', None, 'sx', 'sy')
- adjoint_points: float32 [4, 2, 256, 512], P('tm', None, 'sx', 'sy')
- gradient: float32 [256, 512], P('sx', 'sy')
All inputs are finite; a program needn't handle non-finite values.
Results may differ from a plain program's by a relative error of at most 0.00002.
Values sent between devices are 32-bit elements; how exact they have to be, the bound alone decides.
No kernel may reach another device: no remote copies, remote signals or barrier semaphores. Data moves between devices by JAX's collectives and lax.ppermute only.
A program may use at most 128 MiB of HBM per device.

v0:
```python
import jax
import jax.numpy as jnp
from jax import lax
from jax.sharding import PartitionSpec as P

STEPS = 8


TIME_STEP = 0.1
DIFFUSION_FIRST = 1.0
DIFFUSION_SECOND = 0.4
NEIGHBOURS = ((0, 1), (2, 1), (1, 0), (1, 2))


def extended(cells, sides, width):
    for axis, dim in sides:
        count = lax.axis_size(axis)
        ends = count - 1
        head = lax.slice_in_dim(cells, 0, width, axis=dim)
        tail = lax.slice_in_dim(cells, cells.shape[dim] - width, cells.shape[dim], axis=dim)
        cells = jnp.concatenate(
            [
                lax.ppermute(tail, axis, [(i, (i + 1) % count) for i in range(ends)]),
                cells,
                lax.ppermute(head, axis, [((i + 1) % count, i) for i in range(ends)]),
            ],
            axis=dim,
        )
    return cells


def prefix(part, axis, combine, identity, reverse):
    count = lax.axis_size(axis)
    place = lax.axis_index(axis)
    ahead = count - 1 - place if reverse else place
    gathered = jax.tree.map(lambda a: lax.all_gather(a, axis), part)
    state = jax.tree.map(lambda a, e: jnp.zeros_like(a) + jnp.asarray(e, a.dtype), part, identity)

    def one(turn, state):
        source = count - 1 - turn if reverse else turn
        return combine(
            state, jax.tree.map(lambda a: lax.dynamic_index_in_dim(a, source, 0, False), gathered)
        )

    return lax.fori_loop(0, ahead, one, state)


def shifted_2(block, axis, distance):
    devices = range(lax.axis_size(axis))
    route = [(i - distance, i) for i in devices if i - distance in devices]
    return lax.ppermute(block, axis, route)


def stepped(padded, kappa_pad, decay_rate, coupling, source):
    height = padded.shape[-2] - 2
    width = padded.shape[-1] - 2
    centre = padded[..., 1:-1, 1:-1]
    kappa_mid = kappa_pad[1:-1, 1:-1]
    summed = jnp.zeros(centre.shape, jnp.float32)
    for a, b in NEIGHBOURS:
        summed = summed + 0.5 * (kappa_mid + kappa_pad[a : a + height, b : b + width]) * (
            padded[..., a : a + height, b : b + width] - centre
        )
    first = centre[..., 0, :, :]
    second = centre[..., 1, :, :]
    new_first = first + TIME_STEP * (
        DIFFUSION_FIRST * summed[..., 0, :, :] + decay_rate * (coupling * second - first)
    )
    new_second = second + TIME_STEP * (
        DIFFUSION_SECOND * summed[..., 1, :, :] + decay_rate * (coupling * first - 2.0 * second)
    )
    result = jnp.stack([new_first, new_second], axis=-3)
    if source is not None:
        result = result + TIME_STEP * source
    return result


def face_product(state_pad, adjoint_pad):
    height = state_pad.shape[-2] - 2
    width = state_pad.shape[-1] - 2
    state_mid = state_pad[..., 1:-1, 1:-1]
    adjoint_mid = adjoint_pad[..., 1:-1, 1:-1]
    summed = jnp.zeros(state_mid.shape, jnp.float32)
    for a, b in NEIGHBOURS:
        summed = summed + (state_pad[..., a : a + height, b : b + width] - state_mid) * (
            adjoint_mid - adjoint_pad[..., a : a + height, b : b + width]
        )
    return (
        TIME_STEP
        * 0.5
        * (DIFFUSION_FIRST * summed[..., 0, :, :] + DIFFUSION_SECOND * summed[..., 1, :, :])
    )


def local(state_guess, adjoint_guess, diffusivity, decay_rate, coupling, control, target):
    tile_rows = diffusivity.shape[0]
    tile_cols = diffusivity.shape[1]
    slab_count = lax.axis_size("tm")
    position = lax.axis_index("tm")
    kappa_pad = extended(diffusivity, (("sx", 0), ("sy", 1)), 1)

    def relaxation(start, source):
        history = []
        field = start
        for k in range(STEPS):
            padded = extended(field, (("sx", 1), ("sy", 2)), 1)
            history.append(padded)
            field = stepped(padded, kappa_pad, decay_rate, coupling, source)
        return (history, field)

    factor = STEPS * TIME_STEP * decay_rate
    g_diag_one = 1.0 - factor
    g_side = factor * coupling
    g_diag_two = 1.0 - 2.0 * factor

    def propagate(diag_one, side, diag_two, vector):
        return jnp.stack(
            [diag_one * vector[0] + side * vector[1], side * vector[0] + diag_two * vector[1]]
        )

    def combine(earlier, latter):
        early_map, early_shift = earlier
        late_map, late_shift = latter
        product = jnp.stack(
            [
                late_map[0] * early_map[0] + late_map[1] * early_map[2],
                late_map[0] * early_map[1] + late_map[1] * early_map[3],
                late_map[2] * early_map[0] + late_map[3] * early_map[2],
                late_map[2] * early_map[1] + late_map[3] * early_map[3],
            ]
        )
        shifted = jnp.stack(
            [
                late_map[0] * early_shift[0] + late_map[1] * early_shift[1],
                late_map[2] * early_shift[0] + late_map[3] * early_shift[1],
            ]
        )
        return (product, shifted + late_shift)

    coarse_map = jnp.stack([g_diag_one, g_side, g_side, g_diag_two])
    ones_grid = jnp.ones_like(diffusivity)
    zeros_grid = jnp.zeros_like(diffusivity)
    identity_map = jnp.stack([ones_grid, zeros_grid, zeros_grid, ones_grid])

    def coarse_chain(residual, backward):
        _, carried = prefix(
            (coarse_map, residual),
            "tm",
            combine,
            (identity_map, jnp.zeros_like(residual)),
            backward,
        )
        return carried

    state_start = state_guess[0]
    _, state_end = relaxation(state_start, control)
    previous_end = shifted_2(state_end, "tm", 1)
    state_residual = jnp.where(position > 0, previous_end - state_start, -state_start)
    state_before = coarse_chain(state_residual, False)
    state_points = (
        state_start + propagate(g_diag_one, g_side, g_diag_two, state_before) + state_residual
    )
    state_history, final = relaxation(state_points, control)
    adjoint_start = adjoint_guess[0]
    _, adjoint_end = relaxation(adjoint_start, None)
    next_end = shifted_2(adjoint_end, "tm", -1)
    adjoint_residual = jnp.where(
        position < slab_count - 1, next_end - adjoint_start, final - target - adjoint_start
    )
    adjoint_after = coarse_chain(adjoint_residual, True)
    adjoint_points = (
        adjoint_start + propagate(g_diag_one, g_side, g_diag_two, adjoint_after) + adjoint_residual
    )
    adjoint_history, _ = relaxation(adjoint_points, None)
    local_gradient = jnp.zeros((tile_rows, tile_cols), jnp.float32)
    for k in range(STEPS):
        local_gradient = local_gradient + face_product(
            state_history[STEPS - 1 - k], adjoint_history[k]
        )
    gradient = lax.psum(local_gradient, "tm")
    return (state_points[None], adjoint_points[None], gradient)


def solution(mesh):
    placed = (
        P("tm", None, "sx", "sy"),
        P("tm", None, "sx", "sy"),
        P("sx", "sy"),
        P("sx", "sy"),
        P("sx", "sy"),
        P(None, "sx", "sy"),
        P(None, "sx", "sy"),
    )
    return jax.shard_map(
        local,
        mesh=mesh,
        in_specs=placed,
        out_specs=(P("tm", None, "sx", "sy"), P("tm", None, "sx", "sy"), P("sx", "sy")),
        check_vma=False,
    )
```

profile of v0, /device:TPU:0, one launch (start us, length us, event | category | flops | bytes accessed | tf_op | source)
XLA Modules:
  0.0 533.7 jit_solution(16832647258904404908)
XLA Ops:
  7.9 4.8 collective-permute-start
  14.8 4.5 collective-permute-start.1
  24.4 4.9 collective-permute-start.37
  31.1 2.7 collective-permute-start.5
  38.8 5.4 %collective-permute-start.8 = (f32[2,1,256]{2,1,0:T(1,128)S(1)}, f32[2,1,256]{2,1,0:T(1,128)S(1)}, u32[]{:S(2)}, u32[]{:S(2)}) collective-permute-start(f32[2,1,256]{2,1,0:T(1,128)S(1)} %get-tuple-element.364), channel_id=1, source_target_pairs={{0,2},{2,4},{4,6},{1,3},{3,5},{5,7},{8,10},{10,12},{12,14},{9,11},... | collective-permute-start | bytes 6152 | tf_op jit(solution)/shard_map/ppermute | solution.py:23
  55.3 5.2 collective-permute-start.12
  61.8 5.2 collective-permute-start.41
  71.3 2.1 collective-permute-done.42
  78.2 4.9 collective-permute-start.16
  84.4 5.4 %collective-permute-start.45 = (f32[2,1,256]{2,1,0:T(1,128)S(1)}, f32[2,1,256]{2,1,0:T(1,128)S(1)}, u32[]{:S(2)}, u32[]{:S(2)}) collective-permute-start(f32[2,1,256]{2,1,0:T(1,128)S(1)} %get-tuple-element.326), channel_id=1, source_target_pairs={{0,2},{2,4},{4,6},{1,3},{3,5},{5,7},{8,10},{10,12},{12,14},{9,11},... | collective-permute-start | bytes 6152 | tf_op jit(solution)/shard_map/ppermute | solution.py:23
  94.1 2.1 collective-permute-done.46
  101.1 4.9 collective-permute-start.20
  107.3 5.4 %collective-permute-start.49 = (f32[2,1,256]{2,1,0:T(1,128)S(1)}, f32[2,1,256]{2,1,0:T(1,128)S(1)}, u32[]{:S(2)}, u32[]{:S(2)}) collective-permute-start(f32[2,1,256]{2,1,0:T(1,128)S(1)} %get-tuple-element.322), channel_id=1, source_target_pairs={{0,2},{2,4},{4,6},{1,3},{3,5},{5,7},{8,10},{10,12},{12,14},{9,11},... | collective-permute-start | bytes 6152 | tf_op jit(solution)/shard_map/ppermute | solution.py:23
  117.0 2.1 collective-permute-done.50
  124.0 4.9 collective-permute-start.24
  130.2 5.4 %collective-permute-start.53 = (f32[2,1,256]{2,1,0:T(1,128)S(1)}, f32[2,1,256]{2,1,0:T(1,128)S(1)}, u32[]{:S(2)}, u32[]{:S(2)}) collective-permute-start(f32[2,1,256]{2,1,0:T(1,128)S(1)} %get-tuple-element.318), channel_id=1, source_target_pairs={{0,2},{2,4},{4,6},{1,3},{3,5},{5,7},{8,10},{10,12},{12,14},{9,11},... | collective-permute-start | bytes 6152 | tf_op jit(solution)/shard_map/ppermute | solution.py:23
  139.9 2.1 collective-permute-done.54
  146.9 4.9 collective-permute-start.28
  153.1 5.4 %collective-permute-start.57 = (f32[2,1,256]{2,1,0:T(1,128)S(1)}, f32[2,1,256]{2,1,0:T(1,128)S(1)}, u32[]{:S(2)}, u32[]{:S(2)}) collective-permute-start(f32[2,1,256]{2,1,0:T(1,128)S(1)} %get-tuple-element.314), channel_id=1, source_target_pairs={{0,2},{2,4},{4,6},{1,3},{3,5},{5,7},{8,10},{10,12},{12,14},{9,11},... | collective-permute-start | bytes 6152 | tf_op jit(solution)/shard_map/ppermute | solution.py:23
  162.8 2.1 collective-permute-done.58
  169.8 4.9 collective-permute-start.32
  176.0 5.4 %collective-permute-start.61 = (f32[2,1,256]{2,1,0:T(1,128)S(1)}, f32[2,1,256]{2,1,0:T(1,128)S(1)}, u32[]{:S(2)}, u32[]{:S(2)}) collective-permute-start(f32[2,1,256]{2,1,0:T(1,128)S(1)} %get-tuple-element.310), channel_id=1, source_target_pairs={{0,2},{2,4},{4,6},{1,3},{3,5},{5,7},{8,10},{10,12},{12,14},{9,11},... | collective-permute-start | bytes 6152 | tf_op jit(solution)/shard_map/ppermute | solution.py:23
  185.7 2.1 collective-permute-done.62
  193.5 4.9 collective-permute-start.65
  199.7 5.1 collective-permute-done.66
  207.5 3.5 collective-permute-start.36
  211.1 6.4 %collective-permute-done.36 = f32[2,64,256]{2,1,0:T(8,128)S(1)} collective-permute-done((f32[2,64,256]{2,1,0:T(8,128)S(1)}, f32[2,64,256]{2,1,0:T(8,128)S(1)}, u32[]{:S(2)}, u32[]{:S(2)}) %collective-permute-start.36) | collective-permute-done | bytes 131104 | tf_op jit(solution)/shard_map/ppermute | solution.py:51
  217.6 20.1 %all-gather.1 = f32[8,64,256]{2,1,0:T(8,128)S(1)} all-gather(f32[2,64,256]{2,1,0:T(8,128)S(1)} %negate_select_fusion), channel_id=3, replica_groups=mesh['tm'=4,'sx'=4,'sy'=2] {'tm'}, dimensions={0}, use_global_device_ids=true | all-gather | bytes 655360 | tf_op jit(solution)/shard_map/all_gather | solution.py:36
  239.1 5.4 %collective-permute-start.70 = (f32[2,1,256]{2,1,0:T(1,128)S(1)}, f32[2,1,256]{2,1,0:T(1,128)S(1)}, u32[]{:S(2)}, u32[]{:S(2)}) collective-permute-start(f32[2,1,256]{2,1,0:T(1,128)S(1)} %get-tuple-element.351), channel_id=1, source_target_pairs={{0,2},{2,4},{4,6},{1,3},{3,5},{5,7},{8,10},{10,12},{12,14},{9,11},... | collective-permute-start | bytes 6152 | tf_op jit(solution)/shard_map/ppermute | solution.py:23
  247.2 3.0 collective-permute-start.72
  252.7 5.4 %collective-permute-start.74 = (f32[2,1,256]{2,1,0:T(1,128)S(1)}, f32[2,1,256]{2,1,0:T(1,128)S(1)}, u32[]{:S(2)}, u32[]{:S(2)}) collective-permute-start(f32[2,1,256]{2,1,0:T(1,128)S(1)} %get-tuple-element.349), channel_id=1, source_target_pairs={{0,2},{2,4},{4,6},{1,3},{3,5},{5,7},{8,10},{10,12},{12,14},{9,11},... | collective-permute-start | bytes 6152 | tf_op jit(solution)/shard_map/ppermute | solution.py:23
  260.9 3.0 collective-permute-start.76
  266.4 5.7 %collective-permute-start.78 = (f32[2,1,256]{2,1,0:T(1,128)S(1)}, f32[2,1,256]{2,1,0:T(1,128)S(1)}, u32[]{:S(2)}, u32[]{:S(2)}) collective-permute-start(f32[2,1,256]{2,1,0:T(1,128)S(1)} %get-tuple-element.347), channel_id=1, source_target_pairs={{0,2},{2,4},{4,6},{1,3},{3,5},{5,7},{8,10},{10,12},{12,14},{9,11},... | collective-permute-start | bytes 6152 | tf_op jit(solution)/shard_map/ppermute | solution.py:23
  274.8 3.0 collective-permute-start.80
  280.3 5.7 %collective-permute-start.82 = (f32[2,1,256]{2,1,0:T(1,128)S(1)}, f32[2,1,256]{2,1,0:T(1,128)S(1)}, u32[]{:S(2)}, u32[]{:S(2)}) collective-permute-start(f32[2,1,256]{2,1,0:T(1,128)S(1)} %get-tuple-element.345), channel_id=1, source_target_pairs={{0,2},{2,4},{4,6},{1,3},{3,5},{5,7},{8,10},{10,12},{12,14},{9,11},... | collective-permute-start | bytes 6152 | tf_op jit(solution)/shard_map/ppermute | solution.py:23
  288.7 3.2 collective-permute-start.84
  294.2 5.7 %collective-permute-start.86 = (f32[2,1,256]{2,1,0:T(1,128)S(1)}, f32[2,1,256]{2,1,0:T(1,128)S(1)}, u32[]{:S(2)}, u32[]{:S(2)}) collective-permute-start(f32[2,1,256]{2,1,0:T(1,128)S(1)} %get-tuple-element.343), channel_id=1, source_target_pairs={{0,2},{2,4},{4,6},{1,3},{3,5},{5,7},{8,10},{10,12},{12,14},{9,11},... | collective-permute-start | bytes 6152 | tf_op jit(solution)/shard_map/ppermute | solution.py:23
  302.6 3.0 collective-permute-start.88
  308.1 5.7 %collective-permute-start.90 = (f32[2,1,256]{2,1,0:T(1,128)S(1)}, f32[2,1,256]{2,1,0:T(1,128)S(1)}, u32[]{:S(2)}, u32[]{:S(2)}) collective-permute-start(f32[2,1,256]{2,1,0:T(1,128)S(1)} %get-tuple-element.341), channel_id=1, source_target_pairs={{0,2},{2,4},{4,6},{1,3},{3,5},{5,7},{8,10},{10,12},{12,14},{9,11},... | collective-permute-start | bytes 6152 | tf_op jit(solution)/shard_map/ppermute | solution.py:23
  316.5 3.0 collective-permute-start.92
  322.0 5.7 %collective-permute-start.94 = (f32[2,1,256]{2,1,0:T(1,128)S(1)}, f32[2,1,256]{2,1,0:T(1,128)S(1)}, u32[]{:S(2)}, u32[]{:S(2)}) collective-permute-start(f32[2,1,256]{2,1,0:T(1,128)S(1)} %get-tuple-element.339), channel_id=1, source_target_pairs={{0,2},{2,4},{4,6},{1,3},{3,5},{5,7},{8,10},{10,12},{12,14},{9,11},... | collective-permute-start | bytes 6152 | tf_op jit(solution)/shard_map/ppermute | solution.py:23
  330.4 3.0 collective-permute-start.96
  335.9 5.7 %collective-permute-start.98 = (f32[2,1,256]{2,1,0:T(1,128)S(1)}, f32[2,1,256]{2,1,0:T(1,128)S(1)}, u32[]{:S(2)}, u32[]{:S(2)}) collective-permute-start(f32[2,1,256]{2,1,0:T(1,128)S(1)} %get-tuple-element.337), channel_id=1, source_target_pairs={{0,2},{2,4},{4,6},{1,3},{3,5},{5,7},{8,10},{10,12},{12,14},{9,11},... | collective-permute-start | bytes 6152 | tf_op jit(solution)/shard_map/ppermute | solution.py:23
  344.3 3.0 collective-permute-start.100
  348.9 6.2 %collective-permute-done.69 = f32[2,64,256]{2,1,0:T(8,128)S(1)} collective-permute-done((f32[2,64,256]{2,1,0:T(8,128)S(1)}, f32[2,64,256]{2,1,0:T(8,128)S(1)}, u32[]{:S(2)}, u32[]{:S(2)}) %collective-permute-start.69) | collective-permute-done | bytes 131104 | tf_op jit(solution)/shard_map/ppermute | solution.py:51
  355.2 17.5 %all-gather.2 = f32[8,64,256]{2,1,0:T(8,128)S(1)} all-gather(f32[2,64,256]{2,1,0:T(8,128)S(1)} %fusion.256), channel_id=4, replica_groups=mesh['tm'=4,'sx'=4,'sy'=2] {'tm'}, dimensions={0}, use_global_device_ids=true | all-gather | bytes 655360 | tf_op jit(solution)/shard_map/all_gather | solution.py:36
  372.7 3.1 while.27
  375.9 5.1 collective-permute-start.102
  382.3 5.3 collective-permute-done.103
  393.7 5.4 %collective-permute-start.106 = (f32[2,1,256]{2,1,0:T(1,128)S(1)}, f32[2,1,256]{2,1,0:T(1,128)S(1)}, u32[]{:S(2)}, u32[]{:S(2)}) collective-permute-start(f32[2,1,256]{2,1,0:T(1,128)S(1)} %get-tuple-element.300), channel_id=1, source_target_pairs={{0,2},{2,4},{4,6},{1,3},{3,5},{5,7},{8,10},{10,12},{12,14},{9,11},... | collective-permute-start | bytes 6152 | tf_op jit(solution)/shard_map/ppermute | solution.py:23
  401.9 3.0 collective-permute-start.108
  407.3 5.4 %collective-permute-start.110 = (f32[2,1,256]{2,1,0:T(1,128)S(1)}, f32[2,1,256]{2,1,0:T(1,128)S(1)}, u32[]{:S(2)}, u32[]{:S(2)}) collective-permute-start(f32[2,1,256]{2,1,0:T(1,128)S(1)} %get-tuple-element.298), channel_id=1, source_target_pairs={{0,2},{2,4},{4,6},{1,3},{3,5},{5,7},{8,10},{10,12},{12,14},{9,11},... | collective-permute-start | bytes 6152 | tf_op jit(solution)/shard_map/ppermute | solution.py:23
  415.5 3.0 collective-permute-start.112
  420.9 5.7 %collective-permute-start.114 = (f32[2,1,256]{2,1,0:T(1,128)S(1)}, f32[2,1,256]{2,1,0:T(1,128)S(1)}, u32[]{:S(2)}, u32[]{:S(2)}) collective-permute-start(f32[2,1,256]{2,1,0:T(1,128)S(1)} %get-tuple-element.296), channel_id=1, source_target_pairs={{0,2},{2,4},{4,6},{1,3},{3,5},{5,7},{8,10},{10,12},{12,14},{9,11},... | collective-permute-start | bytes 6152 | tf_op jit(solution)/shard_map/ppermute | solution.py:23
  429.3 3.0 collective-permute-start.116
  434.8 5.7 %collective-permute-start.118 = (f32[2,1,256]{2,1,0:T(1,128)S(1)}, f32[2,1,256]{2,1,0:T(1,128)S(1)}, u32[]{:S(2)}, u32[]{:S(2)}) collective-permute-start(f32[2,1,256]{2,1,0:T(1,128)S(1)} %get-tuple-element.294), channel_id=1, source_target_pairs={{0,2},{2,4},{4,6},{1,3},{3,5},{5,7},{8,10},{10,12},{12,14},{9,11},... | collective-permute-start | bytes 6152 | tf_op jit(solution)/shard_map/ppermute | solution.py:23
  443.3 3.0 collective-permute-start.120
  448.7 5.7 %collective-permute-start.122 = (f32[2,1,256]{2,1,0:T(1,128)S(1)}, f32[2,1,256]{2,1,0:T(1,128)S(1)}, u32[]{:S(2)}, u32[]{:S(2)}) collective-permute-start(f32[2,1,256]{2,1,0:T(1,128)S(1)} %get-tuple-element.292), channel_id=1, source_target_pairs={{0,2},{2,4},{4,6},{1,3},{3,5},{5,7},{8,10},{10,12},{12,14},{9,11},... | collective-permute-start | bytes 6152 | tf_op jit(solution)/shard_map/ppermute | solution.py:23
  457.2 3.0 collective-permute-start.124
  462.7 5.7 %collective-permute-start.126 = (f32[2,1,256]{2,1,0:T(1,128)S(1)}, f32[2,1,256]{2,1,0:T(1,128)S(1)}, u32[]{:S(2)}, u32[]{:S(2)}) collective-permute-start(f32[2,1,256]{2,1,0:T(1,128)S(1)} %get-tuple-element.290), channel_id=1, source_target_pairs={{0,2},{2,4},{4,6},{1,3},{3,5},{5,7},{8,10},{10,12},{12,14},{9,11},... | collective-permute-start | bytes 6152 | tf_op jit(solution)/shard_map/ppermute | solution.py:23
  471.1 3.0 collective-permute-start.128
  475.3 5.1 collective-permute-start.130
  482.0 5.0 collective-permute-done.131
  492.6 32.8 %all-reduce.2.cloned.1.call-done = f32[64,256]{1,0:T(8,128)} async-done(((f32[64,256]{1,0:T(8,128)}), f32[64,256]{1,0:T(8,128)}) %all-reduce.2.cloned.1.call-update) | async-done | bytes 65552 | tf_op jit(solution)/shard_map/psum | solution.py:180
  (475 shorter events, 181.1 us)
Async XLA Ops:
  7.2 230.5 %all-gather.5.cloned.1.call-start = ((), (), s32[]{:S(2)}) async-start(), calls=%async_computation.1 | async-start | bytes 1310720 | tf_op jit(solution)/shard_map/all_gather | solution.py:36
  7.9 12.9 %collective-permute-start = (f32[1,256]{1,0:T(1,128)S(1)}, f32[1,256]{1,0:T(1,128)S(1)}, u32[]{:S(2)}, u32[]{:S(2)}) collective-permute-start(f32[1,256]{1,0:T(1,128)S(1)} %get-tuple-element.376), channel_id=1, source_target_pairs={{0,2},{2,4},{4,6},{1,3},{3,5},{5,7},{8,10},{10,12},{12,14},{9,11},... | collective-permute-start | bytes 3080 | tf_op jit(solution)/shard_map/ppermute | solution.py:23
  12.8 8.0 %collective-permute-start.2 = (f32[1,256]{1,0:T(1,128)S(1)}, f32[1,256]{1,0:T(1,128)S(1)}, u32[]{:S(2)}, u32[]{:S(2)}) collective-permute-start(f32[1,256]{1,0:T(1,128)S(1)} %get-tuple-element.377), channel_id=1, source_target_pairs={{2,0},{4,2},{6,4},{3,1},{5,3},{7,5},{10,8},{12,10},{14,12},{11,9},... | collective-permute-start | bytes 3080 | tf_op jit(solution)/shard_map/ppermute | solution.py:25
  14.8 16.1 %collective-permute-start.1 = (f32[2,1,256]{2,1,0:T(1,128)S(1)}, f32[2,1,256]{2,1,0:T(1,128)S(1)}, u32[]{:S(2)}, u32[]{:S(2)}) collective-permute-start(f32[2,1,256]{2,1,0:T(1,128)S(1)} %get-tuple-element.366), channel_id=1, source_target_pairs={{0,2},{2,4},{4,6},{1,3},{3,5},{5,7},{8,10},{10,12},{12,14},{9,11},... | collective-permute-start | bytes 6152 | tf_op jit(solution)/shard_map/ppermute | solution.py:23
  19.4 11.6 %collective-permute-start.3 = (f32[2,1,256]{2,1,0:T(1,128)S(1)}, f32[2,1,256]{2,1,0:T(1,128)S(1)}, u32[]{:S(2)}, u32[]{:S(2)}) collective-permute-start(f32[2,1,256]{2,1,0:T(1,128)S(1)} %get-tuple-element.367), channel_id=1, source_target_pairs={{2,0},{4,2},{6,4},{3,1},{5,3},{7,5},{10,8},{12,10},{14,12},{11,9},... | collective-permute-start | bytes 6152 | tf_op jit(solution)/shard_map/ppermute | solution.py:25
  21.8 7.6 %collective-permute-start.4 = (f32[66,1]{1,0:T(8,128)S(1)}, f32[66,1]{1,0:T(8,128)S(1)}, u32[]{:S(2)}, u32[]{:S(2)}) collective-permute-start(f32[66,1]{1,0:T(8,128)S(1)} %get-tuple-element.368), channel_id=1, source_target_pairs={{0,1},{2,3},{4,5},{6,7},{8,9},{10,11},{12,13},{14,15},{16,17},{18,... | collective-permute-start | bytes 800 | tf_op jit(solution)/shard_map/ppermute | solution.py:23
  23.1 7.7 %collective-permute-start.6 = (f32[66,1]{1,0:T(8,128)S(1)}, f32[66,1]{1,0:T(8,128)S(1)}, u32[]{:S(2)}, u32[]{:S(2)}) collective-permute-start(f32[66,1]{1,0:T(8,128)S(1)} %get-tuple-element.369), channel_id=1, source_target_pairs={{1,0},{3,2},{5,4},{7,6},{9,8},{11,10},{13,12},{15,14},{17,16},{19,... | collective-permute-start | bytes 800 | tf_op jit(solution)/shard_map/ppermute | solution.py:25
  24.4 10.7 %collective-permute-start.37 = (f32[2,1,256]{2,1,0:T(1,128)S(1)}, f32[2,1,256]{2,1,0:T(1,128)S(1)}, u32[]{:S(2)}, u32[]{:S(2)}) collective-permute-start(f32[2,1,256]{2,1,0:T(1,128)S(1)} %get-tuple-element.334), channel_id=1, source_target_pairs={{0,2},{2,4},{4,6},{1,3},{3,5},{5,7},{8,10},{10,12},{12,14},{9,11},... | collective-permute-start | bytes 6152 | tf_op jit(solution)/shard_map/ppermute | solution.py:23
  38.8 9.9 %collective-permute-start.8 = (f32[2,1,256]{2,1,0:T(1,128)S(1)}, f32[2,1,256]{2,1,0:T(1,128)S(1)}, u32[]{:S(2)}, u32[]{:S(2)}) collective-permute-start(f32[2,1,256]{2,1,0:T(1,128)S(1)} %get-tuple-element.364), channel_id=1, source_target_pairs={{0,2},{2,4},{4,6},{1,3},{3,5},{5,7},{8,10},{10,12},{12,14},{9,11},... | collective-permute-start | bytes 6152 | tf_op jit(solution)/shard_map/ppermute | solution.py:23
  45.6 7.6 %collective-permute-start.39 = (f32[2,66,1]{2,1,0:T(8,128)S(1)}, f32[2,66,1]{2,1,0:T(8,128)S(1)}, u32[]{:S(2)}, u32[]{:S(2)}) collective-permute-start(f32[2,66,1]{2,1,0:T(8,128)S(1)} %get-tuple-element.253), channel_id=1, source_target_pairs={{0,1},{2,3},{4,5},{6,7},{8,9},{10,11},{12,13},{14,15},{16,17},{18,... | collective-permute-start | bytes 1592 | tf_op jit(solution)/shard_map/ppermute | solution.py:23
  55.3 13.0 %collective-permute-start.12 = (f32[2,1,256]{2,1,0:T(1,128)S(1)}, f32[2,1,256]{2,1,0:T(1,128)S(1)}, u32[]{:S(2)}, u32[]{:S(2)}) collective-permute-start(f32[2,1,256]{2,1,0:T(1,128)S(1)} %get-tuple-element.362), channel_id=1, source_target_pairs={{0,2},{2,4},{4,6},{1,3},{3,5},{5,7},{8,10},{10,12},{12,14},{9,11},... | collective-permute-start | bytes 6152 | tf_op jit(solution)/shard_map/ppermute | solution.py:23
  60.5 7.8 %collective-permute-start.13 = (f32[2,1,256]{2,1,0:T(1,128)S(1)}, f32[2,1,256]{2,1,0:T(1,128)S(1)}, u32[]{:S(2)}, u32[]{:S(2)}) collective-permute-start(f32[2,1,256]{2,1,0:T(1,128)S(1)} %get-tuple-element.363), channel_id=1, source_target_pairs={{2,0},{4,2},{6,4},{3,1},{5,3},{7,5},{10,8},{12,10},{14,12},{11,9},... | collective-permute-start | bytes 6152 | tf_op jit(solution)/shard_map/ppermute | solution.py:25
  61.8 9.4 %collective-permute-start.41 = (f32[2,1,256]{2,1,0:T(1,128)S(1)}, f32[2,1,256]{2,1,0:T(1,128)S(1)}, u32[]{:S(2)}, u32[]{:S(2)}) collective-permute-start(f32[2,1,256]{2,1,0:T(1,128)S(1)} %get-tuple-element.330), channel_id=1, source_target_pairs={{0,2},{2,4},{4,6},{1,3},{3,5},{5,7},{8,10},{10,12},{12,14},{9,11},... | collective-permute-start | bytes 6152 | tf_op jit(solution)/shard_map/ppermute | solution.py:23
  68.4 7.7 %collective-permute-start.14 = (f32[2,66,1]{2,1,0:T(8,128)S(1)}, f32[2,66,1]{2,1,0:T(8,128)S(1)}, u32[]{:S(2)}, u32[]{:S(2)}) collective-permute-start(f32[2,66,1]{2,1,0:T(8,128)S(1)} %get-tuple-element.281), channel_id=1, source_target_pairs={{0,1},{2,3},{4,5},{6,7},{8,9},{10,11},{12,13},{14,15},{16,17},{18,... | collective-permute-start | bytes 1592 | tf_op jit(solution)/shard_map/ppermute | solution.py:23
  78.2 12.9 %collective-permute-start.16 = (f32[2,1,256]{2,1,0:T(1,128)S(1)}, f32[2,1,256]{2,1,0:T(1,128)S(1)}, u32[]{:S(2)}, u32[]{:S(2)}) collective-permute-start(f32[2,1,256]{2,1,0:T(1,128)S(1)} %get-tuple-element.360), channel_id=1, source_target_pairs={{0,2},{2,4},{4,6},{1,3},{3,5},{5,7},{8,10},{10,12},{12,14},{9,11},... | collective-permute-start | bytes 6152 | tf_op jit(solution)/shard_map/ppermute | solution.py:23
  83.1 8.1 %collective-permute-start.17 = (f32[2,1,256]{2,1,0:T(1,128)S(1)}, f32[2,1,256]{2,1,0:T(1,128)S(1)}, u32[]{:S(2)}, u32[]{:S(2)}) collective-permute-start(f32[2,1,256]{2,1,0:T(1,128)S(1)} %get-tuple-element.361), channel_id=1, source_target_pairs={{2,0},{4,2},{6,4},{3,1},{5,3},{7,5},{10,8},{12,10},{14,12},{11,9},... | collective-permute-start | bytes 6152 | tf_op jit(solution)/shard_map/ppermute | solution.py:25
  84.4 9.7 %collective-permute-start.45 = (f32[2,1,256]{2,1,0:T(1,128)S(1)}, f32[2,1,256]{2,1,0:T(1,128)S(1)}, u32[]{:S(2)}, u32[]{:S(2)}) collective-permute-start(f32[2,1,256]{2,1,0:T(1,128)S(1)} %get-tuple-element.326), channel_id=1, source_target_pairs={{0,2},{2,4},{4,6},{1,3},{3,5},{5,7},{8,10},{10,12},{12,14},{9,11},... | collective-permute-start | bytes 6152 | tf_op jit(solution)/shard_map/ppermute | solution.py:23
  91.3 7.7 %collective-permute-start.18 = (f32[2,66,1]{2,1,0:T(8,128)S(1)}, f32[2,66,1]{2,1,0:T(8,128)S(1)}, u32[]{:S(2)}, u32[]{:S(2)}) collective-permute-start(f32[2,66,1]{2,1,0:T(8,128)S(1)} %get-tuple-element.279), channel_id=1, source_target_pairs={{0,1},{2,3},{4,5},{6,7},{8,9},{10,11},{12,13},{14,15},{16,17},{18,... | collective-permute-start | bytes 1592 | tf_op jit(solution)/shard_map/ppermute | solution.py:23
  101.1 12.9 %collective-permute-start.20 = (f32[2,1,256]{2,1,0:T(1,128)S(1)}, f32[2,1,256]{2,1,0:T(1,128)S(1)}, u32[]{:S(2)}, u32[]{:S(2)}) collective-permute-start(f32[2,1,256]{2,1,0:T(1,128)S(1)} %get-tuple-element.358), channel_id=1, source_target_pairs={{0,2},{2,4},{4,6},{1,3},{3,5},{5,7},{8,10},{10,12},{12,14},{9,11},... | collective-permute-start | bytes 6152 | tf_op jit(solution)/shard_map/ppermute | solution.py:23
  106.0 8.1 %collective-permute-start.21 = (f32[2,1,256]{2,1,0:T(1,128)S(1)}, f32[2,1,256]{2,1,0:T(1,128)S(1)}, u32[]{:S(2)}, u32[]{:S(2)}) collective-permute-start(f32[2,1,256]{2,1,0:T(1,128)S(1)} %get-tuple-element.359), channel_id=1, source_target_pairs={{2,0},{4,2},{6,4},{3,1},{5,3},{7,5},{10,8},{12,10},{14,12},{11,9},... | collective-permute-start | bytes 6152 | tf_op jit(solution)/shard_map/ppermute | solution.py:25
  107.3 9.7 %collective-permute-start.49 = (f32[2,1,256]{2,1,0:T(1,128)S(1)}, f32[2,1,256]{2,1,0:T(1,128)S(1)}, u32[]{:S(2)}, u32[]{:S(2)}) collective-permute-start(f32[2,1,256]{2,1,0:T(1,128)S(1)} %get-tuple-element.322), channel_id=1, source_target_pairs={{0,2},{2,4},{4,6},{1,3},{3,5},{5,7},{8,10},{10,12},{12,14},{9,11},... | collective-permute-start | bytes 6152 | tf_op jit(solution)/shard_map/ppermute | solution.py:23
  114.2 7.7 %collective-permute-start.22 = (f32[2,66,1]{2,1,0:T(8,128)S(1)}, f32[2,66,1]{2,1,0:T(8,128)S(1)}, u32[]{:S(2)}, u32[]{:S(2)}) collective-permute-start(f32[2,66,1]{2,1,0:T(8,128)S(1)} %get-tuple-element.277), channel_id=1, source_target_pairs={{0,1},{2,3},{4,5},{6,7},{8,9},{10,11},{12,13},{14,15},{16,17},{18,... | collective-permute-start | bytes 1592 | tf_op jit(solution)/shard_map/ppermute | solution.py:23
  124.0 12.9 %collective-permute-start.24 = (f32[2,1,256]{2,1,0:T(1,128)S(1)}, f32[2,1,256]{2,1,0:T(1,128)S(1)}, u32[]{:S(2)}, u32[]{:S(2)}) collective-permute-start(f32[2,1,256]{2,1,0:T(1,128)S(1)} %get-tuple-element.356), channel_id=1, source_target_pairs={{0,2},{2,4},{4,6},{1,3},{3,5},{5,7},{8,10},{10,12},{12,14},{9,11},... | collective-permute-start | bytes 6152 | tf_op jit(solution)/shard_map/ppermute | solution.py:23
  128.9 8.1 %collective-permute-start.25 = (f32[2,1,256]{2,1,0:T(1,128)S(1)}, f32[2,1,256]{2,1,0:T(1,128)S(1)}, u32[]{:S(2)}, u32[]{:S(2)}) collective-permute-start(f32[2,1,256]{2,1,0:T(1,128)S(1)} %get-tuple-element.357), channel_id=1, source_target_pairs={{2,0},{4,2},{6,4},{3,1},{5,3},{7,5},{10,8},{12,10},{14,12},{11,9},... | collective-permute-start | bytes 6152 | tf_op jit(solution)/shard_map/ppermute | solution.py:25
  130.2 9.7 %collective-permute-start.53 = (f32[2,1,256]{2,1,0:T(1,128)S(1)}, f32[2,1,256]{2,1,0:T(1,128)S(1)}, u32[]{:S(2)}, u32[]{:S(2)}) collective-permute-start(f32[2,1,256]{2,1,0:T(1,128)S(1)} %get-tuple-element.318), channel_id=1, source_target_pairs={{0,2},{2,4},{4,6},{1,3},{3,5},{5,7},{8,10},{10,12},{12,14},{9,11},... | collective-permute-start | bytes 6152 | tf_op jit(solution)/shard_map/ppermute | solution.py:23
  137.1 7.7 %collective-permute-start.26 = (f32[2,66,1]{2,1,0:T(8,128)S(1)}, f32[2,66,1]{2,1,0:T(8,128)S(1)}, u32[]{:S(2)}, u32[]{:S(2)}) collective-permute-start(f32[2,66,1]{2,1,0:T(8,128)S(1)} %get-tuple-element.275), channel_id=1, source_target_pairs={{0,1},{2,3},{4,5},{6,7},{8,9},{10,11},{12,13},{14,15},{16,17},{18,... | collective-permute-start | bytes 1592 | tf_op jit(solution)/shard_map/ppermute | solution.py:23
  146.9 12.9 %collective-permute-start.28 = (f32[2,1,256]{2,1,0:T(1,128)S(1)}, f32[2,1,256]{2,1,0:T(1,128)S(1)}, u32[]{:S(2)}, u32[]{:S(2)}) collective-permute-start(f32[2,1,256]{2,1,0:T(1,128)S(1)} %get-tuple-element.354), channel_id=1, source_target_pairs={{0,2},{2,4},{4,6},{1,3},{3,5},{5,7},{8,10},{10,12},{12,14},{9,11},... | collective-permute-start | bytes 6152 | tf_op jit(solution)/shard_map/ppermute | solution.py:23
  151.8 8.1 %collective-permute-start.29 = (f32[2,1,256]{2,1,0:T(1,128)S(1)}, f32[2,1,256]{2,1,0:T(1,128)S(1)}, u32[]{:S(2)}, u32[]{:S(2)}) collective-permute-start(f32[2,1,256]{2,1,0:T(1,128)S(1)} %get-tuple-element.355), channel_id=1, source_target_pairs={{2,0},{4,2},{6,4},{3,1},{5,3},{7,5},{10,8},{12,10},{14,12},{11,9},... | collective-permute-start | bytes 6152 | tf_op jit(solution)/shard_map/ppermute | solution.py:25
  153.1 9.7 %collective-permute-start.57 = (f32[2,1,256]{2,1,0:T(1,128)S(1)}, f32[2,1,256]{2,1,0:T(1,128)S(1)}, u32[]{:S(2)}, u32[]{:S(2)}) collective-permute-start(f32[2,1,256]{2,1,0:T(1,128)S(1)} %get-tuple-element.314), channel_id=1, source_target_pairs={{0,2},{2,4},{4,6},{1,3},{3,5},{5,7},{8,10},{10,12},{12,14},{9,11},... | collective-permute-start | bytes 6152 | tf_op jit(solution)/shard_map/ppermute | solution.py:23
  160.0 7.7 %collective-permute-start.30 = (f32[2,66,1]{2,1,0:T(8,128)S(1)}, f32[2,66,1]{2,1,0:T(8,128)S(1)}, u32[]{:S(2)}, u32[]{:S(2)}) collective-permute-start(f32[2,66,1]{2,1,0:T(8,128)S(1)} %get-tuple-element.273), channel_id=1, source_target_pairs={{0,1},{2,3},{4,5},{6,7},{8,9},{10,11},{12,13},{14,15},{16,17},{18,... | collective-permute-start | bytes 1592 | tf_op jit(solution)/shard_map/ppermute | solution.py:23
  169.8 12.9 %collective-permute-start.32 = (f32[2,1,256]{2,1,0:T(1,128)S(1)}, f32[2,1,256]{2,1,0:T(1,128)S(1)}, u32[]{:S(2)}, u32[]{:S(2)}) collective-permute-start(f32[2,1,256]{2,1,0:T(1,128)S(1)} %get-tuple-element.352), channel_id=1, source_target_pairs={{0,2},{2,4},{4,6},{1,3},{3,5},{5,7},{8,10},{10,12},{12,14},{9,11},... | collective-permute-start | bytes 6152 | tf_op jit(solution)/shard_map/ppermute | solution.py:23
  174.7 8.1 %collective-permute-start.33 = (f32[2,1,256]{2,1,0:T(1,128)S(1)}, f32[2,1,256]{2,1,0:T(1,128)S(1)}, u32[]{:S(2)}, u32[]{:S(2)}) collective-permute-start(f32[2,1,256]{2,1,0:T(1,128)S(1)} %get-tuple-element.353), channel_id=1, source_target_pairs={{2,0},{4,2},{6,4},{3,1},{5,3},{7,5},{10,8},{12,10},{14,12},{11,9},... | collective-permute-start | bytes 6152 | tf_op jit(solution)/shard_map/ppermute | solution.py:25
  176.0 9.7 %collective-permute-start.61 = (f32[2,1,256]{2,1,0:T(1,128)S(1)}, f32[2,1,256]{2,1,0:T(1,128)S(1)}, u32[]{:S(2)}, u32[]{:S(2)}) collective-permute-start(f32[2,1,256]{2,1,0:T(1,128)S(1)} %get-tuple-element.310), channel_id=1, source_target_pairs={{0,2},{2,4},{4,6},{1,3},{3,5},{5,7},{8,10},{10,12},{12,14},{9,11},... | collective-permute-start | bytes 6152 | tf_op jit(solution)/shard_map/ppermute | solution.py:23
  182.9 7.7 %collective-permute-start.34 = (f32[2,66,1]{2,1,0:T(8,128)S(1)}, f32[2,66,1]{2,1,0:T(8,128)S(1)}, u32[]{:S(2)}, u32[]{:S(2)}) collective-permute-start(f32[2,66,1]{2,1,0:T(8,128)S(1)} %get-tuple-element.271), channel_id=1, source_target_pairs={{0,1},{2,3},{4,5},{6,7},{8,9},{10,11},{12,13},{14,15},{16,17},{18,... | collective-permute-start | bytes 1592 | tf_op jit(solution)/shard_map/ppermute | solution.py:23
  193.4 332.0 %all-reduce.2.cloned.1.call-start = ((), (), s32[]{:S(2)}) async-start(), calls=%async_computation | async-start | bytes 131072 | tf_op jit(solution)/shard_map/psum | solution.py:180
  207.5 10.1 %collective-permute-start.36 = (f32[2,64,256]{2,1,0:T(8,128)S(1)}, f32[2,64,256]{2,1,0:T(8,128)S(1)}, u32[]{:S(2)}, u32[]{:S(2)}) collective-permute-start(f32[2,64,256]{2,1,0:T(8,128)S(1)} %maximum_add_fusion.9), channel_id=1, source_target_pairs={{0,8},{8,16},{16,24},{1,9},{9,17},{17,25},{2,10},{10,18},{18,26},{... | collective-permute-start | bytes 393224 | tf_op jit(solution)/shard_map/ppermute | solution.py:51
  237.8 6.7 %collective-permute-start.71 = (f32[2,1,256]{2,1,0:T(1,128)S(1)}, f32[2,1,256]{2,1,0:T(1,128)S(1)}, u32[]{:S(2)}, u32[]{:S(2)}) collective-permute-start(f32[2,1,256]{2,1,0:T(1,128)S(1)} %get-tuple-element.350), channel_id=1, source_target_pairs={{2,0},{4,2},{6,4},{3,1},{5,3},{7,5},{10,8},{12,10},{14,12},{11,9},... | collective-permute-start | bytes 6152 | tf_op jit(solution)/shard_map/ppermute | solution.py:25
  251.4 6.8 %collective-permute-start.75 = (f32[2,1,256]{2,1,0:T(1,128)S(1)}, f32[2,1,256]{2,1,0:T(1,128)S(1)}, u32[]{:S(2)}, u32[]{:S(2)}) collective-permute-start(f32[2,1,256]{2,1,0:T(1,128)S(1)} %get-tuple-element.348), channel_id=1, source_target_pairs={{2,0},{4,2},{6,4},{3,1},{5,3},{7,5},{10,8},{12,10},{14,12},{11,9},... | collective-permute-start | bytes 6152 | tf_op jit(solution)/shard_map/ppermute | solution.py:25
  252.7 6.7 %collective-permute-start.74 = (f32[2,1,256]{2,1,0:T(1,128)S(1)}, f32[2,1,256]{2,1,0:T(1,128)S(1)}, u32[]{:S(2)}, u32[]{:S(2)}) collective-permute-start(f32[2,1,256]{2,1,0:T(1,128)S(1)} %get-tuple-element.349), channel_id=1, source_target_pairs={{0,2},{2,4},{4,6},{1,3},{3,5},{5,7},{8,10},{10,12},{12,14},{9,11},... | collective-permute-start | bytes 6152 | tf_op jit(solution)/shard_map/ppermute | solution.py:23
  265.1 7.0 %collective-permute-start.79 = (f32[2,1,256]{2,1,0:T(1,128)S(1)}, f32[2,1,256]{2,1,0:T(1,128)S(1)}, u32[]{:S(2)}, u32[]{:S(2)}) collective-permute-start(f32[2,1,256]{2,1,0:T(1,128)S(1)} %get-tuple-element.346), channel_id=1, source_target_pairs={{2,0},{4,2},{6,4},{3,1},{5,3},{7,5},{10,8},{12,10},{14,12},{11,9},... | collective-permute-start | bytes 6152 | tf_op jit(solution)/shard_map/ppermute | solution.py:25
  266.4 7.0 %collective-permute-start.78 = (f32[2,1,256]{2,1,0:T(1,128)S(1)}, f32[2,1,256]{2,1,0:T(1,128)S(1)}, u32[]{:S(2)}, u32[]{:S(2)}) collective-permute-start(f32[2,1,256]{2,1,0:T(1,128)S(1)} %get-tuple-element.347), channel_id=1, source_target_pairs={{0,2},{2,4},{4,6},{1,3},{3,5},{5,7},{8,10},{10,12},{12,14},{9,11},... | collective-permute-start | bytes 6152 | tf_op jit(solution)/shard_map/ppermute | solution.py:23
  279.0 7.0 %collective-permute-start.83 = (f32[2,1,256]{2,1,0:T(1,128)S(1)}, f32[2,1,256]{2,1,0:T(1,128)S(1)}, u32[]{:S(2)}, u32[]{:S(2)}) collective-permute-start(f32[2,1,256]{2,1,0:T(1,128)S(1)} %get-tuple-element.344), channel_id=1, source_target_pairs={{2,0},{4,2},{6,4},{3,1},{5,3},{7,5},{10,8},{12,10},{14,12},{11,9},... | collective-permute-start | bytes 6152 | tf_op jit(solution)/shard_map/ppermute | solution.py:25
  280.3 7.0 %collective-permute-start.82 = (f32[2,1,256]{2,1,0:T(1,128)S(1)}, f32[2,1,256]{2,1,0:T(1,128)S(1)}, u32[]{:S(2)}, u32[]{:S(2)}) collective-permute-start(f32[2,1,256]{2,1,0:T(1,128)S(1)} %get-tuple-element.345), channel_id=1, source_target_pairs={{0,2},{2,4},{4,6},{1,3},{3,5},{5,7},{8,10},{10,12},{12,14},{9,11},... | collective-permute-start | bytes 6152 | tf_op jit(solution)/shard_map/ppermute | solution.py:23
  292.9 7.0 %collective-permute-start.87 = (f32[2,1,256]{2,1,0:T(1,128)S(1)}, f32[2,1,256]{2,1,0:T(1,128)S(1)}, u32[]{:S(2)}, u32[]{:S(2)}) collective-permute-start(f32[2,1,256]{2,1,0:T(1,128)S(1)} %get-tuple-element.342), channel_id=1, source_target_pairs={{2,0},{4,2},{6,4},{3,1},{5,3},{7,5},{10,8},{12,10},{14,12},{11,9},... | collective-permute-start | bytes 6152 | tf_op jit(solution)/shard_map/ppermute | solution.py:25
  294.2 7.0 %collective-permute-start.86 = (f32[2,1,256]{2,1,0:T(1,128)S(1)}, f32[2,1,256]{2,1,0:T(1,128)S(1)}, u32[]{:S(2)}, u32[]{:S(2)}) collective-permute-start(f32[2,1,256]{2,1,0:T(1,128)S(1)} %get-tuple-element.343), channel_id=1, source_target_pairs={{0,2},{2,4},{4,6},{1,3},{3,5},{5,7},{8,10},{10,12},{12,14},{9,11},... | collective-permute-start | bytes 6152 | tf_op jit(solution)/shard_map/ppermute | solution.py:23
  306.8 7.0 %collective-permute-start.91 = (f32[2,1,256]{2,1,0:T(1,128)S(1)}, f32[2,1,256]{2,1,0:T(1,128)S(1)}, u32[]{:S(2)}, u32[]{:S(2)}) collective-permute-start(f32[2,1,256]{2,1,0:T(1,128)S(1)} %get-tuple-element.340), channel_id=1, source_target_pairs={{2,0},{4,2},{6,4},{3,1},{5,3},{7,5},{10,8},{12,10},{14,12},{11,9},... | collective-permute-start | bytes 6152 | tf_op jit(solution)/shard_map/ppermute | solution.py:25
  308.1 7.0 %collective-permute-start.90 = (f32[2,1,256]{2,1,0:T(1,128)S(1)}, f32[2,1,256]{2,1,0:T(1,128)S(1)}, u32[]{:S(2)}, u32[]{:S(2)}) collective-permute-start(f32[2,1,256]{2,1,0:T(1,128)S(1)} %get-tuple-element.341), channel_id=1, source_target_pairs={{0,2},{2,4},{4,6},{1,3},{3,5},{5,7},{8,10},{10,12},{12,14},{9,11},... | collective-permute-start | bytes 6152 | tf_op jit(solution)/shard_map/ppermute | solution.py:23
  320.7 7.0 %collective-permute-start.95 = (f32[2,1,256]{2,1,0:T(1,128)S(1)}, f32[2,1,256]{2,1,0:T(1,128)S(1)}, u32[]{:S(2)}, u32[]{:S(2)}) collective-permute-start(f32[2,1,256]{2,1,0:T(1,128)S(1)} %get-tuple-element.338), channel_id=1, source_target_pairs={{2,0},{4,2},{6,4},{3,1},{5,3},{7,5},{10,8},{12,10},{14,12},{11,9},... | collective-permute-start | bytes 6152 | tf_op jit(solution)/shard_map/ppermute | solution.py:25
  322.0 7.0 %collective-permute-start.94 = (f32[2,1,256]{2,1,0:T(1,128)S(1)}, f32[2,1,256]{2,1,0:T(1,128)S(1)}, u32[]{:S(2)}, u32[]{:S(2)}) collective-permute-start(f32[2,1,256]{2,1,0:T(1,128)S(1)} %get-tuple-element.339), channel_id=1, source_target_pairs={{0,2},{2,4},{4,6},{1,3},{3,5},{5,7},{8,10},{10,12},{12,14},{9,11},... | collective-permute-start | bytes 6152 | tf_op jit(solution)/shard_map/ppermute | solution.py:23
  334.6 7.0 %collective-permute-start.99 = (f32[2,1,256]{2,1,0:T(1,128)S(1)}, f32[2,1,256]{2,1,0:T(1,128)S(1)}, u32[]{:S(2)}, u32[]{:S(2)}) collective-permute-start(f32[2,1,256]{2,1,0:T(1,128)S(1)} %get-tuple-element.336), channel_id=1, source_target_pairs={{2,0},{4,2},{6,4},{3,1},{5,3},{7,5},{10,8},{12,10},{14,12},{11,9},... | collective-permute-start | bytes 6152 | tf_op jit(solution)/shard_map/ppermute | solution.py:25
  335.9 7.0 %collective-permute-start.98 = (f32[2,1,256]{2,1,0:T(1,128)S(1)}, f32[2,1,256]{2,1,0:T(1,128)S(1)}, u32[]{:S(2)}, u32[]{:S(2)}) collective-permute-start(f32[2,1,256]{2,1,0:T(1,128)S(1)} %get-tuple-element.337), channel_id=1, source_target_pairs={{0,2},{2,4},{4,6},{1,3},{3,5},{5,7},{8,10},{10,12},{12,14},{9,11},... | collective-permute-start | bytes 6152 | tf_op jit(solution)/shard_map/ppermute | solution.py:23
  347.4 7.7 %collective-permute-start.69 = (f32[2,64,256]{2,1,0:T(8,128)S(1)}, f32[2,64,256]{2,1,0:T(8,128)S(1)}, u32[]{:S(2)}, u32[]{:S(2)}) collective-permute-start(f32[2,64,256]{2,1,0:T(8,128)S(1)} %pad_maximum_fusion.359), channel_id=1, source_target_pairs={{8,0},{16,8},{24,16},{9,1},{17,9},{25,17},{10,2},{18,10},{26,18},{... | collective-permute-start | bytes 393224 | tf_op jit(solution)/shard_map/ppermute | solution.py:51
  392.4 6.8 %collective-permute-start.107 = (f32[2,1,256]{2,1,0:T(1,128)S(1)}, f32[2,1,256]{2,1,0:T(1,128)S(1)}, u32[]{:S(2)}, u32[]{:S(2)}) collective-permute-start(f32[2,1,256]{2,1,0:T(1,128)S(1)} %get-tuple-element.299), channel_id=1, source_target_pairs={{2,0},{4,2},{6,4},{3,1},{5,3},{7,5},{10,8},{12,10},{14,12},{11,9},... | collective-permute-start | bytes 6152 | tf_op jit(solution)/shard_map/ppermute | solution.py:25
  393.7 6.7 %collective-permute-start.106 = (f32[2,1,256]{2,1,0:T(1,128)S(1)}, f32[2,1,256]{2,1,0:T(1,128)S(1)}, u32[]{:S(2)}, u32[]{:S(2)}) collective-permute-start(f32[2,1,256]{2,1,0:T(1,128)S(1)} %get-tuple-element.300), channel_id=1, source_target_pairs={{0,2},{2,4},{4,6},{1,3},{3,5},{5,7},{8,10},{10,12},{12,14},{9,11},... | collective-permute-start | bytes 6152 | tf_op jit(solution)/shard_map/ppermute | solution.py:23
  406.0 6.8 %collective-permute-start.111 = (f32[2,1,256]{2,1,0:T(1,128)S(1)}, f32[2,1,256]{2,1,0:T(1,128)S(1)}, u32[]{:S(2)}, u32[]{:S(2)}) collective-permute-start(f32[2,1,256]{2,1,0:T(1,128)S(1)} %get-tuple-element.297), channel_id=1, source_target_pairs={{2,0},{4,2},{6,4},{3,1},{5,3},{7,5},{10,8},{12,10},{14,12},{11,9},... | collective-permute-start | bytes 6152 | tf_op jit(solution)/shard_map/ppermute | solution.py:25
  407.3 6.7 %collective-permute-start.110 = (f32[2,1,256]{2,1,0:T(1,128)S(1)}, f32[2,1,256]{2,1,0:T(1,128)S(1)}, u32[]{:S(2)}, u32[]{:S(2)}) collective-permute-start(f32[2,1,256]{2,1,0:T(1,128)S(1)} %get-tuple-element.298), channel_id=1, source_target_pairs={{0,2},{2,4},{4,6},{1,3},{3,5},{5,7},{8,10},{10,12},{12,14},{9,11},... | collective-permute-start | bytes 6152 | tf_op jit(solution)/shard_map/ppermute | solution.py:23
  419.6 7.0 %collective-permute-start.115 = (f32[2,1,256]{2,1,0:T(1,128)S(1)}, f32[2,1,256]{2,1,0:T(1,128)S(1)}, u32[]{:S(2)}, u32[]{:S(2)}) collective-permute-start(f32[2,1,256]{2,1,0:T(1,128)S(1)} %get-tuple-element.295), channel_id=1, source_target_pairs={{2,0},{4,2},{6,4},{3,1},{5,3},{7,5},{10,8},{12,10},{14,12},{11,9},... | collective-permute-start | bytes 6152 | tf_op jit(solution)/shard_map/ppermute | solution.py:25
  420.9 7.0 %collective-permute-start.114 = (f32[2,1,256]{2,1,0:T(1,128)S(1)}, f32[2,1,256]{2,1,0:T(1,128)S(1)}, u32[]{:S(2)}, u32[]{:S(2)}) collective-permute-start(f32[2,1,256]{2,1,0:T(1,128)S(1)} %get-tuple-element.296), channel_id=1, source_target_pairs={{0,2},{2,4},{4,6},{1,3},{3,5},{5,7},{8,10},{10,12},{12,14},{9,11},... | collective-permute-start | bytes 6152 | tf_op jit(solution)/shard_map/ppermute | solution.py:23
  433.5 7.0 %collective-permute-start.119 = (f32[2,1,256]{2,1,0:T(1,128)S(1)}, f32[2,1,256]{2,1,0:T(1,128)S(1)}, u32[]{:S(2)}, u32[]{:S(2)}) collective-permute-start(f32[2,1,256]{2,1,0:T(1,128)S(1)} %get-tuple-element.293), channel_id=1, source_target_pairs={{2,0},{4,2},{6,4},{3,1},{5,3},{7,5},{10,8},{12,10},{14,12},{11,9},... | collective-permute-start | bytes 6152 | tf_op jit(solution)/shard_map/ppermute | solution.py:25
  434.8 7.0 %collective-permute-start.118 = (f32[2,1,256]{2,1,0:T(1,128)S(1)}, f32[2,1,256]{2,1,0:T(1,128)S(1)}, u32[]{:S(2)}, u32[]{:S(2)}) collective-permute-start(f32[2,1,256]{2,1,0:T(1,128)S(1)} %get-tuple-element.294), channel_id=1, source_target_pairs={{0,2},{2,4},{4,6},{1,3},{3,5},{5,7},{8,10},{10,12},{12,14},{9,11},... | collective-permute-start | bytes 6152 | tf_op jit(solution)/shard_map/ppermute | solution.py:23
  447.4 7.3 %collective-permute-start.123 = (f32[2,1,256]{2,1,0:T(1,128)S(1)}, f32[2,1,256]{2,1,0:T(1,128)S(1)}, u32[]{:S(2)}, u32[]{:S(2)}) collective-permute-start(f32[2,1,256]{2,1,0:T(1,128)S(1)} %get-tuple-element.291), channel_id=1, source_target_pairs={{2,0},{4,2},{6,4},{3,1},{5,3},{7,5},{10,8},{12,10},{14,12},{11,9},... | collective-permute-start | bytes 6152 | tf_op jit(solution)/shard_map/ppermute | solution.py:25
  448.7 7.0 %collective-permute-start.122 = (f32[2,1,256]{2,1,0:T(1,128)S(1)}, f32[2,1,256]{2,1,0:T(1,128)S(1)}, u32[]{:S(2)}, u32[]{:S(2)}) collective-permute-start(f32[2,1,256]{2,1,0:T(1,128)S(1)} %get-tuple-element.292), channel_id=1, source_target_pairs={{0,2},{2,4},{4,6},{1,3},{3,5},{5,7},{8,10},{10,12},{12,14},{9,11},... | collective-permute-start | bytes 6152 | tf_op jit(solution)/shard_map/ppermute | solution.py:23
  461.4 7.3 %collective-permute-start.127 = (f32[2,1,256]{2,1,0:T(1,128)S(1)}, f32[2,1,256]{2,1,0:T(1,128)S(1)}, u32[]{:S(2)}, u32[]{:S(2)}) collective-permute-start(f32[2,1,256]{2,1,0:T(1,128)S(1)} %get-tuple-element.289), channel_id=1, source_target_pairs={{2,0},{4,2},{6,4},{3,1},{5,3},{7,5},{10,8},{12,10},{14,12},{11,9},... | collective-permute-start | bytes 6152 | tf_op jit(solution)/shard_map/ppermute | solution.py:25
  462.7 7.0 %collective-permute-start.126 = (f32[2,1,256]{2,1,0:T(1,128)S(1)}, f32[2,1,256]{2,1,0:T(1,128)S(1)}, u32[]{:S(2)}, u32[]{:S(2)}) collective-permute-start(f32[2,1,256]{2,1,0:T(1,128)S(1)} %get-tuple-element.290), channel_id=1, source_target_pairs={{0,2},{2,4},{4,6},{1,3},{3,5},{5,7},{8,10},{10,12},{12,14},{9,11},... | collective-permute-start | bytes 6152 | tf_op jit(solution)/shard_map/ppermute | solution.py:23
  (105 other events, 818.1 us)
Sparse Core Ops, SparseCore 0:
  193.5 31.3 all-gather.4
  492.7 32.6 all-reduce.1
where the time goes:
time: 537 us; the launch traced here: 534 us
  starting transfers between devices  336 us (63%)
  waiting for transfers between devices  120 us (22%)
  blocking collectives  37.6 us (7%)
  between operations  16.9 us (3%)
  other arithmetic  15.3 us (3%)
  local copies, waits for them, and re-layouts  7.45 us (1%)
    ppermute x66, starting transfers between devices, extended(): lax.ppermute(tail, axis, [(i, (i + 1) % count) for i in range(ends)])  246 us
    ppermute x66, starting transfers between devices, extended(): lax.ppermute(head, axis, [((i + 1) % count, i) for i in range(ends)])  85.5 us
    ppermute x66, waiting for transfers between devices, extended(): lax.ppermute(head, axis, [((i + 1) % count, i) for i in range(ends)])  46.8 us
    all_gather x2, blocking collectives, prefix(): gathered = jax.tree.map(lambda a: lax.all_gather(a, axis), part)  37.6 us
    psum x1, waiting for transfers between devices, local(): gradient = lax.psum(local_gradient, 'tm')  32.8 us
    ppermute x66, waiting for transfers between devices, extended(): lax.ppermute(tail, axis, [(i, (i + 1) % count) for i in range(ends)])  27.8 us
    ppermute x2, waiting for transfers between devices, shifted_2(): return lax.ppermute(block, axis, route)  12.6 us
  transfers between devices with their start and end apart: 136, of which 51 were waited for; matrix products, arithmetic and copies ran while one was open for 1% of the time, Pallas kernels for 0%

commit v1 on v0

v1 whole, which is shorter than its diff:
```python
import functools

import jax
import jax.numpy as jnp
from jax import lax
from jax.experimental import pallas as pl
from jax.experimental.pallas import tpu as pltpu
from jax.sharding import PartitionSpec as P

STEPS = 8
TIME_STEP = 0.1
DIFFUSION = (1.0, 0.4)
DECAY = (1.0, 2.0)

LANES = 128
SUB = 8
PER_GROUP = 4
HALO = 3 * STEPS
HALO_W = 2 * STEPS
SIDE = 32
BLOCK = 8

VMEM_SPEC = pl.BlockSpec(memory_space=pltpu.VMEM)


def call(body, outs, scratch=(), limit=32 << 20):
    return pl.pallas_call(
        body,
        out_shape=[jax.ShapeDtypeStruct(s, jnp.float32) for s in outs],
        out_specs=[VMEM_SPEC] * len(outs),
        scratch_shapes=list(scratch),
        compiler_params=pltpu.CompilerParams(vmem_limit_bytes=limit),
    )


def strip_body(s_ref, a_ref, k_ref, r_ref, c_ref, q_ref, t_ref, out_ref):
    first = lax.axis_index("sy") == 0
    at = 0
    for ref in (s_ref, a_ref, k_ref, r_ref, c_ref, q_ref, t_ref):
        rows, cols = ref.shape
        out_ref[at : at + rows, :] = jnp.where(
            first, ref[:, cols - LANES :], ref[:, :LANES]
        )
        at += rows


def window_body(count, s_ref, a_ref, k_ref, r_ref, c_ref, q_ref, t_ref, strip_ref, *rest):
    outs, coef_ref, ext = rest[:count], rest[count], rest[count + 1]
    me = lax.axis_index("tm")
    first = lax.axis_index("sy") == 0
    at = 0
    for ref in (s_ref, a_ref, k_ref, r_ref, c_ref, q_ref, t_ref):
        rows, cols = ref.shape
        strip = strip_ref[at : at + rows, :]
        zero = jnp.zeros_like(strip)
        ext[at : at + rows, 0:LANES] = jnp.where(first, zero, strip)
        ext[at : at + rows, LANES : LANES + cols] = ref[...]
        ext[at : at + rows, LANES + cols : 2 * LANES + cols] = jnp.where(first, strip, zero)
        at += rows
    guesses = s_ref.shape[0] + a_ref.shape[0]
    wide = s_ref.shape[1] // count

    def window(lo, hi, t):
        start = LANES - SIDE + wide * t
        base = pl.multiple_of((start // LANES) * LANES, LANES)
        shift = 2 * LANES - start % LANES
        return pltpu.roll(ext[lo:hi, pl.ds(base, 2 * LANES)], shift, 1)[:, :LANES]

    for d in range(count):
        outs[d][...] = window(0, guesses, me ^ d)
    coef_ref[...] = window(guesses, at, me)


def interleave_body(count, tile_rows, *refs):
    cens, coef_ref = refs[:count], refs[count]
    mid_s, mid_a, down_ref, up_ref = refs[count + 1 : count + 5]
    me = lax.axis_index("tm")
    groups = count // PER_GROUP
    for d in range(count):
        slab = me ^ d
        g, j = slab // PER_GROUP, slab % PER_GROUP
        for field, mid in ((0, mid_s), (1, mid_a)):
            for sp in range(2):
                rows = cens[d][(2 * field + sp) * tile_rows : (2 * field + sp + 1) * tile_rows, :]
                mid[g, pl.ds(sp * PER_GROUP + j, tile_rows, stride=SUB), :] = rows
    for ref, low in ((down_ref, False), (up_ref, True)):
        at = 0
        for mid, halo in ((mid_s, HALO), (mid_a, HALO_W)):
            size = halo * SUB
            start = 0 if low else (tile_rows - halo) * SUB
            for g in range(groups):
                ref[at : at + size, :] = mid[g, start : start + size, :]
                at += size
        for f in range(7):
            start = f * tile_rows + (0 if low else tile_rows - HALO)
            ref[at : at + HALO, :] = coef_ref[start : start + HALO, :]
            at += HALO


def main_body(count, tile_rows, wide, mid_s, mid_a, coef_ref, top_ref, bot_ref, *rest):
    outs = rest[:count]
    work, hist, lag, cv, ce, cd, cx, cq, gd, tg, fv, fh, flat = rest[count:]
    groups = count // PER_GROUP
    total = tile_rows + 2 * HALO
    me = lax.axis_index("tm")
    s_at = lax.axis_index("sx")
    has_top = s_at > 0
    has_bot = s_at < lax.axis_size("sx") - 1
    end = HALO + tile_rows

    def each_group(fn):
        if groups == 1:
            fn(0)
        else:
            lax.fori_loop(0, groups, lambda g, c: (fn(g), c)[1], 0)

    def masked(flag, value):
        return jnp.where(flag, value, jnp.zeros_like(value))

    at = groups * (HALO + HALO_W) * SUB
    fields = []
    for f in range(7):
        flat[f, 0:HALO, :] = masked(has_top, top_ref[at + f * HALO : at + (f + 1) * HALO, :])
        flat[f, HALO:end, :] = coef_ref[f * tile_rows : (f + 1) * tile_rows, :]
        flat[f, end:total, :] = masked(has_bot, bot_ref[at + f * HALO : at + (f + 1) * HALO, :])
        fields.append(flat[f])
    k, rate, coupling, q0, q1, t0, t1 = fields
    row = lax.broadcasted_iota(jnp.int32, (total, LANES), 0) + (s_at * tile_rows - HALO)
    col = lax.broadcasted_iota(jnp.int32, (total, LANES), 1) + (
        lax.axis_index("sy") * (wide * count) + me * wide - SIDE
    )
    all_rows = tile_rows * lax.axis_size("sx")
    all_cols = wide * count * lax.axis_size("sy")
    half = 0.5 * TIME_STEP
    above = half * (k + pltpu.roll(k, 1, 0))
    below = half * (k + pltpu.roll(k, total - 1, 0))
    east = half * (k + pltpu.roll(k, LANES - 1, 1))
    west = half * (k + pltpu.roll(k, 1, 1))
    faces = above + below + east + west
    above = jnp.where((row >= 1) & (row < all_rows), above, 0.0)
    east = jnp.where((col >= 0) & (col < all_cols - 1), east, 0.0)
    react = TIME_STEP * rate
    cross = react * coupling
    for sp, source in ((0, q0), (1, q1)):
        spread = (
            (cv, DIFFUSION[sp] * above),
            (ce, DIFFUSION[sp] * east),
            (cd, 1.0 - DIFFUSION[sp] * faces - DECAY[sp] * react),
            (cx, cross),
            (cq, TIME_STEP * source),
            (gd, 1.0 - (DECAY[sp] * STEPS) * react),
        )
        for ref, value in spread:
            for j in range(PER_GROUP):
                ref[pl.ds(sp * PER_GROUP + j, total, stride=SUB), :] = value
    tg[pl.ds(PER_GROUP - 1, total, stride=SUB), :] = t0
    tg[pl.ds(SUB - 1, total, stride=SUB), :] = t1

    def blocks(lo, hi):
        return [(r, min(r + BLOCK, hi)) for r in range(lo, hi, BLOCK)]

    def shift(value, by):
        n = value.shape[0] // SUB
        return pltpu.roll(value.reshape(n, SUB, LANES), by, 1).reshape(n * SUB, LANES)

    def at_rows(ref, lo, hi):
        return ref[lo * SUB : hi * SUB, :]

    def step(src, dst, lo, hi, off, source):
        for a, b in blocks(lo, hi):
            u = at_rows(src, a - off, b - off)
            e = at_rows(ce, a, b)
            new = (
                at_rows(cd, a, b) * u
                + at_rows(cv, a, b) * at_rows(src, a - off - 1, b - off - 1)
                + at_rows(cv, a + 1, b + 1) * at_rows(src, a - off + 1, b - off + 1)
                + e * pltpu.roll(u, LANES - 1, 1)
                + pltpu.roll(e * u, 1, 1)
                + at_rows(cx, a, b) * shift(u, PER_GROUP)
            )
            if source:
                new = new + at_rows(cq, a, b)
            dst[(a - off) * SUB : (b - off) * SUB, :] = new

    def sweep(lo, hi, source):
        def turn(t, carry):
            src = jnp.where(t == 0, 0, 1 + (t + 1) % 2)
            dst = 1 + t % 2
            each_group(lambda g: step(work.at[src, g], work.at[dst, g], lo, hi, 0, source))
            return carry

        lax.fori_loop(0, STEPS, turn, 0)
        return 1 + (STEPS - 1) % 2

    def coarse(value, a, b):
        return at_rows(gd, a, b) * value + (STEPS * at_rows(cx, a, b)) * shift(value, PER_GROUP)

    def load(mid, halo, at):
        def one(g):
            size = halo * SUB
            here = at + g * size
            if groups > 1:
                here = pl.multiple_of(here, SUB)
            work[0, g, (HALO - halo) * SUB : HALO * SUB, :] = masked(
                has_top, top_ref[pl.ds(here, size), :]
            )
            work[0, g, HALO * SUB : end * SUB, :] = mid[g]
            work[0, g, end * SUB : (end + halo) * SUB, :] = masked(
                has_bot, bot_ref[pl.ds(here, size), :]
            )

        each_group(one)

    def slab_of(a, b):
        return lax.broadcasted_iota(jnp.int32, ((b - a) * SUB, LANES), 0) % PER_GROUP

    lo, hi = STEPS, total - STEPS
    load(mid_s, HALO, 0)
    last = sweep(1, total - 1, True)
    for a, b in blocks(lo, hi):
        slab = slab_of(a, b)
        carry = jnp.zeros(((b - a) * SUB, LANES), jnp.float32)

        def chain(g, carry, a=a, b=b, slab=slab):
            x = at_rows(work.at[last, g], a, b) - coarse(at_rows(work.at[0, g], a, b), a, b)
            value = carry
            for _ in range(PER_GROUP - 1):
                value = jnp.where(slab == 0, carry, shift(coarse(value, a, b) + x, 1))
            hist[0, g, (a - lo) * SUB : (b - lo) * SUB, :] = value
            return shift(coarse(value, a, b) + x, SUB - PER_GROUP + 1)

        if groups == 1:
            chain(0, carry)
        else:
            lax.fori_loop(0, groups, chain, carry)

    load(mid_a, HALO_W, groups * HALO * SUB)
    last = sweep(STEPS + 1, total - STEPS - 1, False)
    w_lo, w_hi = 2 * STEPS, total - 2 * STEPS

    def keep(g):
        for a, b in blocks(w_lo, w_hi):
            lag[g, (a - w_lo) * SUB : (b - w_lo) * SUB, :] = at_rows(
                work.at[last, g], a, b
            ) - coarse(at_rows(work.at[0, g], a, b), a, b)

    each_group(keep)

    def forward(t, carry):
        each_group(lambda g: step(hist.at[t, g], hist.at[t + 1, g], lo + 1, hi - 1, lo, True))
        return carry

    lax.fori_loop(0, STEPS, forward, 0)

    for a, b in blocks(w_lo, w_hi):
        slab = slab_of(a, b)
        carry = at_rows(hist.at[STEPS, groups - 1], a - lo, b - lo) - at_rows(tg, a, b)

        def unchain(turn, carry, a=a, b=b, slab=slab):
            g = groups - 1 - turn
            y = lag[g, (a - w_lo) * SUB : (b - w_lo) * SUB, :]
            top = jnp.where(slab == PER_GROUP - 1, carry, 0.0)
            value = top
            for _ in range(PER_GROUP - 1):
                value = jnp.where(
                    slab == PER_GROUP - 1, top, shift(coarse(value, a, b) + y, SUB - 1)
                )
            work[0, g, a * SUB : b * SUB, :] = value
            return shift(coarse(value, a, b) + y, PER_GROUP - 1)

        if groups == 1:
            unchain(0, carry)
        else:
            lax.fori_loop(0, groups, unchain, carry)

    lane = lax.broadcasted_iota(jnp.int32, (tile_rows, LANES), 1)
    left = lane < LANES // 2

    def paired(first, second):
        return jnp.where(
            left,
            pltpu.roll(first, LANES - SIDE, 1),
            pltpu.roll(second, LANES // 2 - SIDE, 1),
        )

    for d in range(count):
        slab = me ^ d
        g, j = slab // PER_GROUP, slab % PER_GROUP
        s_rows = [
            hist[0, g, pl.ds((HALO - lo) * SUB + sp * PER_GROUP + j, tile_rows, stride=SUB), :]
            for sp in range(2)
        ]
        w_rows = [
            work[0, g, pl.ds(HALO * SUB + sp * PER_GROUP + j, tile_rows, stride=SUB), :]
            for sp in range(2)
        ]
        outs[d][0:tile_rows, :] = paired(*s_rows)
        outs[d][tile_rows : 2 * tile_rows, :] = paired(*w_rows)

    fv[...] = jnp.zeros_like(fv)
    fh[...] = jnp.zeros_like(fh)

    def products(u, w):
        for a, b in blocks(HALO, end + 1):
            at = slice((a - HALO) * SUB, (b - HALO) * SUB)
            uc, wc = at_rows(u, a - lo, b - lo), at_rows(w, a, b)
            fv[at, :] += (uc - at_rows(u, a - lo - 1, b - lo - 1)) * (
                wc - at_rows(w, a - 1, b - 1)
            )
            if b <= end:
                fh[at, :] += (pltpu.roll(uc, LANES - 1, 1) - uc) * (
                    pltpu.roll(wc, LANES - 1, 1) - wc
                )

    def back(t, carry):
        src = jnp.where(t == 0, 0, 1 + (t + 1) % 2)
        dst = 1 + t % 2

        def one(g):
            products(hist.at[STEPS - 1 - t, g], work.at[src, g])
            step(work.at[src, g], work.at[dst, g], w_lo + 1, w_hi - 1, 0, False)

        each_group(one)
        return carry

    lax.fori_loop(0, STEPS - 1, back, 0)
    last = 1 + (STEPS - 2) % 2
    each_group(lambda g: products(hist.at[0, g], work.at[last, g]))

    size = tile_rows * SUB
    fh[...] = fv[0:size, :] + fv[SUB : size + SUB, :] + fh[...] + pltpu.roll(fh[...], 1, 1)
    summed = []
    for sp in range(2):
        parts = [
            fh[pl.ds(sp * PER_GROUP + j, tile_rows, stride=SUB), :] for j in range(PER_GROUP)
        ]
        summed.append((parts[0] + parts[1]) + (parts[2] + parts[3]))
    gradient = -half * (DIFFUSION[0] * summed[0] + DIFFUSION[1] * summed[1])
    middle = tile_rows // 2
    fold = jnp.where(
        left[:middle],
        pltpu.roll(gradient[:middle], LANES - SIDE, 1),
        pltpu.roll(gradient[middle:], LANES // 2 - SIDE, 1),
    )
    for d in range(count):
        outs[d][2 * tile_rows :, :] = fold


def collect_body(count, wide, *refs):
    parts = refs[:count]
    s_ref, w_ref, g_ref, held = refs[count:]
    me = lax.axis_index("tm")
    for d in range(count):
        held[me ^ d] = parts[d][...]
    rows = g_ref.shape[0]
    middle = rows // 2
    per = LANES // wide
    lane = lax.broadcasted_iota(jnp.int32, (rows, LANES), 1)

    def joined(lo, hi, start, v):
        value = None
        for i in range(per):
            t = v * per + i
            piece = held[t, lo:hi, :]
            turn = (i * wide - start) % LANES
            if turn:
                piece = pltpu.roll(piece, turn, 1)
            value = piece if i == 0 else jnp.where(lane[: hi - lo] >= i * wide, piece, value)
        return value

    for v in range(count // per):
        at = slice(v * LANES, (v + 1) * LANES)
        for sp in range(2):
            start = sp * (LANES // 2)
            s_ref[sp * rows : (sp + 1) * rows, at] = joined(0, rows, start, v)
            w_ref[sp * rows : (sp + 1) * rows, at] = joined(rows, 2 * rows, start, v)
            g_ref[sp * middle : (sp + 1) * middle, at] = joined(
                2 * rows, 2 * rows + middle, start, v
            )


def local(state_guess, adjoint_guess, diffusivity, decay_rate, coupling, control, target):
    rows, cols = diffusivity.shape
    count = lax.axis_size("tm")
    groups = count // PER_GROUP
    wide = cols // count
    total = rows + 2 * HALO
    fields = (
        state_guess.reshape(2 * rows, cols),
        adjoint_guess.reshape(2 * rows, cols),
        diffusivity,
        decay_rate,
        coupling,
        control.reshape(2 * rows, cols),
        target.reshape(2 * rows, cols),
    )

    def swapped(value, d):
        return lax.ppermute(value, "tm", [(i, i ^ d) for i in range(count)])

    def turned(value, d):
        n = lax.axis_size("sx")
        return lax.ppermute(value, "sx", [(i, (i + d) % n) for i in range(n)])

    (strip,) = call(strip_body, [(11 * rows, LANES)])(*fields)
    strip = lax.ppermute(strip, "sy", [(0, 1), (1, 0)])
    *cens, coef = call(
        functools.partial(window_body, count),
        [(4 * rows, LANES)] * count + [(7 * rows, LANES)],
        [pltpu.VMEM((11 * rows, cols + 2 * LANES), jnp.float32)],
    )(*fields, strip)
    cens = [cens[0]] + [swapped(cens[d], d) for d in range(1, count)]
    edge = groups * (HALO + HALO_W) * SUB + 7 * HALO
    mid = (groups, rows * SUB, LANES)
    mid_s, mid_a, down, up = call(
        functools.partial(interleave_body, count, rows),
        [mid, mid, (edge, LANES), (edge, LANES)],
    )(*cens, coef)
    top = turned(down, 1)
    bot = turned(up, -1)
    plain = pltpu.VMEM((total * SUB, LANES), jnp.float32)
    outs = call(
        functools.partial(main_body, count, rows, wide),
        [(2 * rows + rows // 2, LANES)] * count,
        [
            pltpu.VMEM((3, groups, total * SUB, LANES), jnp.float32),
            pltpu.VMEM((STEPS + 1, groups, (total - 2 * STEPS) * SUB, LANES), jnp.float32),
            pltpu.VMEM((groups, (total - 4 * STEPS) * SUB, LANES), jnp.float32),
            *([plain] * 7),
            pltpu.VMEM(((rows + 1) * SUB, LANES), jnp.float32),
            pltpu.VMEM((rows * SUB, LANES), jnp.float32),
            pltpu.VMEM((7, total, LANES), jnp.float32),
        ],
        60 << 20 if groups > 1 else 32 << 20,
    )(mid_s, mid_a, coef, top, bot)
    outs = [outs[0]] + [swapped(outs[d], d) for d in range(1, count)]
    states, adjoints, gradient = call(
        functools.partial(collect_body, count, wide),
        [(2 * rows, cols), (2 * rows, cols), (rows, cols)],
        [pltpu.VMEM((count, 2 * rows + rows // 2, LANES), jnp.float32)],
    )(*outs)
    return (
        states.reshape(1, 2, rows, cols),
        adjoints.reshape(1, 2, rows, cols),
        gradient,
    )


def solution(mesh):
    placed = (
        P("tm", None, "sx", "sy"),
        P("tm", None, "sx", "sy"),
        P("sx", "sy"),
        P("sx", "sy"),
        P("sx", "sy"),
        P(None, "sx", "sy"),
        P(None, "sx", "sy"),
    )
    return jax.shard_map(
        local,
        mesh=mesh,
        in_specs=placed,
        out_specs=(P("tm", None, "sx", "sy"), P("tm", None, "sx", "sy"), P("sx", "sy")),
        check_vma=False,
    )
```

time: 537 us -> 61.4 us (0.11)
  starting transfers between devices: 336 us -> 14.9 us
  waiting for transfers between devices: 120 us -> 26 us
  blocking collectives: 37.6 us -> 0 us
  between operations: 16.9 us -> 0.68 us
  other arithmetic: 15.3 us -> 0 us
  Pallas kernels: 0 us -> 13.4 us
    ppermute x134 -> x9, starting transfers between devices: 336 us -> 14.9 us  [the longest x6 11.4 us: swapped(): return lax.ppermute(value, 'tm', [(i, i ^ d) for i in range(count)])]
    ppermute x134 -> x9, waiting for transfers between devices: 87.1 us -> 26 us  [the longest x6 15.3 us: swapped(): return lax.ppermute(value, 'tm', [(i, i ^ d) for i in range(count)])]
    all_gather x2 -> x0, blocking collectives: 37.6 us -> none  [prefix(): gathered = jax.tree.map(lambda a: lax.all_gather(a, axis), part)]
    psum x1 -> x0, waiting for transfers between devices: 32.8 us -> none  [local(): gradient = lax.psum(local_gradient, 'tm')]
    pallas_call x0 -> x5, Pallas kernels: none -> 13.4 us  [the longest x1 11.8 us: local(): call(functools.partial(main_body, count, rows, wide), [(2 * rows + rows /...]
    add x71 -> x0, other arithmetic: 12 us -> none  [the longest x31 5.26 us: stepped(): summed + 0.5 * (kappa_mid + kappa_pad[a:a + height, b:b + width]) * (padd...]
  transfers between devices with their start and end apart: 136 -> 9, of which waited for: 51 -> 7; matrix products, arithmetic and copies ran while one was open for 1% -> 0% of each run, Pallas kernels for 0% -> 0%
where the time goes in v1:
time: 61.4 us; the launch traced here: 61.1 us
  waiting for transfers between devices  26 us (42%)
  starting transfers between devices  14.9 us (24%)
  Pallas kernels  13.4 us (22%)
  local copies, waits for them, and re-layouts  6.13 us (10%)
  between operations  0.68 us (1%)
    ppermute x6, waiting for transfers between devices, swapped(): return lax.ppermute(value, 'tm', [(i, i ^ d) for i in range(count)])  15.3 us
    pallas_call x1, Pallas kernels, local(): call(functools.partial(main_body, count, rows, wide), [(2 * rows + rows /...  11.8 us
    ppermute x6, starting transfers between devices, swapped(): return lax.ppermute(value, 'tm', [(i, i ^ d) for i in range(count)])  11.4 us
    ppermute x2, waiting for transfers between devices, turned(): return lax.ppermute(value, 'sx', [(i, (i + d) % n) for i in range(n)])  9.39 us
    unnamed x14, local copies, waits for them, and re-layouts  6.13 us
    ppermute x2, starting transfers between devices, turned(): return lax.ppermute(value, 'sx', [(i, (i + d) % n) for i in range(n)])  2.98 us
    ppermute x1, waiting for transfers between devices, local(): strip = lax.ppermute(strip, 'sy', [(0, 1), (1, 0)])  1.3 us
  transfers between devices with their start and end apart: 9, of which 7 were waited for; matrix products, arithmetic and copies ran while one was open for 0% of the time, Pallas kernels for 0%

profile of v1, /device:TPU:0, one launch (start us, length us, event | category | flops | bytes accessed | tf_op | source)
XLA Modules:
  0.0 61.1 jit_solution(6827884608978738120)
XLA Ops:
  0.6 0.0 copy-start
  0.6 0.9 %copy-done = f32[1,2,64,256]{3,2,1,0:T(8,128)S(1)} copy-done((f32[1,2,64,256]{3,2,1,0:T(8,128)S(1)}, f32[1,2,64,256]{3,2,1,0:T(8,128)}, u32[]{:S(2)}) %copy-start) | copy-done | bytes 131096
  1.5 0.0 copy-start.1
  1.5 0.9 %copy-done.1 = f32[1,2,64,256]{3,2,1,0:T(8,128)S(1)} copy-done((f32[1,2,64,256]{3,2,1,0:T(8,128)S(1)}, f32[1,2,64,256]{3,2,1,0:T(8,128)}, u32[]{:S(2)}) %copy-start.1) | copy-done | bytes 131096
  2.4 0.0 copy-start.2
  2.4 0.9 %copy-done.2 = f32[2,64,256]{2,1,0:T(8,128)S(1)} copy-done((f32[2,64,256]{2,1,0:T(8,128)S(1)}, f32[2,64,256]{2,1,0:T(8,128)}, u32[]{:S(2)}) %copy-start.2) | copy-done | bytes 131096
  3.3 0.0 copy-start.3
  3.3 0.9 %copy-done.3 = f32[2,64,256]{2,1,0:T(8,128)S(1)} copy-done((f32[2,64,256]{2,1,0:T(8,128)S(1)}, f32[2,64,256]{2,1,0:T(8,128)}, u32[]{:S(2)}) %copy-start.3) | copy-done | bytes 131096
  4.3 0.0 copy-start.4
  4.3 0.8 %copy-done.4 = f32[64,256]{1,0:T(8,128)S(1)} copy-done((f32[64,256]{1,0:T(8,128)S(1)}, f32[64,256]{1,0:T(8,128)}, u32[]{:S(2)}) %copy-start.4) | copy-done | bytes 65560
  5.1 0.0 copy-start.5
  5.1 0.8 %copy-done.5 = f32[64,256]{1,0:T(8,128)S(1)} copy-done((f32[64,256]{1,0:T(8,128)S(1)}, f32[64,256]{1,0:T(8,128)}, u32[]{:S(2)}) %copy-start.5) | copy-done | bytes 65560
  5.9 0.0 copy-start.6
  5.9 0.8 %copy-done.6 = f32[64,256]{1,0:T(8,128)S(1)} copy-done((f32[64,256]{1,0:T(8,128)S(1)}, f32[64,256]{1,0:T(8,128)}, u32[]{:S(2)}) %copy-start.6) | copy-done | bytes 65560
  6.8 0.5 collective-permute-start
  7.3 1.3 %collective-permute-done.strip_ref = f32[704,128]{1,0:T(8,128)S(1)} collective-permute-done((f32[704,128]{1,0:T(8,128)S(1)}, f32[704,128]{1,0:T(8,128)S(1)}, u32[]{:S(2)}, u32[]{:S(2)}) %collective-permute-start) | collective-permute-done | bytes 360480 | tf_op jit(solution)/shard_map/ppermute | solution.py:406
  8.6 0.6 shard_map.95
  9.2 3.0 %collective-permute-start.1 = (f32[256,128]{1,0:T(8,128)S(1)}, f32[256,128]{1,0:T(8,128)S(1)}, u32[]{:S(2)}, u32[]{:S(2)}) collective-permute-start(f32[256,128]{1,0:T(8,128)S(1)} %get-tuple-element.20), channel_id=1, source_target_pairs={{0,8},{8,0},{16,24},{24,16},{1,9},{9,1},{17,25},{25,17},{2,10},{10... | collective-permute-start | bytes 393224 | tf_op jit(solution)/shard_map/ppermute | solution.py:399
  12.2 2.6 %collective-permute-start.2 = (f32[256,128]{1,0:T(8,128)S(1)}, f32[256,128]{1,0:T(8,128)S(1)}, u32[]{:S(2)}, u32[]{:S(2)}) collective-permute-start(f32[256,128]{1,0:T(8,128)S(1)} %get-tuple-element.21), channel_id=1, source_target_pairs={{0,16},{8,24},{16,0},{24,8},{1,17},{9,25},{17,1},{25,9},{2,18},{10... | collective-permute-start | bytes 393224 | tf_op jit(solution)/shard_map/ppermute | solution.py:399
  14.8 0.0 collective-permute-start.3
  14.8 3.1 %collective-permute-done.1.refs_1_ = f32[256,128]{1,0:T(8,128)S(1)} collective-permute-done((f32[256,128]{1,0:T(8,128)S(1)}, f32[256,128]{1,0:T(8,128)S(1)}, u32[]{:S(2)}, u32[]{:S(2)}) %collective-permute-start.1) | collective-permute-done | bytes 131104 | tf_op jit(solution)/shard_map/ppermute | solution.py:399
  17.9 7.2 %collective-permute-done.2.refs_2_ = f32[256,128]{1,0:T(8,128)S(1)} collective-permute-done((f32[256,128]{1,0:T(8,128)S(1)}, f32[256,128]{1,0:T(8,128)S(1)}, u32[]{:S(2)}, u32[]{:S(2)}) %collective-permute-start.2) | collective-permute-done | bytes 131104 | tf_op jit(solution)/shard_map/ppermute | solution.py:399
  25.1 0.0 collective-permute-done.3.refs_3_
  25.1 0.2 shard_map.96
  25.3 1.5 %collective-permute-start.4 = (f32[488,128]{1,0:T(8,128)S(1)}, f32[488,128]{1,0:T(8,128)S(1)}, u32[]{:S(2)}, u32[]{:S(2)}) collective-permute-start(f32[488,128]{1,0:T(8,128)S(1)} %get-tuple-element.26), channel_id=1, source_target_pairs={{0,2},{2,4},{4,6},{6,0},{1,3},{3,5},{5,7},{7,1},{8,10},{10,12},{12... | collective-permute-start | bytes 749576 | tf_op jit(solution)/shard_map/ppermute | solution.py:403
  26.8 1.4 %collective-permute-start.5 = (f32[488,128]{1,0:T(8,128)S(1)}, f32[488,128]{1,0:T(8,128)S(1)}, u32[]{:S(2)}, u32[]{:S(2)}) collective-permute-start(f32[488,128]{1,0:T(8,128)S(1)} %get-tuple-element.27), channel_id=1, source_target_pairs={{0,6},{2,0},{4,2},{6,4},{1,7},{3,1},{5,3},{7,5},{8,14},{10,8},{12,... | collective-permute-start | bytes 749576 | tf_op jit(solution)/shard_map/ppermute | solution.py:403
  28.3 6.7 %collective-permute-done.4.top_ref = f32[488,128]{1,0:T(8,128)S(1)} collective-permute-done((f32[488,128]{1,0:T(8,128)S(1)}, f32[488,128]{1,0:T(8,128)S(1)}, u32[]{:S(2)}, u32[]{:S(2)}) %collective-permute-start.4) | collective-permute-done | bytes 249888 | tf_op jit(solution)/shard_map/ppermute | solution.py:403
  34.9 2.7 %collective-permute-done.5.bot_ref = f32[488,128]{1,0:T(8,128)S(1)} collective-permute-done((f32[488,128]{1,0:T(8,128)S(1)}, f32[488,128]{1,0:T(8,128)S(1)}, u32[]{:S(2)}, u32[]{:S(2)}) %collective-permute-start.5) | collective-permute-done | bytes 249888 | tf_op jit(solution)/shard_map/ppermute | solution.py:403
  37.7 11.8 %shard_map.97 = (f32[160,128]{1,0:T(8,128)S(1)}, f32[160,128]{1,0:T(8,128)S(1)}, f32[160,128]{1,0:T(8,128)S(1)}, f32[160,128]{1,0:T(8,128)S(1)}) custom-call(f32[1,512,128]{2,1,0:T(8,128)S(1)} %get-tuple-element.24.mid_s, f32[1,512,128]{2,1,0:T(8,128)S(1)} %get-tuple-element.25.mid_a, f32[448,128]{1,0:T(8,128)S(1)} %get-tuple-element.23.refs_4_.coef_ref, ...), custom_call_target="tpu_custom_call" | custom-call | tf_op jit(solution)/shard_map/pallas_call | solution.py:422
  49.4 3.3 %collective-permute-start.6 = (f32[160,128]{1,0:T(8,128)S(1)}, f32[160,128]{1,0:T(8,128)S(1)}, u32[]{:S(2)}, u32[]{:S(2)}) collective-permute-start(f32[160,128]{1,0:T(8,128)S(1)} %get-tuple-element.29), channel_id=1, source_target_pairs={{0,8},{8,0},{16,24},{24,16},{1,9},{9,1},{17,25},{25,17},{2,10},{10... | collective-permute-start | bytes 245768 | tf_op jit(solution)/shard_map/ppermute | solution.py:399
  52.7 1.1 %collective-permute-start.7 = (f32[160,128]{1,0:T(8,128)S(1)}, f32[160,128]{1,0:T(8,128)S(1)}, u32[]{:S(2)}, u32[]{:S(2)}) collective-permute-start(f32[160,128]{1,0:T(8,128)S(1)} %get-tuple-element.30), channel_id=1, source_target_pairs={{0,16},{8,24},{16,0},{24,8},{1,17},{9,25},{17,1},{25,9},{2,18},{10... | collective-permute-start | bytes 245768 | tf_op jit(solution)/shard_map/ppermute | solution.py:399
  53.8 1.4 %collective-permute-start.8 = (f32[160,128]{1,0:T(8,128)S(1)}, f32[160,128]{1,0:T(8,128)S(1)}, u32[]{:S(2)}, u32[]{:S(2)}) collective-permute-start(f32[160,128]{1,0:T(8,128)S(1)} %get-tuple-element.31), channel_id=1, source_target_pairs={{0,24},{8,16},{16,8},{24,0},{1,25},{9,17},{17,9},{25,1},{2,26},{10... | collective-permute-start | bytes 245768 | tf_op jit(solution)/shard_map/ppermute | solution.py:399
  55.2 0.6 collective-permute-done.6.refs_1_
  55.8 4.4 %collective-permute-done.7.refs_2_ = f32[160,128]{1,0:T(8,128)S(1)} collective-permute-done((f32[160,128]{1,0:T(8,128)S(1)}, f32[160,128]{1,0:T(8,128)S(1)}, u32[]{:S(2)}, u32[]{:S(2)}) %collective-permute-start.7) | collective-permute-done | bytes 81952 | tf_op jit(solution)/shard_map/ppermute | solution.py:399
  60.2 0.0 collective-permute-done.8.refs_3_
  60.2 0.9 %shard_map.98 = (f32[128,256]{1,0:T(8,128)}, f32[128,256]{1,0:T(8,128)}, f32[64,256]{1,0:T(8,128)}) custom-call(f32[160,128]{1,0:T(8,128)S(1)} %get-tuple-element.28.refs_0_, f32[160,128]{1,0:T(8,128)S(1)} %collective-permute-done.6.refs_1_, f32[160,128]{1,0:T(8,128)S(1)} %collective-permute-done.7.refs_2_, f32[160,128]{1,0:T(8,128)S(1)} %collective-permute-done.8.refs_3_), custom_call_target="tpu_custom_call" | custom-call | tf_op jit(solution)/shard_map/pallas_call | solution.py:437
  (1 shorter events, 0.0 us)
Async XLA Ops:
  0.6 0.9 %copy-start = (f32[1,2,64,256]{3,2,1,0:T(8,128)S(1)}, f32[1,2,64,256]{3,2,1,0:T(8,128)}, u32[]{:S(2)}) copy-start(f32[1,2,64,256]{3,2,1,0:T(8,128)} %param.7) | copy-start | bytes 393220
  1.5 0.9 %copy-start.1 = (f32[1,2,64,256]{3,2,1,0:T(8,128)S(1)}, f32[1,2,64,256]{3,2,1,0:T(8,128)}, u32[]{:S(2)}) copy-start(f32[1,2,64,256]{3,2,1,0:T(8,128)} %param.8) | copy-start | bytes 393220
  2.4 0.9 %copy-start.2 = (f32[2,64,256]{2,1,0:T(8,128)S(1)}, f32[2,64,256]{2,1,0:T(8,128)}, u32[]{:S(2)}) copy-start(f32[2,64,256]{2,1,0:T(8,128)} %param.12) | copy-start | bytes 393220
  3.3 0.9 %copy-start.3 = (f32[2,64,256]{2,1,0:T(8,128)S(1)}, f32[2,64,256]{2,1,0:T(8,128)}, u32[]{:S(2)}) copy-start(f32[2,64,256]{2,1,0:T(8,128)} %param.13) | copy-start | bytes 393220
  4.3 0.8 %copy-start.4 = (f32[64,256]{1,0:T(8,128)S(1)}, f32[64,256]{1,0:T(8,128)}, u32[]{:S(2)}) copy-start(f32[64,256]{1,0:T(8,128)} %k_ref.3) | copy-start | bytes 196612
  5.1 0.8 %copy-start.5 = (f32[64,256]{1,0:T(8,128)S(1)}, f32[64,256]{1,0:T(8,128)}, u32[]{:S(2)}) copy-start(f32[64,256]{1,0:T(8,128)} %r_ref.3) | copy-start | bytes 196612
  5.9 0.8 %copy-start.6 = (f32[64,256]{1,0:T(8,128)S(1)}, f32[64,256]{1,0:T(8,128)}, u32[]{:S(2)}) copy-start(f32[64,256]{1,0:T(8,128)} %c_ref.3) | copy-start | bytes 196612
  6.8 1.8 %collective-permute-start = (f32[704,128]{1,0:T(8,128)S(1)}, f32[704,128]{1,0:T(8,128)S(1)}, u32[]{:S(2)}, u32[]{:S(2)}) collective-permute-start(f32[704,128]{1,0:T(8,128)S(1)} %shard_map.94), channel_id=1, source_target_pairs={{0,1},{1,0},{2,3},{3,2},{4,5},{5,4},{6,7},{7,6},{8,9},{9,8},{10,11... | collective-permute-start | bytes 1081352 | tf_op jit(solution)/shard_map/ppermute | solution.py:406
  9.2 8.7 %collective-permute-start.1 = (f32[256,128]{1,0:T(8,128)S(1)}, f32[256,128]{1,0:T(8,128)S(1)}, u32[]{:S(2)}, u32[]{:S(2)}) collective-permute-start(f32[256,128]{1,0:T(8,128)S(1)} %get-tuple-element.20), channel_id=1, source_target_pairs={{0,8},{8,0},{16,24},{24,16},{1,9},{9,1},{17,25},{25,17},{2,10},{10... | collective-permute-start | bytes 393224 | tf_op jit(solution)/shard_map/ppermute | solution.py:399
  12.2 12.9 %collective-permute-start.2 = (f32[256,128]{1,0:T(8,128)S(1)}, f32[256,128]{1,0:T(8,128)S(1)}, u32[]{:S(2)}, u32[]{:S(2)}) collective-permute-start(f32[256,128]{1,0:T(8,128)S(1)} %get-tuple-element.21), channel_id=1, source_target_pairs={{0,16},{8,24},{16,0},{24,8},{1,17},{9,25},{17,1},{25,9},{2,18},{10... | collective-permute-start | bytes 393224 | tf_op jit(solution)/shard_map/ppermute | solution.py:399
  14.8 10.3 %collective-permute-start.3 = (f32[256,128]{1,0:T(8,128)S(1)}, f32[256,128]{1,0:T(8,128)S(1)}, u32[]{:S(2)}, u32[]{:S(2)}) collective-permute-start(f32[256,128]{1,0:T(8,128)S(1)} %get-tuple-element.22), channel_id=1, source_target_pairs={{0,24},{8,16},{16,8},{24,0},{1,25},{9,17},{17,9},{25,1},{2,26},{10... | collective-permute-start | bytes 393224 | tf_op jit(solution)/shard_map/ppermute | solution.py:399
  25.3 9.6 %collective-permute-start.4 = (f32[488,128]{1,0:T(8,128)S(1)}, f32[488,128]{1,0:T(8,128)S(1)}, u32[]{:S(2)}, u32[]{:S(2)}) collective-permute-start(f32[488,128]{1,0:T(8,128)S(1)} %get-tuple-element.26), channel_id=1, source_target_pairs={{0,2},{2,4},{4,6},{6,0},{1,3},{3,5},{5,7},{7,1},{8,10},{10,12},{12... | collective-permute-start | bytes 749576 | tf_op jit(solution)/shard_map/ppermute | solution.py:403
  26.8 10.8 %collective-permute-start.5 = (f32[488,128]{1,0:T(8,128)S(1)}, f32[488,128]{1,0:T(8,128)S(1)}, u32[]{:S(2)}, u32[]{:S(2)}) collective-permute-start(f32[488,128]{1,0:T(8,128)S(1)} %get-tuple-element.27), channel_id=1, source_target_pairs={{0,6},{2,0},{4,2},{6,4},{1,7},{3,1},{5,3},{7,5},{8,14},{10,8},{12,... | collective-permute-start | bytes 749576 | tf_op jit(solution)/shard_map/ppermute | solution.py:403
  49.4 6.4 %collective-permute-start.6 = (f32[160,128]{1,0:T(8,128)S(1)}, f32[160,128]{1,0:T(8,128)S(1)}, u32[]{:S(2)}, u32[]{:S(2)}) collective-permute-start(f32[160,128]{1,0:T(8,128)S(1)} %get-tuple-element.29), channel_id=1, source_target_pairs={{0,8},{8,0},{16,24},{24,16},{1,9},{9,1},{17,25},{25,17},{2,10},{10... | collective-permute-start | bytes 245768 | tf_op jit(solution)/shard_map/ppermute | solution.py:399
  52.7 7.5 %collective-permute-start.7 = (f32[160,128]{1,0:T(8,128)S(1)}, f32[160,128]{1,0:T(8,128)S(1)}, u32[]{:S(2)}, u32[]{:S(2)}) collective-permute-start(f32[160,128]{1,0:T(8,128)S(1)} %get-tuple-element.30), channel_id=1, source_target_pairs={{0,16},{8,24},{16,0},{24,8},{1,17},{9,25},{17,1},{25,9},{2,18},{10... | collective-permute-start | bytes 245768 | tf_op jit(solution)/shard_map/ppermute | solution.py:399
  53.8 6.4 %collective-permute-start.8 = (f32[160,128]{1,0:T(8,128)S(1)}, f32[160,128]{1,0:T(8,128)S(1)}, u32[]{:S(2)}, u32[]{:S(2)}) collective-permute-start(f32[160,128]{1,0:T(8,128)S(1)} %get-tuple-element.31), channel_id=1, source_target_pairs={{0,24},{8,16},{16,8},{24,0},{1,25},{9,17},{17,9},{25,1},{2,26},{10... | collective-permute-start | bytes 245768 | tf_op jit(solution)/shard_map/ppermute | solution.py:399

commit v2 on v1

v2 whole, which is shorter than its diff:
```python
import functools

import jax
import jax.numpy as jnp
from jax import lax
from jax.experimental import pallas as pl
from jax.experimental.pallas import tpu as pltpu
from jax.sharding import PartitionSpec as P

STEPS = 8
TIME_STEP = 0.1
DIFFUSION = (1.0, 0.4)
DECAY = (1.0, 2.0)

LANES = 128
SUB = 8
PER_GROUP = 4
HALO = 3 * STEPS
HALO_W = 2 * STEPS
SIDE = 32
BLOCK = 8

VMEM_SPEC = pl.BlockSpec(memory_space=pltpu.VMEM)
HBM_SPEC = pl.BlockSpec(memory_space=pltpu.HBM)


def call(body, outs, scratch=(), limit=32 << 20, inputs=None):
    def run(*args):
        return pl.pallas_call(
            body,
            out_shape=[jax.ShapeDtypeStruct(s, jnp.float32) for s in outs],
            in_specs=inputs or [VMEM_SPEC] * len(args),
            out_specs=[VMEM_SPEC] * len(outs),
            scratch_shapes=list(scratch),
            compiler_params=pltpu.CompilerParams(vmem_limit_bytes=limit),
        )(*args)

    return run


def fetch_body(*refs):
    fields, (tile_ref, strip_ref, sems) = refs[:7], refs[7:]
    cols = tile_ref.shape[1]
    copies = []
    at = 0
    for i, ref in enumerate(fields):
        rows = ref.shape[0]
        copies.append(
            pltpu.make_async_copy(ref, tile_ref.at[at : at + rows, :], sems.at[i])
        )
        at += rows
    for copy in copies:
        copy.start()
    for copy in copies:
        copy.wait()
    strip_ref[...] = jnp.where(
        lax.axis_index("sy") == 0, tile_ref[:, cols - LANES :], tile_ref[:, :LANES]
    )


def edges_of(tile_rows):
    return (HALO,) * 5 + (SUB,) * 2


def window_body(count, rows, tile_ref, strip_ref, *refs):
    states, adjoints = refs[:count], refs[count : 2 * count]
    coef_ref, down_ref, up_ref, ext = refs[2 * count :]
    me = lax.axis_index("tm")
    first = lax.axis_index("sy") == 0
    cols = tile_ref.shape[1]
    strip = strip_ref[...]
    zero = jnp.zeros_like(strip)
    ext[:, 0:LANES] = jnp.where(first, zero, strip)
    ext[:, LANES : LANES + cols] = tile_ref[...]
    ext[:, LANES + cols : 2 * LANES + cols] = jnp.where(first, strip, zero)
    wide = cols // count

    def window(lo, hi, t):
        start = LANES - SIDE + wide * t
        base = pl.multiple_of((start // LANES) * LANES, LANES)
        shift = 2 * LANES - start % LANES
        return pltpu.roll(ext[lo:hi, pl.ds(base, 2 * LANES)], shift, 1)[:, :LANES]

    for d in range(count):
        states[d][...] = window(0, 2 * rows, me ^ d)
        adjoints[d][...] = window(2 * rows, 4 * rows, me ^ d)
    coef_ref[...] = window(4 * rows, 11 * rows, me)
    at = 0
    for f, size in enumerate(edges_of(rows)):
        down_ref[at : at + size, :] = coef_ref[(f + 1) * rows - size : (f + 1) * rows, :]
        up_ref[at : at + size, :] = coef_ref[f * rows : f * rows + size, :]
        at += size


def interleave_body(count, halo, *refs):
    cens, (mid, down_ref, up_ref) = refs[:count], refs[count:]
    rows = cens[0].shape[0] // 2
    me = lax.axis_index("tm")
    for d in range(count):
        slab = me ^ d
        g, j = slab // PER_GROUP, slab % PER_GROUP
        for sp in range(2):
            mid[g, pl.ds(sp * PER_GROUP + j, rows, stride=SUB), :] = cens[d][
                sp * rows : (sp + 1) * rows, :
            ]
    size = halo * SUB
    down_ref[...] = mid[:, (rows - halo) * SUB :, :]
    up_ref[...] = mid[:, 0:size, :]


def blocks(lo, hi):
    return [(r, min(r + BLOCK, hi)) for r in range(lo, hi, BLOCK)]


def shift(value, by):
    n = value.shape[0] // SUB
    return pltpu.roll(value.reshape(n, SUB, LANES), by, 1).reshape(n * SUB, LANES)


def at_rows(ref, lo, hi):
    return ref[lo * SUB : hi * SUB, :]


def masked(flag, value):
    return jnp.where(flag, value, jnp.zeros_like(value))


def each_group(groups, fn):
    if groups == 1:
        fn(0)
    else:
        lax.fori_loop(0, groups, lambda g, c: (fn(g), c)[1], 0)


def through_groups(groups, fn, carry):
    if groups == 1:
        fn(0, carry)
    else:
        lax.fori_loop(0, groups, fn, carry)


def slab_of(a, b):
    return lax.broadcasted_iota(jnp.int32, ((b - a) * SUB, LANES), 0) % PER_GROUP


def step(src, dst, lo, hi, off, cv, ce, cd, cx, cq=None):
    for a, b in blocks(lo, hi):
        u = at_rows(src, a - off, b - off)
        e = at_rows(ce, a, b)
        new = (
            at_rows(cd, a, b) * u
            + at_rows(cv, a, b) * at_rows(src, a - off - 1, b - off - 1)
            + at_rows(cv, a + 1, b + 1) * at_rows(src, a - off + 1, b - off + 1)
            + e * pltpu.roll(u, LANES - 1, 1)
            + pltpu.roll(e * u, 1, 1)
            + at_rows(cx, a, b) * shift(u, PER_GROUP)
        )
        if cq is not None:
            new = new + at_rows(cq, a, b)
        dst[(a - off) * SUB : (b - off) * SUB, :] = new


def sweep(groups, work, lo, hi, *coefs):
    def turn(t, carry):
        src = jnp.where(t == 0, 0, 1 + (t + 1) % 2)
        dst = 1 + t % 2
        each_group(groups, lambda g: step(work.at[src, g], work.at[dst, g], lo, hi, 0, *coefs))
        return carry

    lax.fori_loop(0, STEPS, turn, 0)
    return 1 + (STEPS - 1) % 2


def coarse(gd, cx, value, a, b):
    return at_rows(gd, a, b) * value + (STEPS * at_rows(cx, a, b)) * shift(value, PER_GROUP)


def load(groups, work, tile_rows, halo, mid, top_ref, bot_ref):
    s_at = lax.axis_index("sx")
    has_top = s_at > 0
    has_bot = s_at < lax.axis_size("sx") - 1
    end = HALO + tile_rows

    def one(g):
        work[0, g, (HALO - halo) * SUB : HALO * SUB, :] = masked(has_top, top_ref[g])
        work[0, g, HALO * SUB : end * SUB, :] = mid[g]
        work[0, g, end * SUB : (end + halo) * SUB, :] = masked(has_bot, bot_ref[g])

    each_group(groups, one)


def state_body(count, tile_rows, wide, mid, top_ref, bot_ref, coef_ref, ctop_ref, cbot_ref, *rest):
    hist, last_ref, cv, ce, cd, cx, gd, work, cq, tg, flat = rest
    groups = count // PER_GROUP
    total = tile_rows + 2 * HALO
    end = HALO + tile_rows
    me = lax.axis_index("tm")
    s_at = lax.axis_index("sx")
    has_top = s_at > 0
    has_bot = s_at < lax.axis_size("sx") - 1

    at = 0
    fields = []
    for f, size in enumerate(edges_of(tile_rows)):
        flat[f, HALO - size : HALO, :] = masked(has_top, ctop_ref[at : at + size, :])
        flat[f, HALO:end, :] = coef_ref[f * tile_rows : (f + 1) * tile_rows, :]
        flat[f, end : end + size, :] = masked(has_bot, cbot_ref[at : at + size, :])
        fields.append(flat[f])
        at += size
    k, rate, coupling, q0, q1, t0, t1 = fields
    row = lax.broadcasted_iota(jnp.int32, (total, LANES), 0) + (s_at * tile_rows - HALO)
    col = lax.broadcasted_iota(jnp.int32, (total, LANES), 1) + (
        lax.axis_index("sy") * (wide * count) + me * wide - SIDE
    )
    all_rows = tile_rows * lax.axis_size("sx")
    all_cols = wide * count * lax.axis_size("sy")
    half = 0.5 * TIME_STEP
    above = half * (k + pltpu.roll(k, 1, 0))
    below = half * (k + pltpu.roll(k, total - 1, 0))
    east = half * (k + pltpu.roll(k, LANES - 1, 1))
    west = half * (k + pltpu.roll(k, 1, 1))
    faces = above + below + east + west
    above = jnp.where((row >= 1) & (row < all_rows), above, 0.0)
    east = jnp.where((col >= 0) & (col < all_cols - 1), east, 0.0)
    react = TIME_STEP * rate
    cross = react * coupling
    for sp, source in ((0, q0), (1, q1)):
        spread = (
            (cv, DIFFUSION[sp] * above),
            (ce, DIFFUSION[sp] * east),
            (cd, 1.0 - DIFFUSION[sp] * faces - DECAY[sp] * react),
            (cx, cross),
            (cq, TIME_STEP * source),
            (gd, 1.0 - (DECAY[sp] * STEPS) * react),
        )
        for ref, value in spread:
            for j in range(PER_GROUP):
                ref[pl.ds(sp * PER_GROUP + j, total, stride=SUB), :] = value
    tg[pl.ds(PER_GROUP - 1, total, stride=SUB), :] = t0
    tg[pl.ds(SUB - 1, total, stride=SUB), :] = t1

    lo, hi = STEPS, total - STEPS
    load(groups, work, tile_rows, HALO, mid, top_ref, bot_ref)
    last = sweep(groups, work, 1, total - 1, cv, ce, cd, cx, cq)
    for a, b in blocks(lo, hi):
        slab = slab_of(a, b)

        def chain(g, carry, a=a, b=b, slab=slab):
            x = at_rows(work.at[last, g], a, b) - coarse(
                gd, cx, at_rows(work.at[0, g], a, b), a, b
            )
            value = carry
            for _ in range(PER_GROUP - 1):
                value = jnp.where(
                    slab == 0, carry, shift(coarse(gd, cx, value, a, b) + x, 1)
                )
            hist[0, g, (a - lo) * SUB : (b - lo) * SUB, :] = value
            return shift(coarse(gd, cx, value, a, b) + x, SUB - PER_GROUP + 1)

        through_groups(groups, chain, jnp.zeros(((b - a) * SUB, LANES), jnp.float32))

    def forward(t, carry):
        each_group(
            groups,
            lambda g: step(
                hist.at[t, g], hist.at[t + 1, g], lo + 1, hi - 1, lo, cv, ce, cd, cx, cq
            ),
        )
        return carry

    lax.fori_loop(0, STEPS, forward, 0)
    w_lo, w_hi = 2 * STEPS, total - 2 * STEPS
    last_ref[...] = at_rows(hist.at[STEPS, groups - 1], w_lo - lo, w_hi - lo) - at_rows(
        tg, w_lo, w_hi
    )


def adjoint_body(count, tile_rows, mid, top_ref, bot_ref, hist, last_ref, cv, ce, cd, cx, gd, *rest):
    outs = rest[:count]
    work, lag, fv, fh = rest[count:]
    groups = count // PER_GROUP
    total = tile_rows + 2 * HALO
    end = HALO + tile_rows
    lo = STEPS
    me = lax.axis_index("tm")
    load(groups, work, tile_rows, HALO_W, mid, top_ref, bot_ref)
    last = sweep(groups, work, STEPS + 1, total - STEPS - 1, cv, ce, cd, cx)
    w_lo, w_hi = 2 * STEPS, total - 2 * STEPS
    for a, b in blocks(w_lo, w_hi):
        slab = slab_of(a, b)

        def keep(g, a=a, b=b):
            lag[g, (a - w_lo) * SUB : (b - w_lo) * SUB, :] = at_rows(
                work.at[last, g], a, b
            ) - coarse(gd, cx, at_rows(work.at[0, g], a, b), a, b)

        each_group(groups, keep)

        def chain(turn, carry, a=a, b=b, slab=slab):
            g = groups - 1 - turn
            y = lag[g, (a - w_lo) * SUB : (b - w_lo) * SUB, :]
            top = jnp.where(slab == PER_GROUP - 1, carry, 0.0)
            value = top
            for _ in range(PER_GROUP - 1):
                value = jnp.where(
                    slab == PER_GROUP - 1,
                    top,
                    shift(coarse(gd, cx, value, a, b) + y, SUB - 1),
                )
            work[0, g, a * SUB : b * SUB, :] = value
            return shift(coarse(gd, cx, value, a, b) + y, PER_GROUP - 1)

        through_groups(groups, chain, at_rows(last_ref, a - w_lo, b - w_lo))

    lane = lax.broadcasted_iota(jnp.int32, (tile_rows, LANES), 1)
    left = lane < LANES // 2

    def paired(first, second):
        return jnp.where(
            left,
            pltpu.roll(first, LANES - SIDE, 1),
            pltpu.roll(second, LANES // 2 - SIDE, 1),
        )

    for d in range(count):
        slab = me ^ d
        g, j = slab // PER_GROUP, slab % PER_GROUP
        s_rows = [
            hist[0, g, pl.ds((HALO - lo) * SUB + sp * PER_GROUP + j, tile_rows, stride=SUB), :]
            for sp in range(2)
        ]
        w_rows = [
            work[0, g, pl.ds(HALO * SUB + sp * PER_GROUP + j, tile_rows, stride=SUB), :]
            for sp in range(2)
        ]
        outs[d][0:tile_rows, :] = paired(*s_rows)
        outs[d][tile_rows : 2 * tile_rows, :] = paired(*w_rows)

    fv[...] = jnp.zeros_like(fv)
    fh[...] = jnp.zeros_like(fh)

    def products(u, w):
        for a, b in blocks(HALO, end + 1):
            at = slice((a - HALO) * SUB, (b - HALO) * SUB)
            uc, wc = at_rows(u, a - lo, b - lo), at_rows(w, a, b)
            fv[at, :] += (uc - at_rows(u, a - lo - 1, b - lo - 1)) * (
                wc - at_rows(w, a - 1, b - 1)
            )
            if b <= end:
                fh[at, :] += (pltpu.roll(uc, LANES - 1, 1) - uc) * (
                    pltpu.roll(wc, LANES - 1, 1) - wc
                )

    def back(t, carry):
        src = jnp.where(t == 0, 0, 1 + (t + 1) % 2)
        dst = 1 + t % 2

        def one(g):
            products(hist.at[STEPS - 1 - t, g], work.at[src, g])
            step(work.at[src, g], work.at[dst, g], w_lo + 1, w_hi - 1, 0, cv, ce, cd, cx)

        each_group(groups, one)
        return carry

    lax.fori_loop(0, STEPS - 1, back, 0)
    last = 1 + (STEPS - 2) % 2
    each_group(groups, lambda g: products(hist.at[0, g], work.at[last, g]))

    size = tile_rows * SUB
    fh[...] = fv[0:size, :] + fv[SUB : size + SUB, :] + fh[...] + pltpu.roll(fh[...], 1, 1)
    summed = []
    for sp in range(2):
        parts = [
            fh[pl.ds(sp * PER_GROUP + j, tile_rows, stride=SUB), :] for j in range(PER_GROUP)
        ]
        summed.append((parts[0] + parts[1]) + (parts[2] + parts[3]))
    gradient = (-0.5 * TIME_STEP) * (DIFFUSION[0] * summed[0] + DIFFUSION[1] * summed[1])
    middle = tile_rows // 2
    fold = jnp.where(
        left[:middle],
        pltpu.roll(gradient[:middle], LANES - SIDE, 1),
        pltpu.roll(gradient[middle:], LANES // 2 - SIDE, 1),
    )
    for d in range(count):
        outs[d][2 * tile_rows :, :] = fold


def collect_body(count, wide, *refs):
    parts = refs[:count]
    s_ref, w_ref, g_ref, held = refs[count:]
    me = lax.axis_index("tm")
    for d in range(count):
        held[me ^ d] = parts[d][...]
    rows = g_ref.shape[0]
    middle = rows // 2
    per = LANES // wide
    lane = lax.broadcasted_iota(jnp.int32, (rows, LANES), 1)

    def joined(lo, hi, start, v):
        value = None
        for i in range(per):
            t = v * per + i
            piece = held[t, lo:hi, :]
            turn = (i * wide - start) % LANES
            if turn:
                piece = pltpu.roll(piece, turn, 1)
            value = piece if i == 0 else jnp.where(lane[: hi - lo] >= i * wide, piece, value)
        return value

    for v in range(count // per):
        at = slice(v * LANES, (v + 1) * LANES)
        for sp in range(2):
            start = sp * (LANES // 2)
            s_ref[sp * rows : (sp + 1) * rows, at] = joined(0, rows, start, v)
            w_ref[sp * rows : (sp + 1) * rows, at] = joined(rows, 2 * rows, start, v)
            g_ref[sp * middle : (sp + 1) * middle, at] = joined(
                2 * rows, 2 * rows + middle, start, v
            )


def local(state_guess, adjoint_guess, diffusivity, decay_rate, coupling, control, target):
    rows, cols = diffusivity.shape
    count = lax.axis_size("tm")
    groups = count // PER_GROUP
    wide = cols // count
    total = rows + 2 * HALO
    fields = (
        state_guess.reshape(2 * rows, cols),
        adjoint_guess.reshape(2 * rows, cols),
        diffusivity,
        decay_rate,
        coupling,
        control.reshape(2 * rows, cols),
        target.reshape(2 * rows, cols),
    )

    def exchanged(parts):
        return [parts[0]] + [
            lax.ppermute(parts[d], "tm", [(i, i ^ d) for i in range(count)])
            for d in range(1, count)
        ]

    def turned(down, up):
        n = lax.axis_size("sx")
        return (
            lax.ppermute(down, "sx", [(i, (i + 1) % n) for i in range(n)]),
            lax.ppermute(up, "sx", [((i + 1) % n, i) for i in range(n)]),
        )

    tile, strip = call(
        fetch_body,
        [(11 * rows, cols), (11 * rows, LANES)],
        [pltpu.SemaphoreType.DMA((7,))],
        inputs=[HBM_SPEC] * 7,
    )(*[pltpu.with_memory_space_constraint(f, pltpu.HBM) for f in fields])
    strip = lax.ppermute(strip, "sy", [(0, 1), (1, 0)])
    edge = (sum(edges_of(rows)), LANES)
    windows = call(
        functools.partial(window_body, count, rows),
        [(2 * rows, LANES)] * (2 * count) + [(7 * rows, LANES), edge, edge],
        [pltpu.VMEM((11 * rows, cols + 2 * LANES), jnp.float32)],
    )(tile, strip)
    coef, down, up = windows[2 * count :]
    states = exchanged(windows[:count])
    adjoints = exchanged(windows[count : 2 * count])
    coef_halo = turned(down, up)

    def interleaved(parts, halo):
        mid, down, up = call(
            functools.partial(interleave_body, count, halo),
            [(groups, rows * SUB, LANES)] + [(groups, halo * SUB, LANES)] * 2,
        )(*parts)
        return (mid, *turned(down, up))

    plain = (total * SUB, LANES)
    work = pltpu.VMEM((3, groups, total * SUB, LANES), jnp.float32)
    limit = 60 << 20 if groups > 1 else 32 << 20
    kept = call(
        functools.partial(state_body, count, rows, wide),
        [
            (STEPS + 1, groups, (total - 2 * STEPS) * SUB, LANES),
            ((total - 4 * STEPS) * SUB, LANES),
            *([plain] * 5),
        ],
        [
            work,
            pltpu.VMEM(plain, jnp.float32),
            pltpu.VMEM(plain, jnp.float32),
            pltpu.VMEM((7, total, LANES), jnp.float32),
        ],
        limit,
    )(*interleaved(states, HALO), coef, *coef_halo)
    outs = call(
        functools.partial(adjoint_body, count, rows),
        [(2 * rows + rows // 2, LANES)] * count,
        [
            work,
            pltpu.VMEM((groups, (total - 4 * STEPS) * SUB, LANES), jnp.float32),
            pltpu.VMEM(((rows + 1) * SUB, LANES), jnp.float32),
            pltpu.VMEM((rows * SUB, LANES), jnp.float32),
        ],
        limit,
    )(*interleaved(adjoints, HALO_W), *kept)
    outs = exchanged(outs)
    states, adjoints, gradient = call(
        functools.partial(collect_body, count, wide),
        [(2 * rows, cols), (2 * rows, cols), (rows, cols)],
        [pltpu.VMEM((count, 2 * rows + rows // 2, LANES), jnp.float32)],
    )(*outs)
    return (
        states.reshape(1, 2, rows, cols),
        adjoints.reshape(1, 2, rows, cols),
        gradient,
    )


def solution(mesh):
    placed = (
        P("tm", None, "sx", "sy"),
        P("tm", None, "sx", "sy"),
        P("sx", "sy"),
        P("sx", "sy"),
        P("sx", "sy"),
        P(None, "sx", "sy"),
        P(None, "sx", "sy"),
    )
    return jax.shard_map(
        local,
        mesh=mesh,
        in_specs=placed,
        out_specs=(P("tm", None, "sx", "sy"), P("tm", None, "sx", "sy"), P("sx", "sy")),
        check_vma=False,
    )
```

time: 61.4 us -> 50.7 us (0.83)
  waiting for transfers between devices: 26 us -> 4.73 us
  starting transfers between devices: 14.9 us -> 29.6 us
  local copies, waits for them, and re-layouts: 6.13 us -> 0 us
  Pallas kernels: 13.4 us -> 15.5 us
    ppermute x8 -> x15, waiting for transfers between devices: 24.7 us -> 3.43 us  [the longest x9 3.42 us: exchanged(): lax.ppermute(parts[d], 'tm', [(i, i ^ d) for i in range(count)])]
    ppermute x8 -> x15, starting transfers between devices: 14.4 us -> 29.1 us  [the longest x9 19.2 us: exchanged(): lax.ppermute(parts[d], 'tm', [(i, i ^ d) for i in range(count)])]
    unnamed x14 -> x0, local copies, waits for them, and re-layouts: 6.13 us -> none
    pallas_call x5 -> x7, Pallas kernels: 13.4 us -> 15.5 us  [run(): pl.pallas_call(body, out_shape=[jax.ShapeDtypeStruct(s, jnp.float32) for...]
  transfers between devices with their start and end apart: 9 -> 16, of which waited for: 7 -> 4; matrix products, arithmetic and copies ran while one was open for 0% -> 0% of each run, Pallas kernels for 0% -> 13%
where the time goes in v2:
time: 50.7 us; the launch traced here: 50.6 us
  starting transfers between devices  29.6 us (58%)
  Pallas kernels  15.5 us (31%)
  waiting for transfers between devices  4.73 us (9%)
  between operations  0.73 us (1%)
    ppermute x9, starting transfers between devices, exchanged(): lax.ppermute(parts[d], 'tm', [(i, i ^ d) for i in range(count)])  19.2 us
    pallas_call x7, Pallas kernels, run(): pl.pallas_call(body, out_shape=[jax.ShapeDtypeStruct(s, jnp.float32) for...  15.5 us
    ppermute x3, starting transfers between devices, turned(): lax.ppermute(up, 'sx', [((i + 1) % n, i) for i in range(n)])  8.32 us
    ppermute x9, waiting for transfers between devices, exchanged(): lax.ppermute(parts[d], 'tm', [(i, i ^ d) for i in range(count)])  3.42 us
    ppermute x3, starting transfers between devices, turned(): lax.ppermute(down, 'sx', [(i, (i + 1) % n) for i in range(n)])  1.55 us
    ppermute x1, waiting for transfers between devices, local(): strip = lax.ppermute(strip, 'sy', [(0, 1), (1, 0)])  1.3 us
  transfers between devices with their start and end apart: 16, of which 4 were waited for; matrix products, arithmetic and copies ran while one was open for 0% of the time, Pallas kernels for 13%

profile of v2, /device:TPU:0, one launch (start us, length us, event | category | flops | bytes accessed | tf_op | source)
XLA Modules:
  0.0 50.6 jit_solution(5293501128611794700)
XLA Ops:
  0.6 1.3 %shard_map.94 = (f32[704,256]{1,0:T(8,128)S(1)}, f32[704,128]{1,0:T(8,128)S(1)}) custom-call(f32[128,256]{1,0:T(8,128)} %bitcast.6, f32[128,256]{1,0:T(8,128)} %bitcast.7, f32[64,256]{1,0:T(8,128)} %refs_2_.1, f32[64,256]{1,0:T(8,128)} %refs_3_.1, f32[64,256]{1,0:T(8,128)} %refs_4_.1, f32[128,256]{1,0:T(8,128)} %bitcast.8, f32[128,256]{1,0:T(8,128)} %bitcast.9), custom_call_target="tpu_custom_call" | custom-call | tf_op jit(solution)/shard_map/pallas_call | solution.py:29
  1.9 0.5 %collective-permute-start = (f32[704,128]{1,0:T(8,128)S(1)}, f32[704,128]{1,0:T(8,128)S(1)}, u32[]{:S(2)}, u32[]{:S(2)}) collective-permute-start(f32[704,128]{1,0:T(8,128)S(1)} %get-tuple-element.37), channel_id=1, source_target_pairs={{0,1},{1,0},{2,3},{3,2},{4,5},{5,4},{6,7},{7,6},{8,9},{9,8},{10,11... | collective-permute-start | bytes 1081352 | tf_op jit(solution)/shard_map/ppermute | solution.py:456
  2.5 1.3 %collective-permute-done.strip_ref = f32[704,128]{1,0:T(8,128)S(1)} collective-permute-done((f32[704,128]{1,0:T(8,128)S(1)}, f32[704,128]{1,0:T(8,128)S(1)}, u32[]{:S(2)}, u32[]{:S(2)}) %collective-permute-start) | collective-permute-done | bytes 360480 | tf_op jit(solution)/shard_map/ppermute | solution.py:456
  3.8 0.6 %shard_map.95 = (f32[128,128]{1,0:T(8,128)S(1)}, f32[128,128]{1,0:T(8,128)S(1)}, f32[128,128]{1,0:T(8,128)S(1)}, f32[128,128]{1,0:T(8,128)S(1)}, f32[128,128]{1,...) custom-call(f32[704,256]{1,0:T(8,128)S(1)} %get-tuple-element.36.til, ...), custom_call_target="tpu_custom_call" | custom-call | tf_op jit(solution)/shard_map/pallas_call | solution.py:29
  4.4 3.0 %collective-permute-start.6 = (f32[128,128]{1,0:T(8,128)S(1)}, f32[128,128]{1,0:T(8,128)S(1)}, u32[]{:S(2)}, u32[]{:S(2)}) collective-permute-start(f32[128,128]{1,0:T(8,128)S(1)} %get-tuple-element.46), channel_id=1, source_target_pairs={{0,8},{8,0},{16,24},{24,16},{1,9},{9,1},{17,25},{25,17},{2,10},{10... | collective-permute-start | bytes 196616 | tf_op jit(solution)/shard_map/ppermute | solution.py:439
  7.4 2.6 %collective-permute-start.7 = (f32[128,128]{1,0:T(8,128)S(1)}, f32[128,128]{1,0:T(8,128)S(1)}, u32[]{:S(2)}, u32[]{:S(2)}) collective-permute-start(f32[128,128]{1,0:T(8,128)S(1)} %get-tuple-element.47), channel_id=1, source_target_pairs={{0,16},{8,24},{16,0},{24,8},{1,17},{9,25},{17,1},{25,9},{2,18},{10... | collective-permute-start | bytes 196616 | tf_op jit(solution)/shard_map/ppermute | solution.py:439
  10.0 0.0 collective-permute-start.8
  10.0 0.9 %collective-permute-start.1 = (f32[128,128]{1,0:T(8,128)S(1)}, f32[128,128]{1,0:T(8,128)S(1)}, u32[]{:S(2)}, u32[]{:S(2)}) collective-permute-start(f32[128,128]{1,0:T(8,128)S(1)} %get-tuple-element.39), channel_id=1, source_target_pairs={{0,8},{8,0},{16,24},{24,16},{1,9},{9,1},{17,25},{25,17},{2,10},{10... | collective-permute-start | bytes 196616 | tf_op jit(solution)/shard_map/ppermute | solution.py:439
  10.9 3.5 %collective-permute-start.2 = (f32[128,128]{1,0:T(8,128)S(1)}, f32[128,128]{1,0:T(8,128)S(1)}, u32[]{:S(2)}, u32[]{:S(2)}) collective-permute-start(f32[128,128]{1,0:T(8,128)S(1)} %get-tuple-element.40), channel_id=1, source_target_pairs={{0,16},{8,24},{16,0},{24,8},{1,17},{9,25},{17,1},{25,9},{2,18},{10... | collective-permute-start | bytes 196616 | tf_op jit(solution)/shard_map/ppermute | solution.py:439
  14.3 0.0 collective-permute-done.6.refs_1_
  14.3 1.5 %collective-permute-start.11 = (f32[136,128]{1,0:T(8,128)S(1)}, f32[136,128]{1,0:T(8,128)S(1)}, u32[]{:S(2)}, u32[]{:S(2)}) collective-permute-start(f32[136,128]{1,0:T(8,128)S(1)} %get-tuple-element.53), channel_id=1, source_target_pairs={{0,2},{2,4},{4,6},{6,0},{1,3},{3,5},{5,7},{7,1},{8,10},{10,12},{12... | collective-permute-start | bytes 208904 | tf_op jit(solution)/shard_map/ppermute | solution.py:446
  15.8 0.0 collective-permute-done.7.refs_2_
  15.8 4.8 %collective-permute-start.3 = (f32[128,128]{1,0:T(8,128)S(1)}, f32[128,128]{1,0:T(8,128)S(1)}, u32[]{:S(2)}, u32[]{:S(2)}) collective-permute-start(f32[128,128]{1,0:T(8,128)S(1)} %get-tuple-element.41), channel_id=1, source_target_pairs={{0,24},{8,16},{16,8},{24,0},{1,25},{9,17},{17,9},{25,1},{2,26},{10... | collective-permute-start | bytes 196616 | tf_op jit(solution)/shard_map/ppermute | solution.py:439
  20.6 0.0 collective-permute-done.8.refs_3_
  20.6 0.1 shard_map.97
  20.7 2.5 %collective-permute-start.10 = (f32[1,192,128]{2,1,0:T(8,128)S(1)}, f32[1,192,128]{2,1,0:T(8,128)S(1)}, u32[]{:S(2)}, u32[]{:S(2)}) collective-permute-start(f32[1,192,128]{2,1,0:T(8,128)S(1)} %get-tuple-element.51), channel_id=1, source_target_pairs={{2,0},{4,2},{6,4},{0,6},{3,1},{5,3},{7,5},{1,7},{10,8},{12,10},{14... | collective-permute-start | bytes 294920 | tf_op jit(solution)/shard_map/ppermute | solution.py:447
  23.2 0.0 collective-permute-done.1.refs_1_
  23.2 0.0 collective-permute-start.9
  23.2 0.0 collective-permute-done.2.refs_2_
  23.2 2.9 %collective-permute-start.12 = (f32[136,128]{1,0:T(8,128)S(1)}, f32[136,128]{1,0:T(8,128)S(1)}, u32[]{:S(2)}, u32[]{:S(2)}) collective-permute-start(f32[136,128]{1,0:T(8,128)S(1)} %get-tuple-element.54), channel_id=1, source_target_pairs={{2,0},{4,2},{6,4},{0,6},{3,1},{5,3},{7,5},{1,7},{10,8},{12,10},{14... | collective-permute-start | bytes 208904 | tf_op jit(solution)/shard_map/ppermute | solution.py:447
  26.1 0.0 collective-permute-done.3.refs_3_
  26.2 0.1 shard_map.96
  26.2 0.1 collective-permute-start.4
  26.3 0.0 collective-permute-done.11.ctop_ref
  26.3 2.9 %collective-permute-start.5 = (f32[1,128,128]{2,1,0:T(8,128)S(1)}, f32[1,128,128]{2,1,0:T(8,128)S(1)}, u32[]{:S(2)}, u32[]{:S(2)}) collective-permute-start(f32[1,128,128]{2,1,0:T(8,128)S(1)} %get-tuple-element.44), channel_id=1, source_target_pairs={{2,0},{4,2},{6,4},{0,6},{3,1},{5,3},{7,5},{1,7},{10,8},{12,10},{14... | collective-permute-start | bytes 196616 | tf_op jit(solution)/shard_map/ppermute | solution.py:447
  29.2 0.0 collective-permute-done.12.cbot_ref
  29.2 0.0 collective-permute-done.10.bot_ref
  29.2 0.0 collective-permute-done.9.top_ref
  29.2 6.3 %shard_map.98 = (f32[9,1,768,128]{3,2,1,0:T(8,128)S(1)}, f32[640,128]{1,0:T(8,128)S(1)}, f32[896,128]{1,0:T(8,128)S(1)}, f32[896,128]{1,0:T(8,128)S(1)}, f32[896...) custom-call(f32[1,512,128]{2,1,0:T(8,128)S(1)} %get-tuple-element.49.mid, ...), custom_call_target="tpu_custom_call" | custom-call | tf_op jit(solution)/shard_map/pallas_call | solution.py:29
  35.5 0.0 collective-permute-done.4.top_ref
  35.5 0.0 collective-permute-done.5.bot_ref
  35.5 6.4 %shard_map.99 = (f32[160,128]{1,0:T(8,128)S(1)}, f32[160,128]{1,0:T(8,128)S(1)}, f32[160,128]{1,0:T(8,128)S(1)}, f32[160,128]{1,0:T(8,128)S(1)}) custom-call(f32[1,512,128]{2,1,0:T(8,128)S(1)} %get-tuple-element.42.mid, f32[1,128,128]{2,1,0:T(8,128)S(1)} %collective-permute-done.4.top_ref, f32[1,128,128]{2,1,0:T(8,128)S(1)} %collective-permute-done.5.bot_ref, ...), custom_call_target="tpu_custom_call" | custom-call | tf_op jit(solution)/shard_map/pallas_call | solution.py:29
  41.9 0.1 collective-permute-start.13
  41.9 1.1 %collective-permute-start.14 = (f32[160,128]{1,0:T(8,128)S(1)}, f32[160,128]{1,0:T(8,128)S(1)}, u32[]{:S(2)}, u32[]{:S(2)}) collective-permute-start(f32[160,128]{1,0:T(8,128)S(1)} %get-tuple-element.64), channel_id=1, source_target_pairs={{0,16},{8,24},{16,0},{24,8},{1,17},{9,25},{17,1},{25,9},{2,18},{10... | collective-permute-start | bytes 245768 | tf_op jit(solution)/shard_map/ppermute | solution.py:439
  43.0 3.3 %collective-permute-start.15 = (f32[160,128]{1,0:T(8,128)S(1)}, f32[160,128]{1,0:T(8,128)S(1)}, u32[]{:S(2)}, u32[]{:S(2)}) collective-permute-start(f32[160,128]{1,0:T(8,128)S(1)} %get-tuple-element.65), channel_id=1, source_target_pairs={{0,24},{8,16},{16,8},{24,0},{1,25},{9,17},{17,9},{25,1},{2,26},{10... | collective-permute-start | bytes 245768 | tf_op jit(solution)/shard_map/ppermute | solution.py:439
  46.3 0.1 collective-permute-done.13.refs_1_
  46.4 1.0 %collective-permute-done.14.refs_2_ = f32[160,128]{1,0:T(8,128)S(1)} collective-permute-done((f32[160,128]{1,0:T(8,128)S(1)}, f32[160,128]{1,0:T(8,128)S(1)}, u32[]{:S(2)}, u32[]{:S(2)}) %collective-permute-start.14) | collective-permute-done | bytes 81952 | tf_op jit(solution)/shard_map/ppermute | solution.py:439
  47.3 2.4 %collective-permute-done.15.refs_3_ = f32[160,128]{1,0:T(8,128)S(1)} collective-permute-done((f32[160,128]{1,0:T(8,128)S(1)}, f32[160,128]{1,0:T(8,128)S(1)}, u32[]{:S(2)}, u32[]{:S(2)}) %collective-permute-start.15) | collective-permute-done | bytes 81952 | tf_op jit(solution)/shard_map/ppermute | solution.py:439
  49.7 0.9 %shard_map.100 = (f32[128,256]{1,0:T(8,128)}, f32[128,256]{1,0:T(8,128)}, f32[64,256]{1,0:T(8,128)}) custom-call(f32[160,128]{1,0:T(8,128)S(1)} %get-tuple-element.62.refs_0_, f32[160,128]{1,0:T(8,128)S(1)} %collective-permute-done.13.refs_1_, f32[160,128]{1,0:T(8,128)S(1)} %collective-permute-done.14.refs_2_, f32[160,128]{1,0:T(8,128)S(1)} %collective-permute-done.15.refs_3_), custom_call_target="tpu_custom_call" | custom-call | tf_op jit(solution)/shard_map/pallas_call | solution.py:29
Async XLA Ops:
  1.9 1.8 %collective-permute-start = (f32[704,128]{1,0:T(8,128)S(1)}, f32[704,128]{1,0:T(8,128)S(1)}, u32[]{:S(2)}, u32[]{:S(2)}) collective-permute-start(f32[704,128]{1,0:T(8,128)S(1)} %get-tuple-element.37), channel_id=1, source_target_pairs={{0,1},{1,0},{2,3},{3,2},{4,5},{5,4},{6,7},{7,6},{8,9},{9,8},{10,11... | collective-permute-start | bytes 1081352 | tf_op jit(solution)/shard_map/ppermute | solution.py:456
  4.4 10.0 %collective-permute-start.6 = (f32[128,128]{1,0:T(8,128)S(1)}, f32[128,128]{1,0:T(8,128)S(1)}, u32[]{:S(2)}, u32[]{:S(2)}) collective-permute-start(f32[128,128]{1,0:T(8,128)S(1)} %get-tuple-element.46), channel_id=1, source_target_pairs={{0,8},{8,0},{16,24},{24,16},{1,9},{9,1},{17,25},{25,17},{2,10},{10... | collective-permute-start | bytes 196616 | tf_op jit(solution)/shard_map/ppermute | solution.py:439
  7.4 8.5 %collective-permute-start.7 = (f32[128,128]{1,0:T(8,128)S(1)}, f32[128,128]{1,0:T(8,128)S(1)}, u32[]{:S(2)}, u32[]{:S(2)}) collective-permute-start(f32[128,128]{1,0:T(8,128)S(1)} %get-tuple-element.47), channel_id=1, source_target_pairs={{0,16},{8,24},{16,0},{24,8},{1,17},{9,25},{17,1},{25,9},{2,18},{10... | collective-permute-start | bytes 196616 | tf_op jit(solution)/shard_map/ppermute | solution.py:439
  10.0 10.7 %collective-permute-start.8 = (f32[128,128]{1,0:T(8,128)S(1)}, f32[128,128]{1,0:T(8,128)S(1)}, u32[]{:S(2)}, u32[]{:S(2)}) collective-permute-start(f32[128,128]{1,0:T(8,128)S(1)} %get-tuple-element.48), channel_id=1, source_target_pairs={{0,24},{8,16},{16,8},{24,0},{1,25},{9,17},{17,9},{25,1},{2,26},{10... | collective-permute-start | bytes 196616 | tf_op jit(solution)/shard_map/ppermute | solution.py:439
  10.0 13.3 %collective-permute-start.1 = (f32[128,128]{1,0:T(8,128)S(1)}, f32[128,128]{1,0:T(8,128)S(1)}, u32[]{:S(2)}, u32[]{:S(2)}) collective-permute-start(f32[128,128]{1,0:T(8,128)S(1)} %get-tuple-element.39), channel_id=1, source_target_pairs={{0,8},{8,0},{16,24},{24,16},{1,9},{9,1},{17,25},{25,17},{2,10},{10... | collective-permute-start | bytes 196616 | tf_op jit(solution)/shard_map/ppermute | solution.py:439
  10.9 12.4 %collective-permute-start.2 = (f32[128,128]{1,0:T(8,128)S(1)}, f32[128,128]{1,0:T(8,128)S(1)}, u32[]{:S(2)}, u32[]{:S(2)}) collective-permute-start(f32[128,128]{1,0:T(8,128)S(1)} %get-tuple-element.40), channel_id=1, source_target_pairs={{0,16},{8,24},{16,0},{24,8},{1,17},{9,25},{17,1},{25,9},{2,18},{10... | collective-permute-start | bytes 196616 | tf_op jit(solution)/shard_map/ppermute | solution.py:439
  14.3 12.0 %collective-permute-start.11 = (f32[136,128]{1,0:T(8,128)S(1)}, f32[136,128]{1,0:T(8,128)S(1)}, u32[]{:S(2)}, u32[]{:S(2)}) collective-permute-start(f32[136,128]{1,0:T(8,128)S(1)} %get-tuple-element.53), channel_id=1, source_target_pairs={{0,2},{2,4},{4,6},{6,0},{1,3},{3,5},{5,7},{7,1},{8,10},{10,12},{12... | collective-permute-start | bytes 208904 | tf_op jit(solution)/shard_map/ppermute | solution.py:446
  15.8 10.3 %collective-permute-start.3 = (f32[128,128]{1,0:T(8,128)S(1)}, f32[128,128]{1,0:T(8,128)S(1)}, u32[]{:S(2)}, u32[]{:S(2)}) collective-permute-start(f32[128,128]{1,0:T(8,128)S(1)} %get-tuple-element.41), channel_id=1, source_target_pairs={{0,24},{8,16},{16,8},{24,0},{1,25},{9,17},{17,9},{25,1},{2,26},{10... | collective-permute-start | bytes 196616 | tf_op jit(solution)/shard_map/ppermute | solution.py:439
  20.7 8.5 %collective-permute-start.10 = (f32[1,192,128]{2,1,0:T(8,128)S(1)}, f32[1,192,128]{2,1,0:T(8,128)S(1)}, u32[]{:S(2)}, u32[]{:S(2)}) collective-permute-start(f32[1,192,128]{2,1,0:T(8,128)S(1)} %get-tuple-element.51), channel_id=1, source_target_pairs={{2,0},{4,2},{6,4},{0,6},{3,1},{5,3},{7,5},{1,7},{10,8},{12,10},{14... | collective-permute-start | bytes 294920 | tf_op jit(solution)/shard_map/ppermute | solution.py:447
  23.2 6.0 %collective-permute-start.9 = (f32[1,192,128]{2,1,0:T(8,128)S(1)}, f32[1,192,128]{2,1,0:T(8,128)S(1)}, u32[]{:S(2)}, u32[]{:S(2)}) collective-permute-start(f32[1,192,128]{2,1,0:T(8,128)S(1)} %get-tuple-element.50), channel_id=1, source_target_pairs={{0,2},{2,4},{4,6},{6,0},{1,3},{3,5},{5,7},{7,1},{8,10},{10,12},{12... | collective-permute-start | bytes 294920 | tf_op jit(solution)/shard_map/ppermute | solution.py:446
  23.2 6.0 %collective-permute-start.12 = (f32[136,128]{1,0:T(8,128)S(1)}, f32[136,128]{1,0:T(8,128)S(1)}, u32[]{:S(2)}, u32[]{:S(2)}) collective-permute-start(f32[136,128]{1,0:T(8,128)S(1)} %get-tuple-element.54), channel_id=1, source_target_pairs={{2,0},{4,2},{6,4},{0,6},{3,1},{5,3},{7,5},{1,7},{10,8},{12,10},{14... | collective-permute-start | bytes 208904 | tf_op jit(solution)/shard_map/ppermute | solution.py:447
  26.2 9.3 %collective-permute-start.4 = (f32[1,128,128]{2,1,0:T(8,128)S(1)}, f32[1,128,128]{2,1,0:T(8,128)S(1)}, u32[]{:S(2)}, u32[]{:S(2)}) collective-permute-start(f32[1,128,128]{2,1,0:T(8,128)S(1)} %get-tuple-element.43), channel_id=1, source_target_pairs={{0,2},{2,4},{4,6},{6,0},{1,3},{3,5},{5,7},{7,1},{8,10},{10,12},{12... | collective-permute-start | bytes 196616 | tf_op jit(solution)/shard_map/ppermute | solution.py:446
  26.3 9.2 %collective-permute-start.5 = (f32[1,128,128]{2,1,0:T(8,128)S(1)}, f32[1,128,128]{2,1,0:T(8,128)S(1)}, u32[]{:S(2)}, u32[]{:S(2)}) collective-permute-start(f32[1,128,128]{2,1,0:T(8,128)S(1)} %get-tuple-element.44), channel_id=1, source_target_pairs={{2,0},{4,2},{6,4},{0,6},{3,1},{5,3},{7,5},{1,7},{10,8},{12,10},{14... | collective-permute-start | bytes 196616 | tf_op jit(solution)/shard_map/ppermute | solution.py:447
  41.9 4.5 %collective-permute-start.13 = (f32[160,128]{1,0:T(8,128)S(1)}, f32[160,128]{1,0:T(8,128)S(1)}, u32[]{:S(2)}, u32[]{:S(2)}) collective-permute-start(f32[160,128]{1,0:T(8,128)S(1)} %get-tuple-element.63), channel_id=1, source_target_pairs={{0,8},{8,0},{16,24},{24,16},{1,9},{9,1},{17,25},{25,17},{2,10},{10... | collective-permute-start | bytes 245768 | tf_op jit(solution)/shard_map/ppermute | solution.py:439
  41.9 5.4 %collective-permute-start.14 = (f32[160,128]{1,0:T(8,128)S(1)}, f32[160,128]{1,0:T(8,128)S(1)}, u32[]{:S(2)}, u32[]{:S(2)}) collective-permute-start(f32[160,128]{1,0:T(8,128)S(1)} %get-tuple-element.64), channel_id=1, source_target_pairs={{0,16},{8,24},{16,0},{24,8},{1,17},{9,25},{17,1},{25,9},{2,18},{10... | collective-permute-start | bytes 245768 | tf_op jit(solution)/shard_map/ppermute | solution.py:439
  43.0 6.7 %collective-permute-start.15 = (f32[160,128]{1,0:T(8,128)S(1)}, f32[160,128]{1,0:T(8,128)S(1)}, u32[]{:S(2)}, u32[]{:S(2)}) collective-permute-start(f32[160,128]{1,0:T(8,128)S(1)} %get-tuple-element.65), channel_id=1, source_target_pairs={{0,24},{8,16},{16,8},{24,0},{1,25},{9,17},{17,9},{25,1},{2,26},{10... | collective-permute-start | bytes 245768 | tf_op jit(solution)/shard_map/ppermute | solution.py:439

commit v3 on v2

--- a/solution.py
+++ b/solution.py
@@ -62,34 +62,81 @@
     return (HALO,) * 5 + (SUB,) * 2
 
 
+def extend(ext, lo, hi, tile, strip):
+    first = lax.axis_index("sy") == 0
+    cols = tile.shape[1]
+    zero = jnp.zeros_like(strip)
+    ext[lo:hi, 0:LANES] = jnp.where(first, zero, strip)
+    ext[lo:hi, LANES : LANES + cols] = tile
+    ext[lo:hi, LANES + cols : 2 * LANES + cols] = jnp.where(first, strip, zero)
+
+
+def window(ext, lo, hi, start):
+    start = start + LANES - SIDE
+    base = pl.multiple_of((start // LANES) * LANES, LANES)
+    turn = 2 * LANES - start % LANES
+    return pltpu.roll(ext[lo:hi, pl.ds(base, 2 * LANES)], turn, 1)[:, :LANES]
+
+
 def window_body(count, rows, tile_ref, strip_ref, *refs):
-    states, adjoints = refs[:count], refs[count : 2 * count]
-    coef_ref, down_ref, up_ref, ext = refs[2 * count :]
+    states, (coef_ref, down_ref, up_ref, ext) = refs[:count], refs[count:]
     me = lax.axis_index("tm")
-    first = lax.axis_index("sy") == 0
     cols = tile_ref.shape[1]
-    strip = strip_ref[...]
-    zero = jnp.zeros_like(strip)
-    ext[:, 0:LANES] = jnp.where(first, zero, strip)
-    ext[:, LANES : LANES + cols] = tile_ref[...]
-    ext[:, LANES + cols : 2 * LANES + cols] = jnp.where(first, strip, zero)
     wide = cols // count
-
-    def window(lo, hi, t):
-        start = LANES - SIDE + wide * t
-        base = pl.multiple_of((start // LANES) * LANES, LANES)
-        shift = 2 * LANES - start % LANES
-        return pltpu.roll(ext[lo:hi, pl.ds(base, 2 * LANES)], shift, 1)[:, :LANES]
-
+    extend(ext, 0, 11 * rows, tile_ref[...], strip_ref[...])
     for d in range(count):
-        states[d][...] = window(0, 2 * rows, me ^ d)
-        adjoints[d][...] = window(2 * rows, 4 * rows, me ^ d)
-    coef_ref[...] = window(4 * rows, 11 * rows, me)
+        states[d][...] = window(ext, 0, 2 * rows, wide * (me ^ d))
+    coef_ref[...] = window(ext, 4 * rows, 11 * rows, wide * me)
     at = 0
     for f, size in enumerate(edges_of(rows)):
         down_ref[at : at + size, :] = coef_ref[(f + 1) * rows - size : (f + 1) * rows, :]
         up_ref[at : at + size, :] = coef_ref[f * rows : f * rows + size, :]
         at += size
+    for sp in range(2):
+        lo = (2 + sp) * rows
+        for ref, low in ((down_ref, lo + rows - HALO_W), (up_ref, lo)):
+            here = slice(low, low + HALO_W)
+            for i in range(cols // LANES):
+                ref[at + i * HALO_W : at + (i + 1) * HALO_W, :] = tile_ref[
+                    here, i * LANES : (i + 1) * LANES
+                ]
+            i = cols // LANES
+            ref[at + i * HALO_W : at + (i + 1) * HALO_W, :] = strip_ref[here, :]
+        at += (cols // LANES + 1) * HALO_W
+
+
+def adjoint_window_body(count, rows, tile_ref, strip_ref, top_ref, bot_ref, after, *refs):
+    del after
+    outs, ext = refs[:count], refs[count]
+    me = lax.axis_index("tm")
+    s_at = lax.axis_index("sx")
+    cols = tile_ref.shape[1]
+    wide = cols // count
+    tall = rows + 2 * HALO_W
+    for sp in range(2):
+        lo = (2 + sp) * rows
+        base = sp * tall
+        at = sum(edges_of(rows)) + sp * (cols // LANES + 1) * HALO_W
+        extend(
+            ext,
+            base + HALO_W,
+            base + HALO_W + rows,
+            tile_ref[lo : lo + rows, :],
+            strip_ref[lo : lo + rows, :],
+        )
+        for ref, start, flag in (
+            (top_ref, base, s_at > 0),
+            (bot_ref, base + HALO_W + rows, s_at < lax.axis_size("sx") - 1),
+        ):
+            parts = [
+                masked(flag, ref[at + i * HALO_W : at + (i + 1) * HALO_W, :])
+                for i in range(cols // LANES + 1)
+            ]
+            extend(
+                ext, start, start + HALO_W, jnp.concatenate(parts[:-1], axis=1), parts[-1]
+            )
+    for d in range(count):
+        outs[d][...] = window(ext, 0, 2 * tall, wide * (me ^ d))
 
 
 def interleave_body(count, halo, *refs):
@@ -143,62 +190,64 @@
     return lax.broadcasted_iota(jnp.int32, ((b - a) * SUB, LANES), 0) % PER_GROUP
 
 
-def step(src, dst, lo, hi, off, cv, ce, cd, cx, cq=None):
+def step(src, dst, lo, hi, coefs, seen=None):
+    cv, ce, cd, cx = coefs[:4]
     for a, b in blocks(lo, hi):
-        u = at_rows(src, a - off, b - off)
+        n = (b - a) * SUB
+        rows = at_rows(src, a - 1, b + 1)
+        face = at_rows(cv, a, b + 1)
+        u = rows[SUB : SUB + n]
         e = at_rows(ce, a, b)
-        new = (
-            at_rows(cd, a, b) * u
-            + at_rows(cv, a, b) * at_rows(src, a - off - 1, b - off - 1)
-            + at_rows(cv, a + 1, b + 1) * at_rows(src, a - off + 1, b - off + 1)
-            + e * pltpu.roll(u, LANES - 1, 1)
-            + pltpu.roll(e * u, 1, 1)
-            + at_rows(cx, a, b) * shift(u, PER_GROUP)
-        )
-        if cq is not None:
-            new = new + at_rows(cq, a, b)
-        dst[(a - off) * SUB : (b - off) * SUB, :] = new
-
-
-def sweep(groups, work, lo, hi, *coefs):
+        east = pltpu.roll(u, LANES - 1, 1)
+        new = at_rows(cd, a, b) * u + face[:n] * rows[:n] + face[SUB:] * rows[2 * SUB :]
+        if len(coefs) > 4:
+            new = new + at_rows(coefs[4], a, b)
+        new = new + (e * east + pltpu.roll(e * u, 1, 1))
+        new = new + at_rows(cx, a, b) * shift(u, PER_GROUP)
+        dst[a * SUB : b * SUB, :] = new
+        if seen is not None:
+            seen(a, b, rows[:n], u, east, new)
+
+
+def sweep(groups, one, two, lo, hi, coefs):
     def turn(t, carry):
-        src = jnp.where(t == 0, 0, 1 + (t + 1) % 2)
-        dst = 1 + t % 2
-        each_group(groups, lambda g: step(work.at[src, g], work.at[dst, g], lo, hi, 0, *coefs))
+        def run(g):
+            step(one.at[g], two.at[g], lo, hi, coefs)
+            step(two.at[g], one.at[g], lo, hi, coefs)
+
+        each_group(groups, run)
         return carry
 
-    lax.fori_loop(0, STEPS, turn, 0)
-    return 1 + (STEPS - 1) % 2
+    lax.fori_loop(0, STEPS // 2, turn, 0)
 
 
 def coarse(gd, cx, value, a, b):
     return at_rows(gd, a, b) * value + (STEPS * at_rows(cx, a, b)) * shift(value, PER_GROUP)
 
 
-def load(groups, work, tile_rows, halo, mid, top_ref, bot_ref):
+def load(groups, refs, tile_rows, halo, mid, top_ref, bot_ref):
     s_at = lax.axis_index("sx")
     has_top = s_at > 0
     has_bot = s_at < lax.axis_size("sx") - 1
     end = HALO + tile_rows
 
     def one(g):
-        work[0, g, (HALO - halo) * SUB : HALO * SUB, :] = masked(has_top, top_ref[g])
-        work[0, g, HALO * SUB : end * SUB, :] = mid[g]
-        work[0, g, end * SUB : (end + halo) * SUB, :] = masked(has_bot, bot_ref[g])
+        for ref in refs:
+            ref[g, (HALO - halo) * SUB : HALO * SUB, :] = masked(has_top, top_ref[g])
+            ref[g, HALO * SUB : end * SUB, :] = mid[g]
+            ref[g, end * SUB : (end + halo) * SUB, :] = masked(has_bot, bot_ref[g])
 
     each_group(groups, one)
 
 
-def state_body(count, tile_rows, wide, mid, top_ref, bot_ref, coef_ref, ctop_ref, cbot_ref, *rest):
-    hist, last_ref, cv, ce, cd, cx, gd, work, cq, tg, flat = rest
-    groups = count // PER_GROUP
+def coef_body(count, tile_rows, wide, coef_ref, ctop_ref, cbot_ref, *rest):
+    cv, ce, cd, cx, cq, gd, tg, flat = rest
     total = tile_rows + 2 * HALO
     end = HALO + tile_rows
     me = lax.axis_index("tm")
     s_at = lax.axis_index("sx")
     has_top = s_at > 0
     has_bot = s_at < lax.axis_size("sx") - 1
-
     at = 0
     fields = []
     for f, size in enumerate(edges_of(tile_rows)):
@@ -232,69 +281,97 @@
             (cx, cross),
             (cq, TIME_STEP * source),
             (gd, 1.0 - (DECAY[sp] * STEPS) * react),
+            (tg, (t0, t1)[sp]),
         )
         for ref, value in spread:
             for j in range(PER_GROUP):
                 ref[pl.ds(sp * PER_GROUP + j, total, stride=SUB), :] = value
-    tg[pl.ds(PER_GROUP - 1, total, stride=SUB), :] = t0
-    tg[pl.ds(SUB - 1, total, stride=SUB), :] = t1
-
+
+
+def state_body(
+    count, tile_rows, mid, top_ref, bot_ref, cv, ce, cd, cx, cq, gd, tg, hist, slope, last_ref, *rest
+):
+    guess, one, two = rest
+    groups = count // PER_GROUP
+    total = tile_rows + 2 * HALO
+    coefs = (cv, ce, cd, cx, cq)
     lo, hi = STEPS, total - STEPS
-    load(groups, work, tile_rows, HALO, mid, top_ref, bot_ref)
-    last = sweep(groups, work, 1, total - 1, cv, ce, cd, cx, cq)
+    load(groups, (guess, one), tile_rows, HALO, mid, top_ref, bot_ref)
+    sweep(groups, one, two, 1, total - 1, coefs)
     for a, b in blocks(lo, hi):
         slab = slab_of(a, b)
 
         def chain(g, carry, a=a, b=b, slab=slab):
-            x = at_rows(work.at[last, g], a, b) - coarse(
-                gd, cx, at_rows(work.at[0, g], a, b), a, b
-            )
+            x = at_rows(one.at[g], a, b) - coarse(gd, cx, at_rows(guess.at[g], a, b), a, b)
             value = carry
             for _ in range(PER_GROUP - 1):
                 value = jnp.where(
                     slab == 0, carry, shift(coarse(gd, cx, value, a, b) + x, 1)
                 )
-            hist[0, g, (a - lo) * SUB : (b - lo) * SUB, :] = value
+            two[g, a * SUB : b * SUB, :] = value
             return shift(coarse(gd, cx, value, a, b) + x, SUB - PER_GROUP + 1)
 
         through_groups(groups, chain, jnp.zeros(((b - a) * SUB, LANES), jnp.float32))
 
-    def forward(t, carry):
-        each_group(
-            groups,
-            lambda g: step(
-                hist.at[t, g], hist.at[t + 1, g], lo + 1, hi - 1, lo, cv, ce, cd, cx, cq
-            ),
-        )
+    def forward(turn, carry):
+        def run(g):
+            for k, (src, dst) in enumerate(((two, one), (one, two))):
+                t = 2 * turn + k
+
+                def seen(a, b, before, here, east, new, t=t):
+                    hist[t, g, (a - lo) * SUB : (b - lo) * SUB, :] = here
+                    if HALO <= a < HALO + tile_rows:
+                        at = slice((a - HALO) * SUB, (b - HALO) * SUB)
+                        slope[t, g, at, :] = east - here
+
+                step(src.at[g], dst.at[g], lo, hi, coefs, seen)
+
+        each_group(groups, run)
         return carry
 
-    lax.fori_loop(0, STEPS, forward, 0)
+    lax.fori_loop(0, STEPS // 2, forward, 0)
     w_lo, w_hi = 2 * STEPS, total - 2 * STEPS
-    last_ref[...] = at_rows(hist.at[STEPS, groups - 1], w_lo - lo, w_hi - lo) - at_rows(
-        tg, w_lo, w_hi
-    )
-
-
-def adjoint_body(count, tile_rows, mid, top_ref, bot_ref, hist, last_ref, cv, ce, cd, cx, gd, *rest):
+    last_ref[...] = at_rows(two.at[groups - 1], w_lo, w_hi) - at_rows(tg, w_lo, w_hi)
+
+
+def lag_body(count, tile_rows, *refs):
+    cens, (cv, ce, cd, cx, gd, lag, guess, one, two) = refs[:count], refs[count:]
+    groups = count // PER_GROUP
+    total = tile_rows + 2 * HALO
+    tall = tile_rows + 2 * HALO_W
+    me = lax.axis_index("tm")
+    for d in range(count):
+        slab = me ^ d
+        g, j = slab // PER_GROUP, slab % PER_GROUP
+        for sp in range(2):
+            start = (HALO - HALO_W) * SUB + sp * PER_GROUP + j
+            value = cens[d][sp * tall : (sp + 1) * tall, :]
+            guess[g, pl.ds(start, tall, stride=SUB), :] = value
+            one[g, pl.ds(start, tall, stride=SUB), :] = value
+    sweep(groups, one, two, STEPS + 1, total - STEPS - 1, (cv, ce, cd, cx))
+    w_lo, w_hi = 2 * STEPS, total - 2 * STEPS
+
+    def run(g):
+        for a, b in blocks(w_lo, w_hi):
+            lag[g, (a - w_lo) * SUB : (b - w_lo) * SUB, :] = at_rows(
+                one.at[g], a, b
+            ) - coarse(gd, cx, at_rows(guess.at[g], a, b), a, b)
+
+    each_group(groups, run)
+
+
+def adjoint_body(count, tile_rows, lag, hist, slope, last_ref, cv, ce, cd, cx, gd, *rest):
     outs = rest[:count]
-    work, lag, fv, fh = rest[count:]
+    one, two, fv, fh = rest[count:]
     groups = count // PER_GROUP
     total = tile_rows + 2 * HALO
     end = HALO + tile_rows
+    coefs = (cv, ce, cd, cx)
     lo = STEPS
     me = lax.axis_index("tm")
-    load(groups, work, tile_rows, HALO_W, mid, top_ref, bot_ref)
-    last = sweep(groups, work, STEPS + 1, total - STEPS - 1, cv, ce, cd, cx)
     w_lo, w_hi = 2 * STEPS, total - 2 * STEPS
     for a, b in blocks(w_lo, w_hi):
         slab = slab_of(a, b)
-
-        def keep(g, a=a, b=b):
-            lag[g, (a - w_lo) * SUB : (b - w_lo) * SUB, :] = at_rows(
-                work.at[last, g], a, b
-            ) - coarse(gd, cx, at_rows(work.at[0, g], a, b), a, b)
-
-        each_group(groups, keep)
 
         def chain(turn, carry, a=a, b=b, slab=slab):
             g = groups - 1 - turn
@@ -307,10 +384,17 @@
                     top,
                     shift(coarse(gd, cx, value, a, b) + y, SUB - 1),
                 )
-            work[0, g, a * SUB : b * SUB, :] = value
+            two[g, a * SUB : b * SUB, :] = value
             return shift(coarse(gd, cx, value, a, b) + y, PER_GROUP - 1)
 
         through_groups(groups, chain, at_rows(last_ref, a - w_lo, b - w_lo))
+
+    def clear(g):
+        for r in (w_lo - 1, w_hi):
+            for ref in (one, two):
+                ref[g, r * SUB : (r + 1) * SUB, :] = jnp.zeros((SUB, LANES), jnp.float32)
+
+    each_group(groups, clear)
 
     lane = lax.broadcasted_iota(jnp.int32, (tile_rows, LANES), 1)
     left = lane < LANES // 2
@@ -330,7 +414,7 @@
             for sp in range(2)
         ]
         w_rows = [
-            work[0, g, pl.ds(HALO * SUB + sp * PER_GROUP + j, tile_rows, stride=SUB), :]
+            two[g, pl.ds(HALO * SUB + sp * PER_GROUP + j, tile_rows, stride=SUB), :]
             for sp in range(2)
         ]
         outs[d][0:tile_rows, :] = paired(*s_rows)
@@ -339,32 +423,28 @@
     fv[...] = jnp.zeros_like(fv)
     fh[...] = jnp.zeros_like(fh)
 
-    def products(u, w):
-        for a, b in blocks(HALO, end + 1):
-            at = slice((a - HALO) * SUB, (b - HALO) * SUB)
-            uc, wc = at_rows(u, a - lo, b - lo), at_rows(w, a, b)
-            fv[at, :] += (uc - at_rows(u, a - lo - 1, b - lo - 1)) * (
-                wc - at_rows(w, a - 1, b - 1)
-            )
-            if b <= end:
-                fh[at, :] += (pltpu.roll(uc, LANES - 1, 1) - uc) * (
-                    pltpu.roll(wc, LANES - 1, 1) - wc
-                )
-
-    def back(t, carry):
-        src = jnp.where(t == 0, 0, 1 + (t + 1) % 2)
-        dst = 1 + t % 2
-
-        def one(g):
-            products(hist.at[STEPS - 1 - t, g], work.at[src, g])
-            step(work.at[src, g], work.at[dst, g], w_lo + 1, w_hi - 1, 0, cv, ce, cd, cx)
-
-        each_group(groups, one)
+    def back(turn, carry):
+        def run(g):
+            for k, (src, dst) in enumerate(((two, one), (one, two))):
+                t = STEPS - 1 - 2 * turn - k
+
+                def seen(a, b, before, here, east, new, t=t):
+                    if a < HALO or a > end:
+                        return
+                    at = slice((a - HALO) * SUB, (b - HALO) * SUB)
+                    u = hist[t, g, (a - lo - 1) * SUB : (b - lo) * SUB, :]
+                    fv[at, :] += (u[SUB:] - u[:-SUB]) * (here - before)
+                    if b <= end:
+                        fh[at, :] += slope[t, g, at, :] * (
+                            east - here
+                        )
+
+                step(src.at[g], dst.at[g], w_lo, w_hi, coefs, seen)
+
+        each_group(groups, run)
         return carry
 
-    lax.fori_loop(0, STEPS - 1, back, 0)
-    last = 1 + (STEPS - 2) % 2
-    each_group(groups, lambda g: products(hist.at[0, g], work.at[last, g]))
+    lax.fori_loop(0, STEPS // 2, back, 0)
 
     size = tile_rows * SUB
     fh[...] = fv[0:size, :] + fv[SUB : size + SUB, :] + fh[...] + pltpu.roll(fh[...], 1, 1)
@@ -454,53 +534,61 @@
         inputs=[HBM_SPEC] * 7,
     )(*[pltpu.with_memory_space_constraint(f, pltpu.HBM) for f in fields])
     strip = lax.ppermute(strip, "sy", [(0, 1), (1, 0)])
-    edge = (sum(edges_of(rows)), LANES)
-    windows = call(
+    pieces = cols // LANES + 1
+    edge = (sum(edges_of(rows)) + 2 * pieces * HALO_W, LANES)
+    *windows, coef, down, up = call(
         functools.partial(window_body, count, rows),
-        [(2 * rows, LANES)] * (2 * count) + [(7 * rows, LANES), edge, edge],
+        [(2 * rows, LANES)] * count + [(7 * rows, LANES), edge, edge],
         [pltpu.VMEM((11 * rows, cols + 2 * LANES), jnp.float32)],
     )(tile, strip)
-    coef, down, up = windows[2 * count :]
-    states = exchanged(windows[:count])
-    adjoints = exchanged(windows[count : 2 * count])
-    coef_halo = turned(down, up)
-
-    def interleaved(parts, halo):
-        mid, down, up = call(
-            functools.partial(interleave_body, count, halo),
-            [(groups, rows * SUB, LANES)] + [(groups, halo * SUB, LANES)] * 2,
-        )(*parts)
-        return (mid, *turned(down, up))
-
+    states = exchanged(windows)
+    edges = turned(down, up)
+    mid, down, up = call(
+        functools.partial(interleave_body, count, HALO),
+        [(groups, rows * SUB, LANES)] + [(groups, HALO * SUB, LANES)] * 2,
+    )(*states)
+    state_edges = turned(down, up)
+    tall = rows + 2 * HALO_W
+    windows = call(
+        functools.partial(adjoint_window_body, count, rows),
+        [(2 * tall, LANES)] * count,
+        [pltpu.VMEM((2 * tall, cols + 2 * LANES), jnp.float32)],
+    )(tile, strip, *edges, mid)
+    adjoints = exchanged(windows)
     plain = (total * SUB, LANES)
-    work = pltpu.VMEM((3, groups, total * SUB, LANES), jnp.float32)
+    work = pltpu.VMEM((groups, total * SUB, LANES), jnp.float32)
     limit = 60 << 20 if groups > 1 else 32 << 20
-    kept = call(
-        functools.partial(state_body, count, rows, wide),
+    *coefs, gd, tg = call(
+        functools.partial(coef_body, count, rows, wide),
+        [plain] * 7,
+        [pltpu.VMEM((7, total, LANES), jnp.float32)],
+    )(coef, *edges)
+    (lag,) = call(
+        functools.partial(lag_body, count, rows),
+        [(groups, (total - 4 * STEPS) * SUB, LANES)],
+        [work] * 3,
+        limit,
+    )(*adjoints, *coefs[:4], gd)
+    hist, slope, last = call(
+        functools.partial(state_body, count, rows),
         [
-            (STEPS + 1, groups, (total - 2 * STEPS) * SUB, LANES),
+            (STEPS, groups, (total - 2 * STEPS) * SUB, LANES),
+            (STEPS, groups, rows * SUB, LANES),
             ((total - 4 * STEPS) * SUB, LANES),
-            *([plain] * 5),
         ],
-        [
-            work,
-            pltpu.VMEM(plain, jnp.float32),
-            pltpu.VMEM(plain, jnp.float32),
-            pltpu.VMEM((7, total, LANES), jnp.float32),
-        ],
+        [work] * 3,
         limit,
-    )(*interleaved(states, HALO), coef, *coef_halo)
+    )(mid, *state_edges, *coefs, gd, tg)
     outs = call(
         functools.partial(adjoint_body, count, rows),
         [(2 * rows + rows // 2, LANES)] * count,
         [
-            work,
-            pltpu.VMEM((groups, (total - 4 * STEPS) * SUB, LANES), jnp.float32),
-            pltpu.VMEM(((rows + 1) * SUB, LANES), jnp.float32),
+            *([work] * 2),
+            pltpu.VMEM(((rows + BLOCK) * SUB, LANES), jnp.float32),
             pltpu.VMEM((rows * SUB, LANES), jnp.float32),
         ],
         limit,
-    )(*interleaved(adjoints, HALO_W), *kept)
+    )(lag, hist, slope, last, *coefs[:4], gd)
     outs = exchanged(outs)
     states, adjoints, gradient = call(
         functools.partial(collect_body, count, wide),

time: 50.7 us -> 47.1 us (0.929)
  starting transfers between devices: 29.6 us -> 20.9 us
  waiting for transfers between devices: 4.73 us -> 11.4 us
  Pallas kernels: 15.5 us -> 13.9 us
    ppermute x9, waiting for transfers between devices: 3.42 us -> 10.1 us  [exchanged(): lax.ppermute(parts[d], 'tm', [(i, i ^ d) for i in range(count)])]
    ppermute x9, starting transfers between devices: 19.2 us -> 13.5 us  [exchanged(): lax.ppermute(parts[d], 'tm', [(i, i ^ d) for i in range(count)])]
    ppermute x3 -> x2, starting transfers between devices: 8.32 us -> 3.35 us  [turned(): lax.ppermute(up, 'sx', [((i + 1) % n, i) for i in range(n)])]
    ppermute x3 -> x2, starting transfers between devices: 1.55 us -> 3.56 us  [turned(): lax.ppermute(down, 'sx', [(i, (i + 1) % n) for i in range(n)])]
    pallas_call x7 -> x9, Pallas kernels: 15.5 us -> 13.9 us  [run(): pl.pallas_call(body, out_shape=[jax.ShapeDtypeStruct(s, jnp.float32) for...]
  transfers between devices with their start and end apart: 16 -> 14, of which waited for: 4 -> 6; matrix products, arithmetic and copies ran while one was open for 0% -> 0% of each run, Pallas kernels for 13% -> 13%
where the time goes in v3:
time: 47.1 us; the launch traced here: 47 us
  starting transfers between devices  20.9 us (44%)
  Pallas kernels  13.9 us (30%)
  waiting for transfers between devices  11.4 us (24%)
  between operations  0.74 us (2%)
    pallas_call x9, Pallas kernels, run(): pl.pallas_call(body, out_shape=[jax.ShapeDtypeStruct(s, jnp.float32) for...  13.9 us
    ppermute x9, starting transfers between devices, exchanged(): lax.ppermute(parts[d], 'tm', [(i, i ^ d) for i in range(count)])  13.5 us
    ppermute x9, waiting for transfers between devices, exchanged(): lax.ppermute(parts[d], 'tm', [(i, i ^ d) for i in range(count)])  10.1 us
    ppermute x2, starting transfers between devices, turned(): lax.ppermute(down, 'sx', [(i, (i + 1) % n) for i in range(n)])  3.56 us
    ppermute x2, starting transfers between devices, turned(): lax.ppermute(up, 'sx', [((i + 1) % n, i) for i in range(n)])  3.35 us
    ppermute x1, waiting for transfers between devices, local(): strip = lax.ppermute(strip, 'sy', [(0, 1), (1, 0)])  1.3 us
  transfers between devices with their start and end apart: 14, of which 6 were waited for; matrix products, arithmetic and copies ran while one was open for 0% of the time, Pallas kernels for 13%

profile of v3, /device:TPU:0, one launch (start us, length us, event | category | flops | bytes accessed | tf_op | source)
XLA Modules:
  0.0 47.0 jit_solution(2190784906125756908)
XLA Ops:
  0.6 1.3 %shard_map.94 = (f32[704,256]{1,0:T(8,128)S(1)}, f32[704,128]{1,0:T(8,128)S(1)}) custom-call(f32[128,256]{1,0:T(8,128)} %bitcast.6, f32[128,256]{1,0:T(8,128)} %bitcast.7, f32[64,256]{1,0:T(8,128)} %refs_2_.1, f32[64,256]{1,0:T(8,128)} %refs_3_.1, f32[64,256]{1,0:T(8,128)} %refs_4_.1, f32[128,256]{1,0:T(8,128)} %bitcast.8, f32[128,256]{1,0:T(8,128)} %bitcast.9), custom_call_target="tpu_custom_call" | custom-call | tf_op jit(solution)/shard_map/pallas_call | solution.py:29
  1.9 0.5 %collective-permute-start = (f32[704,128]{1,0:T(8,128)S(1)}, f32[704,128]{1,0:T(8,128)S(1)}, u32[]{:S(2)}, u32[]{:S(2)}) collective-permute-start(f32[704,128]{1,0:T(8,128)S(1)} %get-tuple-element.37), channel_id=1, source_target_pairs={{0,1},{1,0},{2,3},{3,2},{4,5},{5,4},{6,7},{7,6},{8,9},{9,8},{10,11... | collective-permute-start | bytes 1081352 | tf_op jit(solution)/shard_map/ppermute | solution.py:536
  2.5 1.3 %collective-permute-done.strip_ref = f32[704,128]{1,0:T(8,128)S(1)} collective-permute-done((f32[704,128]{1,0:T(8,128)S(1)}, f32[704,128]{1,0:T(8,128)S(1)}, u32[]{:S(2)}, u32[]{:S(2)}) %collective-permute-start) | collective-permute-done | bytes 360480 | tf_op jit(solution)/shard_map/ppermute | solution.py:536
  3.8 0.5 %shard_map.95 = (f32[128,128]{1,0:T(8,128)S(1)}, f32[128,128]{1,0:T(8,128)S(1)}, f32[128,128]{1,0:T(8,128)S(1)}, f32[128,128]{1,0:T(8,128)S(1)}, f32[448,128]{1,...) custom-call(f32[704,256]{1,0:T(8,128)S(1)} %get-tuple-element.36.tile_ref, ...), custom_call_target="tpu_custom_call" | custom-call | tf_op jit(solution)/shard_map/pallas_call | solution.py:29
  4.2 2.9 %collective-permute-start.1 = (f32[232,128]{1,0:T(8,128)S(1)}, f32[232,128]{1,0:T(8,128)S(1)}, u32[]{:S(2)}, u32[]{:S(2)}) collective-permute-start(f32[232,128]{1,0:T(8,128)S(1)} %get-tuple-element.38), channel_id=1, source_target_pairs={{0,2},{2,4},{4,6},{6,0},{1,3},{3,5},{5,7},{7,1},{8,10},{10,12},{12... | collective-permute-start | bytes 356360 | tf_op jit(solution)/shard_map/ppermute | solution.py:526
  7.2 1.0 %collective-permute-start.2 = (f32[232,128]{1,0:T(8,128)S(1)}, f32[232,128]{1,0:T(8,128)S(1)}, u32[]{:S(2)}, u32[]{:S(2)}) collective-permute-start(f32[232,128]{1,0:T(8,128)S(1)} %get-tuple-element.39), channel_id=1, source_target_pairs={{2,0},{4,2},{6,4},{0,6},{3,1},{5,3},{7,5},{1,7},{10,8},{12,10},{14... | collective-permute-start | bytes 356360 | tf_op jit(solution)/shard_map/ppermute | solution.py:527
  8.2 2.0 %collective-permute-start.3 = (f32[128,128]{1,0:T(8,128)S(1)}, f32[128,128]{1,0:T(8,128)S(1)}, u32[]{:S(2)}, u32[]{:S(2)}) collective-permute-start(f32[128,128]{1,0:T(8,128)S(1)} %get-tuple-element.41), channel_id=1, source_target_pairs={{0,8},{8,0},{16,24},{24,16},{1,9},{9,1},{17,25},{25,17},{2,10},{10... | collective-permute-start | bytes 196616 | tf_op jit(solution)/shard_map/ppermute | solution.py:519
  10.2 2.6 %collective-permute-start.4 = (f32[128,128]{1,0:T(8,128)S(1)}, f32[128,128]{1,0:T(8,128)S(1)}, u32[]{:S(2)}, u32[]{:S(2)}) collective-permute-start(f32[128,128]{1,0:T(8,128)S(1)} %get-tuple-element.42), channel_id=1, source_target_pairs={{0,16},{8,24},{16,0},{24,8},{1,17},{9,25},{17,1},{25,9},{2,18},{10... | collective-permute-start | bytes 196616 | tf_op jit(solution)/shard_map/ppermute | solution.py:519
  12.8 0.0 collective-permute-start.5
  12.8 0.0 collective-permute-done.3.refs_1_
  12.8 4.4 %collective-permute-done.4.refs_2_ = f32[128,128]{1,0:T(8,128)S(1)} collective-permute-done((f32[128,128]{1,0:T(8,128)S(1)}, f32[128,128]{1,0:T(8,128)S(1)}, u32[]{:S(2)}, u32[]{:S(2)}) %collective-permute-start.4) | collective-permute-done | bytes 65568 | tf_op jit(solution)/shard_map/ppermute | solution.py:519
  17.2 1.6 %collective-permute-done.5.refs_3_ = f32[128,128]{1,0:T(8,128)S(1)} collective-permute-done((f32[128,128]{1,0:T(8,128)S(1)}, f32[128,128]{1,0:T(8,128)S(1)}, u32[]{:S(2)}, u32[]{:S(2)}) %collective-permute-start.5) | collective-permute-done | bytes 65568 | tf_op jit(solution)/shard_map/ppermute | solution.py:519
  18.8 0.1 shard_map.96
  18.9 0.6 %collective-permute-start.9 = (f32[1,192,128]{2,1,0:T(8,128)S(1)}, f32[1,192,128]{2,1,0:T(8,128)S(1)}, u32[]{:S(2)}, u32[]{:S(2)}) collective-permute-start(f32[1,192,128]{2,1,0:T(8,128)S(1)} %get-tuple-element.55), channel_id=1, source_target_pairs={{0,2},{2,4},{4,6},{6,0},{1,3},{3,5},{5,7},{7,1},{8,10},{10,12},{12... | collective-permute-start | bytes 294920 | tf_op jit(solution)/shard_map/ppermute | solution.py:526
  19.5 2.3 %collective-permute-start.10 = (f32[1,192,128]{2,1,0:T(8,128)S(1)}, f32[1,192,128]{2,1,0:T(8,128)S(1)}, u32[]{:S(2)}, u32[]{:S(2)}) collective-permute-start(f32[1,192,128]{2,1,0:T(8,128)S(1)} %get-tuple-element.56), channel_id=1, source_target_pairs={{2,0},{4,2},{6,4},{0,6},{3,1},{5,3},{7,5},{1,7},{10,8},{12,10},{14... | collective-permute-start | bytes 294920 | tf_op jit(solution)/shard_map/ppermute | solution.py:527
  21.9 0.0 collective-permute-done.1.top_ref.ctop_ref
  21.9 0.0 collective-permute-done.2.bot_ref.cbot_ref
  21.9 0.3 shard_map.97
  22.2 0.1 collective-permute-start.6
  22.3 2.1 %collective-permute-start.7 = (f32[192,128]{1,0:T(8,128)S(1)}, f32[192,128]{1,0:T(8,128)S(1)}, u32[]{:S(2)}, u32[]{:S(2)}) collective-permute-start(f32[192,128]{1,0:T(8,128)S(1)} %get-tuple-element.47), channel_id=1, source_target_pairs={{0,16},{8,24},{16,0},{24,8},{1,17},{9,25},{17,1},{25,9},{2,18},{10... | collective-permute-start | bytes 294920 | tf_op jit(solution)/shard_map/ppermute | solution.py:519
  24.4 2.3 %collective-permute-start.8 = (f32[192,128]{1,0:T(8,128)S(1)}, f32[192,128]{1,0:T(8,128)S(1)}, u32[]{:S(2)}, u32[]{:S(2)}) collective-permute-start(f32[192,128]{1,0:T(8,128)S(1)} %get-tuple-element.48), channel_id=1, source_target_pairs={{0,24},{8,16},{16,8},{24,0},{1,25},{9,17},{17,9},{25,1},{2,26},{10... | collective-permute-start | bytes 294920 | tf_op jit(solution)/shard_map/ppermute | solution.py:519
  26.6 0.5 %shard_map.98 = (f32[896,128]{1,0:T(8,128)S(1)}, f32[896,128]{1,0:T(8,128)S(1)}, f32[896,128]{1,0:T(8,128)S(1)}, f32[896,128]{1,0:T(8,128)S(1)}, f32[896,128]{1,...) custom-call(f32[448,128]{1,0:T(8,128)S(1)} %get-tuple-element.49.coef_ref, ...), custom_call_target="tpu_custom_call" | custom-call | tf_op jit(solution)/shard_map/pallas_call | solution.py:29
  27.1 0.0 collective-permute-done.9.top_ref
  27.1 0.0 collective-permute-done.10.bot_ref
  27.2 5.2 %shard_map.100 = (f32[8,1,768,128]{3,2,1,0:T(8,128)S(1)}, f32[8,1,512,128]{3,2,1,0:T(8,128)S(1)}, f32[640,128]{1,0:T(8,128)S(1)}) custom-call(f32[1,512,128]{2,1,0:T(8,128)S(1)} %get-tuple-element.44.after.mid, f32[1,192,128]{2,1,0:T(8,128)S(1)} %collective-permute-done.9.top_ref, f32[1,192,128]{2,1,0:T(8,128)S(1)} %collective-permute-done.10.bot_ref, ...), custom_call_target="tpu_custom_call" | custom-call | tf_op jit(solution)/shard_map/pallas_call | solution.py:29
  32.4 0.0 collective-permute-done.6.refs_1_
  32.4 0.0 collective-permute-done.7.refs_2_
  32.4 0.0 collective-permute-done.8.refs_3_
  32.4 2.3 %shard_map.99.lag = f32[1,640,128]{2,1,0:T(8,128)S(1)} custom-call(f32[192,128]{1,0:T(8,128)S(1)} %get-tuple-element.45.refs_0_, f32[192,128]{1,0:T(8,128)S(1)} %collective-permute-done.6.refs_1_, f32[192,128]{1,0:T(8,128)S(1)} %collective-permute-done.7.refs_2_, f32[192,128]{1,0:T(8,128)S(1)} %collective-permute-done.8.refs_3_, ...), custom_call_target="tpu_custom_call" | custom-call | tf_op jit(solution)/shard_map/pallas_call | solution.py:29
  34.7 2.9 %shard_map.101 = (f32[160,128]{1,0:T(8,128)S(1)}, f32[160,128]{1,0:T(8,128)S(1)}, f32[160,128]{1,0:T(8,128)S(1)}, f32[160,128]{1,0:T(8,128)S(1)}) custom-call(f32[1,640,128]{2,1,0:T(8,128)S(1)} %shard_map.99.lag, f32[8,1,768,128]{3,2,1,0:T(8,128)S(1)} %get-tuple-element.59.hist, f32[8,1,512,128]{3,2,1,0:T(8,128)S(1)} %get-tuple-element.60.slope, ...), custom_call_target="tpu_custom_call" | custom-call | tf_op jit(solution)/shard_map/pallas_call | solution.py:29
  37.6 0.3 collective-permute-start.11
  37.9 1.8 %collective-permute-start.12 = (f32[160,128]{1,0:T(8,128)S(1)}, f32[160,128]{1,0:T(8,128)S(1)}, u32[]{:S(2)}, u32[]{:S(2)}) collective-permute-start(f32[160,128]{1,0:T(8,128)S(1)} %get-tuple-element.64), channel_id=1, source_target_pairs={{0,16},{8,24},{16,0},{24,8},{1,17},{9,25},{17,1},{25,9},{2,18},{10... | collective-permute-start | bytes 245768 | tf_op jit(solution)/shard_map/ppermute | solution.py:519
  39.8 2.3 %collective-permute-start.13 = (f32[160,128]{1,0:T(8,128)S(1)}, f32[160,128]{1,0:T(8,128)S(1)}, u32[]{:S(2)}, u32[]{:S(2)}) collective-permute-start(f32[160,128]{1,0:T(8,128)S(1)} %get-tuple-element.65), channel_id=1, source_target_pairs={{0,24},{8,16},{16,8},{24,0},{1,25},{9,17},{17,9},{25,1},{2,26},{10... | collective-permute-start | bytes 245768 | tf_op jit(solution)/shard_map/ppermute | solution.py:519
  42.1 1.6 %collective-permute-done.11.refs_1_ = f32[160,128]{1,0:T(8,128)S(1)} collective-permute-done((f32[160,128]{1,0:T(8,128)S(1)}, f32[160,128]{1,0:T(8,128)S(1)}, u32[]{:S(2)}, u32[]{:S(2)}) %collective-permute-start.11) | collective-permute-done | bytes 81952 | tf_op jit(solution)/shard_map/ppermute | solution.py:519
  43.6 1.2 %collective-permute-done.12.refs_2_ = f32[160,128]{1,0:T(8,128)S(1)} collective-permute-done((f32[160,128]{1,0:T(8,128)S(1)}, f32[160,128]{1,0:T(8,128)S(1)}, u32[]{:S(2)}, u32[]{:S(2)}) %collective-permute-start.12) | collective-permute-done | bytes 81952 | tf_op jit(solution)/shard_map/ppermute | solution.py:519
  44.8 1.3 %collective-permute-done.13.refs_3_ = f32[160,128]{1,0:T(8,128)S(1)} collective-permute-done((f32[160,128]{1,0:T(8,128)S(1)}, f32[160,128]{1,0:T(8,128)S(1)}, u32[]{:S(2)}, u32[]{:S(2)}) %collective-permute-start.13) | collective-permute-done | bytes 81952 | tf_op jit(solution)/shard_map/ppermute | solution.py:519
  46.1 0.9 %shard_map.102 = (f32[128,256]{1,0:T(8,128)}, f32[128,256]{1,0:T(8,128)}, f32[64,256]{1,0:T(8,128)}) custom-call(f32[160,128]{1,0:T(8,128)S(1)} %get-tuple-element.62.refs_0_, f32[160,128]{1,0:T(8,128)S(1)} %collective-permute-done.11.refs_1_, f32[160,128]{1,0:T(8,128)S(1)} %collective-permute-done.12.refs_2_, f32[160,128]{1,0:T(8,128)S(1)} %collective-permute-done.13.refs_3_), custom_call_target="tpu_custom_call" | custom-call | tf_op jit(solution)/shard_map/pallas_call | solution.py:29
Async XLA Ops:
  1.9 1.8 %collective-permute-start = (f32[704,128]{1,0:T(8,128)S(1)}, f32[704,128]{1,0:T(8,128)S(1)}, u32[]{:S(2)}, u32[]{:S(2)}) collective-permute-start(f32[704,128]{1,0:T(8,128)S(1)} %get-tuple-element.37), channel_id=1, source_target_pairs={{0,1},{1,0},{2,3},{3,2},{4,5},{5,4},{6,7},{7,6},{8,9},{9,8},{10,11... | collective-permute-start | bytes 1081352 | tf_op jit(solution)/shard_map/ppermute | solution.py:536
  4.2 17.6 %collective-permute-start.1 = (f32[232,128]{1,0:T(8,128)S(1)}, f32[232,128]{1,0:T(8,128)S(1)}, u32[]{:S(2)}, u32[]{:S(2)}) collective-permute-start(f32[232,128]{1,0:T(8,128)S(1)} %get-tuple-element.38), channel_id=1, source_target_pairs={{0,2},{2,4},{4,6},{6,0},{1,3},{3,5},{5,7},{7,1},{8,10},{10,12},{12... | collective-permute-start | bytes 356360 | tf_op jit(solution)/shard_map/ppermute | solution.py:526
  7.2 14.7 %collective-permute-start.2 = (f32[232,128]{1,0:T(8,128)S(1)}, f32[232,128]{1,0:T(8,128)S(1)}, u32[]{:S(2)}, u32[]{:S(2)}) collective-permute-start(f32[232,128]{1,0:T(8,128)S(1)} %get-tuple-element.39), channel_id=1, source_target_pairs={{2,0},{4,2},{6,4},{0,6},{3,1},{5,3},{7,5},{1,7},{10,8},{12,10},{14... | collective-permute-start | bytes 356360 | tf_op jit(solution)/shard_map/ppermute | solution.py:527
  8.2 4.6 %collective-permute-start.3 = (f32[128,128]{1,0:T(8,128)S(1)}, f32[128,128]{1,0:T(8,128)S(1)}, u32[]{:S(2)}, u32[]{:S(2)}) collective-permute-start(f32[128,128]{1,0:T(8,128)S(1)} %get-tuple-element.41), channel_id=1, source_target_pairs={{0,8},{8,0},{16,24},{24,16},{1,9},{9,1},{17,25},{25,17},{2,10},{10... | collective-permute-start | bytes 196616 | tf_op jit(solution)/shard_map/ppermute | solution.py:519
  10.2 7.0 %collective-permute-start.4 = (f32[128,128]{1,0:T(8,128)S(1)}, f32[128,128]{1,0:T(8,128)S(1)}, u32[]{:S(2)}, u32[]{:S(2)}) collective-permute-start(f32[128,128]{1,0:T(8,128)S(1)} %get-tuple-element.42), channel_id=1, source_target_pairs={{0,16},{8,24},{16,0},{24,8},{1,17},{9,25},{17,1},{25,9},{2,18},{10... | collective-permute-start | bytes 196616 | tf_op jit(solution)/shard_map/ppermute | solution.py:519
  12.8 6.1 %collective-permute-start.5 = (f32[128,128]{1,0:T(8,128)S(1)}, f32[128,128]{1,0:T(8,128)S(1)}, u32[]{:S(2)}, u32[]{:S(2)}) collective-permute-start(f32[128,128]{1,0:T(8,128)S(1)} %get-tuple-element.43), channel_id=1, source_target_pairs={{0,24},{8,16},{16,8},{24,0},{1,25},{9,17},{17,9},{25,1},{2,26},{10... | collective-permute-start | bytes 196616 | tf_op jit(solution)/shard_map/ppermute | solution.py:519
  18.9 8.2 %collective-permute-start.9 = (f32[1,192,128]{2,1,0:T(8,128)S(1)}, f32[1,192,128]{2,1,0:T(8,128)S(1)}, u32[]{:S(2)}, u32[]{:S(2)}) collective-permute-start(f32[1,192,128]{2,1,0:T(8,128)S(1)} %get-tuple-element.55), channel_id=1, source_target_pairs={{0,2},{2,4},{4,6},{6,0},{1,3},{3,5},{5,7},{7,1},{8,10},{10,12},{12... | collective-permute-start | bytes 294920 | tf_op jit(solution)/shard_map/ppermute | solution.py:526
  19.5 7.6 %collective-permute-start.10 = (f32[1,192,128]{2,1,0:T(8,128)S(1)}, f32[1,192,128]{2,1,0:T(8,128)S(1)}, u32[]{:S(2)}, u32[]{:S(2)}) collective-permute-start(f32[1,192,128]{2,1,0:T(8,128)S(1)} %get-tuple-element.56), channel_id=1, source_target_pairs={{2,0},{4,2},{6,4},{0,6},{3,1},{5,3},{7,5},{1,7},{10,8},{12,10},{14... | collective-permute-start | bytes 294920 | tf_op jit(solution)/shard_map/ppermute | solution.py:527
  22.2 10.2 %collective-permute-start.6 = (f32[192,128]{1,0:T(8,128)S(1)}, f32[192,128]{1,0:T(8,128)S(1)}, u32[]{:S(2)}, u32[]{:S(2)}) collective-permute-start(f32[192,128]{1,0:T(8,128)S(1)} %get-tuple-element.46), channel_id=1, source_target_pairs={{0,8},{8,0},{16,24},{24,16},{1,9},{9,1},{17,25},{25,17},{2,10},{10... | collective-permute-start | bytes 294920 | tf_op jit(solution)/shard_map/ppermute | solution.py:519
  22.3 10.1 %collective-permute-start.7 = (f32[192,128]{1,0:T(8,128)S(1)}, f32[192,128]{1,0:T(8,128)S(1)}, u32[]{:S(2)}, u32[]{:S(2)}) collective-permute-start(f32[192,128]{1,0:T(8,128)S(1)} %get-tuple-element.47), channel_id=1, source_target_pairs={{0,16},{8,24},{16,0},{24,8},{1,17},{9,25},{17,1},{25,9},{2,18},{10... | collective-permute-start | bytes 294920 | tf_op jit(solution)/shard_map/ppermute | solution.py:519
  24.4 8.0 %collective-permute-start.8 = (f32[192,128]{1,0:T(8,128)S(1)}, f32[192,128]{1,0:T(8,128)S(1)}, u32[]{:S(2)}, u32[]{:S(2)}) collective-permute-start(f32[192,128]{1,0:T(8,128)S(1)} %get-tuple-element.48), channel_id=1, source_target_pairs={{0,24},{8,16},{16,8},{24,0},{1,25},{9,17},{17,9},{25,1},{2,26},{10... | collective-permute-start | bytes 294920 | tf_op jit(solution)/shard_map/ppermute | solution.py:519
  37.6 6.0 %collective-permute-start.11 = (f32[160,128]{1,0:T(8,128)S(1)}, f32[160,128]{1,0:T(8,128)S(1)}, u32[]{:S(2)}, u32[]{:S(2)}) collective-permute-start(f32[160,128]{1,0:T(8,128)S(1)} %get-tuple-element.63), channel_id=1, source_target_pairs={{0,8},{8,0},{16,24},{24,16},{1,9},{9,1},{17,25},{25,17},{2,10},{10... | collective-permute-start | bytes 245768 | tf_op jit(solution)/shard_map/ppermute | solution.py:519
  37.9 6.9 %collective-permute-start.12 = (f32[160,128]{1,0:T(8,128)S(1)}, f32[160,128]{1,0:T(8,128)S(1)}, u32[]{:S(2)}, u32[]{:S(2)}) collective-permute-start(f32[160,128]{1,0:T(8,128)S(1)} %get-tuple-element.64), channel_id=1, source_target_pairs={{0,16},{8,24},{16,0},{24,8},{1,17},{9,25},{17,1},{25,9},{2,18},{10... | collective-permute-start | bytes 245768 | tf_op jit(solution)/shard_map/ppermute | solution.py:519
  39.8 6.3 %collective-permute-start.13 = (f32[160,128]{1,0:T(8,128)S(1)}, f32[160,128]{1,0:T(8,128)S(1)}, u32[]{:S(2)}, u32[]{:S(2)}) collective-permute-start(f32[160,128]{1,0:T(8,128)S(1)} %get-tuple-element.65), channel_id=1, source_target_pairs={{0,24},{8,16},{16,8},{24,0},{1,25},{9,17},{17,9},{25,1},{2,26},{10... | collective-permute-start | bytes 245768 | tf_op jit(solution)/shard_map/ppermute | solution.py:519

commit v4 on v3

--- a/solution.py
+++ b/solution.py
@@ -58,8 +58,36 @@
     )
 
 
-def edges_of(tile_rows):
-    return (HALO,) * 5 + (SUB,) * 2
+EARLY = (HALO,) * 2
+LATE = (HALO,) * 3 + (SUB,) * 2
+
+
+def edge_rows(refs, coef_ref, first, sizes, at):
+    down_ref, up_ref = refs
+    rows = coef_ref.shape[0] // 7
+    for f, size in enumerate(sizes, first):
+        down_ref[at : at + size, :] = coef_ref[(f + 1) * rows - size : (f + 1) * rows, :]
+        up_ref[at : at + size, :] = coef_ref[f * rows : f * rows + size, :]
+        at += size
+    return at
+
+
+def joined_rows(flat, coef_ref, refs, first, sizes, at):
+    s_at = lax.axis_index("sx")
+    has_top = s_at > 0
+    has_bot = s_at < lax.axis_size("sx") - 1
+    top_ref, bot_ref = refs
+    rows = coef_ref.shape[0] // 7
+    end = HALO + rows
+    fields = []
+    for i, size in enumerate(sizes):
+        f = first + i
+        flat[i, HALO - size : HALO, :] = masked(has_top, top_ref[at : at + size, :])
+        flat[i, HALO:end, :] = coef_ref[f * rows : (f + 1) * rows, :]
+        flat[i, end : end + size, :] = masked(has_bot, bot_ref[at : at + size, :])
+        fields.append(flat[i])
+        at += size
+    return fields
 
 
 def extend(ext, lo, hi, tile, strip):
@@ -79,30 +107,71 @@
 
 
 def window_body(count, rows, tile_ref, strip_ref, *refs):
-    states, (coef_ref, down_ref, up_ref, ext) = refs[:count], refs[count:]
+    outs, ext = refs[:count], refs[count]
+    me = lax.axis_index("tm")
+    wide = tile_ref.shape[1] // count
+    extend(ext, 0, 2 * rows, tile_ref[: 2 * rows, :], strip_ref[: 2 * rows, :])
+    for d in range(count):
+        outs[d][...] = window(ext, 0, 2 * rows, wide * (me ^ d))
+
+
+def edge_body(count, rows, tile_ref, strip_ref, after, coef_ref, down_ref, up_ref, ext):
+    del after
     me = lax.axis_index("tm")
     cols = tile_ref.shape[1]
-    wide = cols // count
-    extend(ext, 0, 11 * rows, tile_ref[...], strip_ref[...])
-    for d in range(count):
-        states[d][...] = window(ext, 0, 2 * rows, wide * (me ^ d))
-    coef_ref[...] = window(ext, 4 * rows, 11 * rows, wide * me)
-    at = 0
-    for f, size in enumerate(edges_of(rows)):
-        down_ref[at : at + size, :] = coef_ref[(f + 1) * rows - size : (f + 1) * rows, :]
-        up_ref[at : at + size, :] = coef_ref[f * rows : f * rows + size, :]
-        at += size
-    for sp in range(2):
-        lo = (2 + sp) * rows
-        for ref, low in ((down_ref, lo + rows - HALO_W), (up_ref, lo)):
-            here = slice(low, low + HALO_W)
+    extend(ext, 0, 7 * rows, tile_ref[4 * rows :, :], strip_ref[4 * rows :, :])
+    coef_ref[...] = window(ext, 0, 7 * rows, cols // count * me)
+    at = edge_rows((down_ref, up_ref), coef_ref, 0, EARLY, 0)
+    lane = lax.broadcasted_iota(jnp.int32, (SUB, LANES), 1)
+    for ref, low in ((down_ref, rows - HALO_W), (up_ref, 0)):
+        put, sides = at, None
+        for sp in range(2):
+            here = (2 + sp) * rows + low
             for i in range(cols // LANES):
-                ref[at + i * HALO_W : at + (i + 1) * HALO_W, :] = tile_ref[
-                    here, i * LANES : (i + 1) * LANES
+                ref[put : put + HALO_W, :] = tile_ref[
+                    here : here + HALO_W, i * LANES : (i + 1) * LANES
                 ]
-            i = cols // LANES
-            ref[at + i * HALO_W : at + (i + 1) * HALO_W, :] = strip_ref[here, :]
-        at += (cols // LANES + 1) * HALO_W
+                put += HALO_W
+            for i in range(HALO_W // SUB):
+                strip = strip_ref[here + i * SUB : here + (i + 1) * SUB, :]
+                n = sp * (HALO_W // SUB) + i
+                strip = jnp.where(
+                    lax.axis_index("sy") == 0,
+                    pltpu.roll(strip, n * SIDE, 1),
+                    pltpu.roll(strip, (n + 1) * SIDE % LANES, 1),
+                )
+                sides = strip if n == 0 else jnp.where(lane >= n * SIDE, strip, sides)
+        ref[put : put + SUB, :] = sides
+
+
+PACKED = 3 * LANES // 4
+
+
+def packed(value):
+    n = value.shape[0] // 4
+    cut = (LANES - PACKED) // 2
+    lane = lax.broadcasted_iota(jnp.int32, (n, LANES), 1)
+    last = value[3 * n :]
+    parts = []
+    for i in range(3):
+        main = pltpu.roll(value[i * n : (i + 1) * n], LANES - cut, 1)
+        rest = pltpu.roll(last, (PACKED - cut - i * (LANES - PACKED)) % LANES, 1)
+        parts.append(jnp.where(lane < PACKED, main, rest))
+    return jnp.concatenate(parts, axis=0)
+
+
+def unpacked(value):
+    n = value.shape[0] // 3
+    cut = (LANES - PACKED) // 2
+    side = LANES - PACKED
+    lane = lax.broadcasted_iota(jnp.int32, (n, LANES), 1)
+    parts, last = [], None
+    for i in range(3):
+        part = value[i * n : (i + 1) * n]
+        parts.append(pltpu.roll(part, cut, 1))
+        rest = pltpu.roll(part, (cut + i * side - PACKED) % LANES, 1)
+        last = rest if i == 0 else jnp.where(lane >= cut + i * side, rest, last)
+    return jnp.concatenate([*parts, last], axis=0)
 
 
 def adjoint_window_body(count, rows, tile_ref, strip_ref, top_ref, bot_ref, after, *refs):
@@ -116,7 +185,8 @@
     for sp in range(2):
         lo = (2 + sp) * rows
         base = sp * tall
-        at = sum(edges_of(rows)) + sp * (cols // LANES + 1) * HALO_W
+        at = sum(EARLY) + sp * (cols // LANES) * HALO_W
+        side_at = sum(EARLY) + 2 * (cols // LANES) * HALO_W
         extend(
             ext,
             base + HALO_W,
@@ -130,17 +200,33 @@
         ):
             parts = [
                 masked(flag, ref[at + i * HALO_W : at + (i + 1) * HALO_W, :])
-                for i in range(cols // LANES + 1)
+                for i in range(cols // LANES)
             ]
+            sides = masked(flag, ref[side_at : side_at + SUB, :])
+            strips = []
+            for i in range(HALO_W // SUB):
+                n = sp * (HALO_W // SUB) + i
+                strips.append(
+                    jnp.where(
+                        lax.axis_index("sy") == 0,
+                        pltpu.roll(sides, (LANES - n * SIDE) % LANES, 1),
+                        pltpu.roll(sides, (2 * LANES - (n + 1) * SIDE) % LANES, 1),
+                    )
+                )
             extend(
-                ext, start, start + HALO_W, jnp.concatenate(parts[:-1], axis=1), parts[-1]
+                ext,
+                start,
+                start + HALO_W,
+                jnp.concatenate(parts, axis=1),
+                jnp.concatenate(strips, axis=0),
             )
     for d in range(count):
-        outs[d][...] = window(ext, 0, 2 * tall, wide * (me ^ d))
-
-
-def interleave_body(count, halo, *refs):
-    cens, (mid, down_ref, up_ref) = refs[:count], refs[count:]
+        outs[d][...] = packed(window(ext, 0, 2 * tall, wide * (me ^ d)))
+
+
+def interleave_body(count, *refs):
+    cens, (coef_ref, mid, down_ref, up_ref) = refs[:count], refs[count:]
+    edge_rows((down_ref, up_ref), coef_ref, len(EARLY), LATE, (count - 1) * 2 * HALO)
     rows = cens[0].shape[0] // 2
     me = lax.axis_index("tm")
     for d in range(count):
@@ -150,9 +236,13 @@
             mid[g, pl.ds(sp * PER_GROUP + j, rows, stride=SUB), :] = cens[d][
                 sp * rows : (sp + 1) * rows, :
             ]
-    size = halo * SUB
-    down_ref[...] = mid[:, (rows - halo) * SUB :, :]
-    up_ref[...] = mid[:, 0:size, :]
+
+        @pl.when(slab < count - 1)
+        def _(d=d, slab=slab):
+            for sp in range(2):
+                at = pl.multiple_of((slab * 2 + sp) * HALO, SUB)
+                down_ref[pl.ds(at, HALO), :] = cens[d][(sp + 1) * rows - HALO : (sp + 1) * rows, :]
+                up_ref[pl.ds(at, HALO), :] = cens[d][sp * rows : sp * rows + HALO, :]
 
 
 def blocks(lo, hi):
@@ -225,41 +315,39 @@
     return at_rows(gd, a, b) * value + (STEPS * at_rows(cx, a, b)) * shift(value, PER_GROUP)
 
 
-def load(groups, refs, tile_rows, halo, mid, top_ref, bot_ref):
+def load(groups, refs, tile_rows, mid, top_ref, bot_ref):
     s_at = lax.axis_index("sx")
     has_top = s_at > 0
     has_bot = s_at < lax.axis_size("sx") - 1
     end = HALO + tile_rows
-
-    def one(g):
+    for g in range(groups):
         for ref in refs:
-            ref[g, (HALO - halo) * SUB : HALO * SUB, :] = masked(has_top, top_ref[g])
             ref[g, HALO * SUB : end * SUB, :] = mid[g]
-            ref[g, end * SUB : (end + halo) * SUB, :] = masked(has_bot, bot_ref[g])
-
-    each_group(groups, one)
-
-
-def coef_body(count, tile_rows, wide, coef_ref, ctop_ref, cbot_ref, *rest):
-    cv, ce, cd, cx, cq, gd, tg, flat = rest
+        for j in range(PER_GROUP):
+            for sp in range(2):
+                slab = min(g * PER_GROUP + j, groups * PER_GROUP - 2)
+                at = (slab * 2 + sp) * HALO
+                for halo, start, flag in ((top_ref, 0, has_top), (bot_ref, end, has_bot)):
+                    value = masked(flag, halo[at : at + HALO, :])
+                    for ref in refs:
+                        first = start * SUB + sp * PER_GROUP + j
+                        ref[g, pl.ds(first, HALO, stride=SUB), :] = value
+
+
+def spread(ref, sp, value):
+    for j in range(PER_GROUP):
+        ref[pl.ds(sp * PER_GROUP + j, value.shape[0], stride=SUB), :] = value
+
+
+def coef_body(count, tile_rows, wide, coef_ref, top_ref, bot_ref, *rest):
+    cv, ce, cd, gd, react_ref, flat = rest
     total = tile_rows + 2 * HALO
-    end = HALO + tile_rows
-    me = lax.axis_index("tm")
-    s_at = lax.axis_index("sx")
-    has_top = s_at > 0
-    has_bot = s_at < lax.axis_size("sx") - 1
-    at = 0
-    fields = []
-    for f, size in enumerate(edges_of(tile_rows)):
-        flat[f, HALO - size : HALO, :] = masked(has_top, ctop_ref[at : at + size, :])
-        flat[f, HALO:end, :] = coef_ref[f * tile_rows : (f + 1) * tile_rows, :]
-        flat[f, end : end + size, :] = masked(has_bot, cbot_ref[at : at + size, :])
-        fields.append(flat[f])
-        at += size
-    k, rate, coupling, q0, q1, t0, t1 = fields
-    row = lax.broadcasted_iota(jnp.int32, (total, LANES), 0) + (s_at * tile_rows - HALO)
+    k, rate = joined_rows(flat, coef_ref, (top_ref, bot_ref), 0, EARLY, 0)
+    row = lax.broadcasted_iota(jnp.int32, (total, LANES), 0) + (
+        lax.axis_index("sx") * tile_rows - HALO
+    )
     col = lax.broadcasted_iota(jnp.int32, (total, LANES), 1) + (
-        lax.axis_index("sy") * (wide * count) + me * wide - SIDE
+        lax.axis_index("sy") * (wide * count) + lax.axis_index("tm") * wide - SIDE
     )
     all_rows = tile_rows * lax.axis_size("sx")
     all_cols = wide * count * lax.axis_size("sy")
@@ -272,31 +360,46 @@
     above = jnp.where((row >= 1) & (row < all_rows), above, 0.0)
     east = jnp.where((col >= 0) & (col < all_cols - 1), east, 0.0)
     react = TIME_STEP * rate
-    cross = react * coupling
-    for sp, source in ((0, q0), (1, q1)):
-        spread = (
-            (cv, DIFFUSION[sp] * above),
-            (ce, DIFFUSION[sp] * east),
-            (cd, 1.0 - DIFFUSION[sp] * faces - DECAY[sp] * react),
-            (cx, cross),
-            (cq, TIME_STEP * source),
-            (gd, 1.0 - (DECAY[sp] * STEPS) * react),
-            (tg, (t0, t1)[sp]),
-        )
-        for ref, value in spread:
-            for j in range(PER_GROUP):
-                ref[pl.ds(sp * PER_GROUP + j, total, stride=SUB), :] = value
+    react_ref[...] = react
+    for sp in range(2):
+        spread(cv, sp, DIFFUSION[sp] * above)
+        spread(ce, sp, DIFFUSION[sp] * east)
+        spread(cd, sp, 1.0 - DIFFUSION[sp] * faces - DECAY[sp] * react)
+        spread(gd, sp, 1.0 - (DECAY[sp] * STEPS) * react)
 
 
 def state_body(
-    count, tile_rows, mid, top_ref, bot_ref, cv, ce, cd, cx, cq, gd, tg, hist, slope, last_ref, *rest
+    count,
+    tile_rows,
+    mid,
+    top_ref,
+    bot_ref,
+    coef_ref,
+    cv,
+    ce,
+    cd,
+    gd,
+    react_ref,
+    hist,
+    slope,
+    last_ref,
+    cx,
+    *rest,
 ):
-    guess, one, two = rest
+    guess, one, two, cq, tg, flat = rest
     groups = count // PER_GROUP
     total = tile_rows + 2 * HALO
     coefs = (cv, ce, cd, cx, cq)
+    coupling, *sources = joined_rows(
+        flat, coef_ref, (top_ref, bot_ref), len(EARLY), LATE, (count - 1) * 2 * HALO
+    )
+    cross = react_ref[...] * coupling
+    for sp in range(2):
+        spread(cx, sp, cross)
+        spread(cq, sp, TIME_STEP * sources[sp])
+        spread(tg, sp, sources[2 + sp])
     lo, hi = STEPS, total - STEPS
-    load(groups, (guess, one), tile_rows, HALO, mid, top_ref, bot_ref)
+    load(groups, (guess, one), tile_rows, mid, top_ref, bot_ref)
     sweep(groups, one, two, 1, total - 1, coefs)
     for a, b in blocks(lo, hi):
         slab = slab_of(a, b)
@@ -343,9 +446,10 @@
     for d in range(count):
         slab = me ^ d
         g, j = slab // PER_GROUP, slab % PER_GROUP
+        both = unpacked(cens[d][...])
         for sp in range(2):
             start = (HALO - HALO_W) * SUB + sp * PER_GROUP + j
-            value = cens[d][sp * tall : (sp + 1) * tall, :]
+            value = both[sp * tall : (sp + 1) * tall, :]
             guess[g, pl.ds(start, tall, stride=SUB), :] = value
             one[g, pl.ds(start, tall, stride=SUB), :] = value
     sweep(groups, one, two, STEPS + 1, total - STEPS - 1, (cv, ce, cd, cx))
@@ -423,28 +527,46 @@
     fv[...] = jnp.zeros_like(fv)
     fh[...] = jnp.zeros_like(fh)
 
+    def products(t, g, a, b, before, here, east):
+        if a < HALO or a > end:
+            return
+        at = slice((a - HALO) * SUB, (b - HALO) * SUB)
+        u = hist[t, g, (a - lo - 1) * SUB : (b - lo) * SUB, :]
+        fv[at, :] += (u[SUB:] - u[:-SUB]) * (here - before)
+        if b <= end:
+            fh[at, :] += slope[t, g, at, :] * (east - here)
+
+    def back_step(src, dst, t, g):
+        step(
+            src.at[g],
+            dst.at[g],
+            w_lo,
+            w_hi,
+            coefs,
+            lambda a, b, before, here, east, new: products(t, g, a, b, before, here, east),
+        )
+
     def back(turn, carry):
+        t = STEPS - 1 - 2 * turn
+
         def run(g):
-            for k, (src, dst) in enumerate(((two, one), (one, two))):
-                t = STEPS - 1 - 2 * turn - k
-
-                def seen(a, b, before, here, east, new, t=t):
-                    if a < HALO or a > end:
-                        return
-                    at = slice((a - HALO) * SUB, (b - HALO) * SUB)
-                    u = hist[t, g, (a - lo - 1) * SUB : (b - lo) * SUB, :]
-                    fv[at, :] += (u[SUB:] - u[:-SUB]) * (here - before)
-                    if b <= end:
-                        fh[at, :] += slope[t, g, at, :] * (
-                            east - here
-                        )
-
-                step(src.at[g], dst.at[g], w_lo, w_hi, coefs, seen)
+            back_step(two, one, t, g)
+            back_step(one, two, t - 1, g)
 
         each_group(groups, run)
         return carry
 
-    lax.fori_loop(0, STEPS // 2, back, 0)
+    lax.fori_loop(0, STEPS // 2 - 1, back, 0)
+
+    def finish(g):
+        back_step(two, one, 1, g)
+        for a, b in blocks(HALO, end + BLOCK):
+            rows = at_rows(one.at[g], a - 1, b)
+            here = rows[SUB:]
+            east = pltpu.roll(here, LANES - 1, 1) if b <= end else None
+            products(0, g, a, b, rows[:-SUB], here, east)
+
+    each_group(groups, finish)
 
     size = tile_rows * SUB
     fh[...] = fv[0:size, :] + fv[SUB : size + SUB, :] + fh[...] + pltpu.roll(fh[...], 1, 1)
@@ -534,51 +656,60 @@
         inputs=[HBM_SPEC] * 7,
     )(*[pltpu.with_memory_space_constraint(f, pltpu.HBM) for f in fields])
     strip = lax.ppermute(strip, "sy", [(0, 1), (1, 0)])
-    pieces = cols // LANES + 1
-    edge = (sum(edges_of(rows)) + 2 * pieces * HALO_W, LANES)
-    *windows, coef, down, up = call(
+    edge = (sum(EARLY) + 2 * (cols // LANES) * HALO_W + SUB, LANES)
+    windows = call(
         functools.partial(window_body, count, rows),
-        [(2 * rows, LANES)] * count + [(7 * rows, LANES), edge, edge],
-        [pltpu.VMEM((11 * rows, cols + 2 * LANES), jnp.float32)],
+        [(2 * rows, LANES)] * count,
+        [pltpu.VMEM((2 * rows, cols + 2 * LANES), jnp.float32)],
     )(tile, strip)
     states = exchanged(windows)
+    coef, down, up = call(
+        functools.partial(edge_body, count, rows),
+        [(7 * rows, LANES), edge, edge],
+        [pltpu.VMEM((7 * rows, cols + 2 * LANES), jnp.float32)],
+    )(tile, strip, windows[0])
     edges = turned(down, up)
     mid, down, up = call(
-        functools.partial(interleave_body, count, HALO),
-        [(groups, rows * SUB, LANES)] + [(groups, HALO * SUB, LANES)] * 2,
-    )(*states)
+        functools.partial(interleave_body, count),
+        [(groups, rows * SUB, LANES)] + [((count - 1) * 2 * HALO + sum(LATE), LANES)] * 2,
+    )(*states, coef)
     state_edges = turned(down, up)
     tall = rows + 2 * HALO_W
     windows = call(
         functools.partial(adjoint_window_body, count, rows),
-        [(2 * tall, LANES)] * count,
+        [(2 * tall * 3 // 4, LANES)] * count,
         [pltpu.VMEM((2 * tall, cols + 2 * LANES), jnp.float32)],
     )(tile, strip, *edges, mid)
     adjoints = exchanged(windows)
     plain = (total * SUB, LANES)
     work = pltpu.VMEM((groups, total * SUB, LANES), jnp.float32)
     limit = 60 << 20 if groups > 1 else 32 << 20
-    *coefs, gd, tg = call(
+    cv, ce, cd, gd, react = call(
         functools.partial(coef_body, count, rows, wide),
-        [plain] * 7,
-        [pltpu.VMEM((7, total, LANES), jnp.float32)],
+        [plain] * 4 + [(total, LANES)],
+        [pltpu.VMEM((len(EARLY), total, LANES), jnp.float32)],
     )(coef, *edges)
+    hist, slope, last, cx = call(
+        functools.partial(state_body, count, rows),
+        [
+            (STEPS, groups, (total - 2 * STEPS) * SUB, LANES),
+            (STEPS, groups, rows * SUB, LANES),
+            ((total - 4 * STEPS) * SUB, LANES),
+            plain,
+        ],
+        [
+            *([work] * 3),
+            *([pltpu.VMEM(plain, jnp.float32)] * 2),
+            pltpu.VMEM((len(LATE), total, LANES), jnp.float32),
+        ],
+        limit,
+    )(mid, *state_edges, coef, cv, ce, cd, gd, react)
     (lag,) = call(
         functools.partial(lag_body, count, rows),
         [(groups, (total - 4 * STEPS) * SUB, LANES)],
         [work] * 3,
         limit,
-    )(*adjoints, *coefs[:4], gd)
-    hist, slope, last = call(
-        functools.partial(state_body, count, rows),
-        [
-            (STEPS, groups, (total - 2 * STEPS) * SUB, LANES),
-            (STEPS, groups, rows * SUB, LANES),
-            ((total - 4 * STEPS) * SUB, LANES),
-        ],
-        [work] * 3,
-        limit,
-    )(mid, *state_edges, *coefs, gd, tg)
+    )(*adjoints, cv, ce, cd, cx, gd)
     outs = call(
         functools.partial(adjoint_body, count, rows),
         [(2 * rows + rows // 2, LANES)] * count,
@@ -588,7 +719,7 @@
             pltpu.VMEM((rows * SUB, LANES), jnp.float32),
         ],
         limit,
-    )(lag, hist, slope, last, *coefs[:4], gd)
+    )(lag, hist, slope, last, cv, ce, cd, cx, gd)
     outs = exchanged(outs)
     states, adjoints, gradient = call(
         functools.partial(collect_body, count, wide),

time: 47.1 us -> 43.7 us (0.928)
  waiting for transfers between devices: 11.4 us -> 8.61 us
  Pallas kernels: 13.9 us -> 13.2 us
    ppermute x9, waiting for transfers between devices: 10.1 us -> 7.29 us  [exchanged(): lax.ppermute(parts[d], 'tm', [(i, i ^ d) for i in range(count)])]
    ppermute x9, starting transfers between devices: 13.5 us -> 14.5 us  [exchanged(): lax.ppermute(parts[d], 'tm', [(i, i ^ d) for i in range(count)])]
    ppermute x2, starting transfers between devices: 3.35 us -> 2.65 us  [turned(): lax.ppermute(up, 'sx', [((i + 1) % n, i) for i in range(n)])]
    pallas_call x9 -> x10, Pallas kernels: 13.9 us -> 13.2 us  [run(): pl.pallas_call(body, out_shape=[jax.ShapeDtypeStruct(s, jnp.float32) for...]
  transfers between devices with their start and end apart: 14 -> 14, of which waited for: 6 -> 5; matrix products, arithmetic and copies ran while one was open for 0% -> 0% of each run, Pallas kernels for 13% -> 14%
where the time goes in v4:
time: 43.7 us; the launch traced here: 43.5 us
  starting transfers between devices  21 us (48%)
  Pallas kernels  13.2 us (30%)
  waiting for transfers between devices  8.61 us (20%)
  between operations  0.75 us (2%)
    ppermute x9, starting transfers between devices, exchanged(): lax.ppermute(parts[d], 'tm', [(i, i ^ d) for i in range(count)])  14.5 us
    pallas_call x10, Pallas kernels, run(): pl.pallas_call(body, out_shape=[jax.ShapeDtypeStruct(s, jnp.float32) for...  13.2 us
    ppermute x9, waiting for transfers between devices, exchanged(): lax.ppermute(parts[d], 'tm', [(i, i ^ d) for i in range(count)])  7.29 us
    ppermute x2, starting transfers between devices, turned(): lax.ppermute(down, 'sx', [(i, (i + 1) % n) for i in range(n)])  3.3 us
    ppermute x2, starting transfers between devices, turned(): lax.ppermute(up, 'sx', [((i + 1) % n, i) for i in range(n)])  2.65 us
    ppermute x1, waiting for transfers between devices, local(): strip = lax.ppermute(strip, 'sy', [(0, 1), (1, 0)])  1.3 us
  transfers between devices with their start and end apart: 14, of which 5 were waited for; matrix products, arithmetic and copies ran while one was open for 0% of the time, Pallas kernels for 14%

profile of v4, /device:TPU:0, one launch (start us, length us, event | category | flops | bytes accessed | tf_op | source)
XLA Modules:
  0.0 43.5 jit_solution(8207851146245783717)
XLA Ops:
  0.6 1.3 %shard_map.94 = (f32[704,256]{1,0:T(8,128)S(1)}, f32[704,128]{1,0:T(8,128)S(1)}) custom-call(f32[128,256]{1,0:T(8,128)} %bitcast.6, f32[128,256]{1,0:T(8,128)} %bitcast.7, f32[64,256]{1,0:T(8,128)} %refs_2_.1, f32[64,256]{1,0:T(8,128)} %refs_3_.1, f32[64,256]{1,0:T(8,128)} %refs_4_.1, f32[128,256]{1,0:T(8,128)} %bitcast.8, f32[128,256]{1,0:T(8,128)} %bitcast.9), custom_call_target="tpu_custom_call" | custom-call | tf_op jit(solution)/shard_map/pallas_call | solution.py:29
  1.9 0.5 %collective-permute-start = (f32[704,128]{1,0:T(8,128)S(1)}, f32[704,128]{1,0:T(8,128)S(1)}, u32[]{:S(2)}, u32[]{:S(2)}) collective-permute-start(f32[704,128]{1,0:T(8,128)S(1)} %get-tuple-element.36), channel_id=1, source_target_pairs={{0,1},{1,0},{2,3},{3,2},{4,5},{5,4},{6,7},{7,6},{8,9},{9,8},{10,11... | collective-permute-start | bytes 1081352 | tf_op jit(solution)/shard_map/ppermute | solution.py:658
  2.5 1.3 %collective-permute-done.strip_ref = f32[704,128]{1,0:T(8,128)S(1)} collective-permute-done((f32[704,128]{1,0:T(8,128)S(1)}, f32[704,128]{1,0:T(8,128)S(1)}, u32[]{:S(2)}, u32[]{:S(2)}) %collective-permute-start) | collective-permute-done | bytes 360480 | tf_op jit(solution)/shard_map/ppermute | solution.py:658
  3.8 0.2 shard_map.95
  4.0 3.0 %collective-permute-start.3 = (f32[128,128]{1,0:T(8,128)S(1)}, f32[128,128]{1,0:T(8,128)S(1)}, u32[]{:S(2)}, u32[]{:S(2)}) collective-permute-start(f32[128,128]{1,0:T(8,128)S(1)} %get-tuple-element.40), channel_id=1, source_target_pairs={{0,8},{8,0},{16,24},{24,16},{1,9},{9,1},{17,25},{25,17},{2,10},{10... | collective-permute-start | bytes 196616 | tf_op jit(solution)/shard_map/ppermute | solution.py:641
  7.0 2.6 %collective-permute-start.4 = (f32[128,128]{1,0:T(8,128)S(1)}, f32[128,128]{1,0:T(8,128)S(1)}, u32[]{:S(2)}, u32[]{:S(2)}) collective-permute-start(f32[128,128]{1,0:T(8,128)S(1)} %get-tuple-element.41), channel_id=1, source_target_pairs={{0,16},{8,24},{16,0},{24,8},{1,17},{9,25},{17,1},{25,9},{2,18},{10... | collective-permute-start | bytes 196616 | tf_op jit(solution)/shard_map/ppermute | solution.py:641
  9.6 0.0 collective-permute-start.5
  9.6 0.3 shard_map.96
  9.9 1.8 %collective-permute-start.1 = (f32[120,128]{1,0:T(8,128)S(1)}, f32[120,128]{1,0:T(8,128)S(1)}, u32[]{:S(2)}, u32[]{:S(2)}) collective-permute-start(f32[120,128]{1,0:T(8,128)S(1)} %get-tuple-element.38), channel_id=1, source_target_pairs={{0,2},{2,4},{4,6},{6,0},{1,3},{3,5},{5,7},{7,1},{8,10},{10,12},{12... | collective-permute-start | bytes 184328 | tf_op jit(solution)/shard_map/ppermute | solution.py:648
  11.7 1.2 %collective-permute-start.2 = (f32[120,128]{1,0:T(8,128)S(1)}, f32[120,128]{1,0:T(8,128)S(1)}, u32[]{:S(2)}, u32[]{:S(2)}) collective-permute-start(f32[120,128]{1,0:T(8,128)S(1)} %get-tuple-element.39), channel_id=1, source_target_pairs={{2,0},{4,2},{6,4},{0,6},{3,1},{5,3},{7,5},{1,7},{10,8},{12,10},{14... | collective-permute-start | bytes 184328 | tf_op jit(solution)/shard_map/ppermute | solution.py:649
  12.9 0.0 collective-permute-done.3.refs_1_
  12.9 1.7 %collective-permute-done.4.refs_2_ = f32[128,128]{1,0:T(8,128)S(1)} collective-permute-done((f32[128,128]{1,0:T(8,128)S(1)}, f32[128,128]{1,0:T(8,128)S(1)}, u32[]{:S(2)}, u32[]{:S(2)}) %collective-permute-start.4) | collective-permute-done | bytes 65568 | tf_op jit(solution)/shard_map/ppermute | solution.py:641
  14.5 1.2 %collective-permute-done.5.refs_3_ = f32[128,128]{1,0:T(8,128)S(1)} collective-permute-done((f32[128,128]{1,0:T(8,128)S(1)}, f32[128,128]{1,0:T(8,128)S(1)}, u32[]{:S(2)}, u32[]{:S(2)}) %collective-permute-start.5) | collective-permute-done | bytes 65568 | tf_op jit(solution)/shard_map/ppermute | solution.py:641
  15.8 0.1 shard_map.97
  15.9 1.5 %collective-permute-start.9 = (f32[232,128]{1,0:T(8,128)S(1)}, f32[232,128]{1,0:T(8,128)S(1)}, u32[]{:S(2)}, u32[]{:S(2)}) collective-permute-start(f32[232,128]{1,0:T(8,128)S(1)} %get-tuple-element.52), channel_id=1, source_target_pairs={{0,2},{2,4},{4,6},{6,0},{1,3},{3,5},{5,7},{7,1},{8,10},{10,12},{12... | collective-permute-start | bytes 356360 | tf_op jit(solution)/shard_map/ppermute | solution.py:648
  17.4 1.4 %collective-permute-start.10 = (f32[232,128]{1,0:T(8,128)S(1)}, f32[232,128]{1,0:T(8,128)S(1)}, u32[]{:S(2)}, u32[]{:S(2)}) collective-permute-start(f32[232,128]{1,0:T(8,128)S(1)} %get-tuple-element.53), channel_id=1, source_target_pairs={{2,0},{4,2},{6,4},{0,6},{3,1},{5,3},{7,5},{1,7},{10,8},{12,10},{14... | collective-permute-start | bytes 356360 | tf_op jit(solution)/shard_map/ppermute | solution.py:649
  18.8 0.0 collective-permute-done.1.top_ref
  18.8 0.0 collective-permute-done.2.bot_ref
  18.8 0.6 %shard_map.98 = (f32[144,128]{1,0:T(8,128)S(1)}, f32[144,128]{1,0:T(8,128)S(1)}, f32[144,128]{1,0:T(8,128)S(1)}, f32[144,128]{1,0:T(8,128)S(1)}) custom-call(f32[704,256]{1,0:T(8,128)S(1)} %get-tuple-element.35.tile_ref, f32[704,128]{1,0:T(8,128)S(1)} %collective-permute-done.strip_ref, f32[120,128]{1,0:T(8,128)S(1)} %collective-permute-done.1.top_ref, ...), custom_call_target="tpu_custom_call" | custom-call | tf_op jit(solution)/shard_map/pallas_call | solution.py:29
  19.5 0.9 %collective-permute-start.6 = (f32[144,128]{1,0:T(8,128)S(1)}, f32[144,128]{1,0:T(8,128)S(1)}, u32[]{:S(2)}, u32[]{:S(2)}) collective-permute-start(f32[144,128]{1,0:T(8,128)S(1)} %get-tuple-element.46), channel_id=1, source_target_pairs={{0,8},{8,0},{16,24},{24,16},{1,9},{9,1},{17,25},{25,17},{2,10},{10... | collective-permute-start | bytes 221192 | tf_op jit(solution)/shard_map/ppermute | solution.py:641
  20.4 1.7 %collective-permute-start.7 = (f32[144,128]{1,0:T(8,128)S(1)}, f32[144,128]{1,0:T(8,128)S(1)}, u32[]{:S(2)}, u32[]{:S(2)}) collective-permute-start(f32[144,128]{1,0:T(8,128)S(1)} %get-tuple-element.47), channel_id=1, source_target_pairs={{0,16},{8,24},{16,0},{24,8},{1,17},{9,25},{17,1},{25,9},{2,18},{10... | collective-permute-start | bytes 221192 | tf_op jit(solution)/shard_map/ppermute | solution.py:641
  22.1 1.8 %collective-permute-start.8 = (f32[144,128]{1,0:T(8,128)S(1)}, f32[144,128]{1,0:T(8,128)S(1)}, u32[]{:S(2)}, u32[]{:S(2)}) collective-permute-start(f32[144,128]{1,0:T(8,128)S(1)} %get-tuple-element.48), channel_id=1, source_target_pairs={{0,24},{8,16},{16,8},{24,0},{1,25},{9,17},{17,9},{25,1},{2,26},{10... | collective-permute-start | bytes 221192 | tf_op jit(solution)/shard_map/ppermute | solution.py:641
  23.9 0.3 shard_map.99
  24.2 0.0 collective-permute-done.9.top_ref
  24.2 0.0 collective-permute-done.10.bot_ref
  24.3 4.8 %shard_map.100 = (f32[8,1,768,128]{3,2,1,0:T(8,128)S(1)}, f32[8,1,512,128]{3,2,1,0:T(8,128)S(1)}, f32[640,128]{1,0:T(8,128)S(1)}, f32[896,128]{1,0:T(8,128)S(1)}) custom-call(f32[1,512,128]{2,1,0:T(8,128)S(1)} %get-tuple-element.44.after.mid, f32[232,128]{1,0:T(8,128)S(1)} %collective-permute-done.9.top_ref, f32[232,128]{1,0:T(8,128)S(1)} %collective-permute-done.10.bot_ref, ...), custom_call_target="tpu_custom_call" | custom-call | tf_op jit(solution)/shard_map/pallas_call | solution.py:29
  29.0 0.0 collective-permute-done.6.refs_1_
  29.0 0.0 collective-permute-done.7.refs_2_
  29.1 0.0 collective-permute-done.8.refs_3_
  29.1 2.2 %shard_map.101.lag = f32[1,640,128]{2,1,0:T(8,128)S(1)} custom-call(f32[144,128]{1,0:T(8,128)S(1)} %get-tuple-element.45.refs_0_, f32[144,128]{1,0:T(8,128)S(1)} %collective-permute-done.6.refs_1_, f32[144,128]{1,0:T(8,128)S(1)} %collective-permute-done.7.refs_2_, f32[144,128]{1,0:T(8,128)S(1)} %collective-permute-done.8.refs_3_, ...), custom_call_target="tpu_custom_call" | custom-call | tf_op jit(solution)/shard_map/pallas_call | solution.py:29
  31.3 2.5 %shard_map.102 = (f32[160,128]{1,0:T(8,128)S(1)}, f32[160,128]{1,0:T(8,128)S(1)}, f32[160,128]{1,0:T(8,128)S(1)}, f32[160,128]{1,0:T(8,128)S(1)}) custom-call(f32[1,640,128]{2,1,0:T(8,128)S(1)} %shard_map.101.lag, f32[8,1,768,128]{3,2,1,0:T(8,128)S(1)} %get-tuple-element.57.hist, f32[8,1,512,128]{3,2,1,0:T(8,128)S(1)} %get-tuple-element.58.slope, ...), custom_call_target="tpu_custom_call" | custom-call | tf_op jit(solution)/shard_map/pallas_call | solution.py:29
  33.8 0.1 collective-permute-start.11
  33.9 2.5 %collective-permute-start.12 = (f32[160,128]{1,0:T(8,128)S(1)}, f32[160,128]{1,0:T(8,128)S(1)}, u32[]{:S(2)}, u32[]{:S(2)}) collective-permute-start(f32[160,128]{1,0:T(8,128)S(1)} %get-tuple-element.62), channel_id=1, source_target_pairs={{0,16},{8,24},{16,0},{24,8},{1,17},{9,25},{17,1},{25,9},{2,18},{10... | collective-permute-start | bytes 245768 | tf_op jit(solution)/shard_map/ppermute | solution.py:641
  36.4 1.8 %collective-permute-start.13 = (f32[160,128]{1,0:T(8,128)S(1)}, f32[160,128]{1,0:T(8,128)S(1)}, u32[]{:S(2)}, u32[]{:S(2)}) collective-permute-start(f32[160,128]{1,0:T(8,128)S(1)} %get-tuple-element.63), channel_id=1, source_target_pairs={{0,24},{8,16},{16,8},{24,0},{1,25},{9,17},{17,9},{25,1},{2,26},{10... | collective-permute-start | bytes 245768 | tf_op jit(solution)/shard_map/ppermute | solution.py:641
  38.3 1.8 %collective-permute-done.11.refs_1_ = f32[160,128]{1,0:T(8,128)S(1)} collective-permute-done((f32[160,128]{1,0:T(8,128)S(1)}, f32[160,128]{1,0:T(8,128)S(1)}, u32[]{:S(2)}, u32[]{:S(2)}) %collective-permute-start.11) | collective-permute-done | bytes 81952 | tf_op jit(solution)/shard_map/ppermute | solution.py:641
  40.1 0.0 collective-permute-done.12.refs_2_
  40.1 2.6 %collective-permute-done.13.refs_3_ = f32[160,128]{1,0:T(8,128)S(1)} collective-permute-done((f32[160,128]{1,0:T(8,128)S(1)}, f32[160,128]{1,0:T(8,128)S(1)}, u32[]{:S(2)}, u32[]{:S(2)}) %collective-permute-start.13) | collective-permute-done | bytes 81952 | tf_op jit(solution)/shard_map/ppermute | solution.py:641
  42.7 0.9 %shard_map.103 = (f32[128,256]{1,0:T(8,128)}, f32[128,256]{1,0:T(8,128)}, f32[64,256]{1,0:T(8,128)}) custom-call(f32[160,128]{1,0:T(8,128)S(1)} %get-tuple-element.60.refs_0_, f32[160,128]{1,0:T(8,128)S(1)} %collective-permute-done.11.refs_1_, f32[160,128]{1,0:T(8,128)S(1)} %collective-permute-done.12.refs_2_, f32[160,128]{1,0:T(8,128)S(1)} %collective-permute-done.13.refs_3_), custom_call_target="tpu_custom_call" | custom-call | tf_op jit(solution)/shard_map/pallas_call | solution.py:29
Async XLA Ops:
  1.9 1.8 %collective-permute-start = (f32[704,128]{1,0:T(8,128)S(1)}, f32[704,128]{1,0:T(8,128)S(1)}, u32[]{:S(2)}, u32[]{:S(2)}) collective-permute-start(f32[704,128]{1,0:T(8,128)S(1)} %get-tuple-element.36), channel_id=1, source_target_pairs={{0,1},{1,0},{2,3},{3,2},{4,5},{5,4},{6,7},{7,6},{8,9},{9,8},{10,11... | collective-permute-start | bytes 1081352 | tf_op jit(solution)/shard_map/ppermute | solution.py:658
  4.0 8.9 %collective-permute-start.3 = (f32[128,128]{1,0:T(8,128)S(1)}, f32[128,128]{1,0:T(8,128)S(1)}, u32[]{:S(2)}, u32[]{:S(2)}) collective-permute-start(f32[128,128]{1,0:T(8,128)S(1)} %get-tuple-element.40), channel_id=1, source_target_pairs={{0,8},{8,0},{16,24},{24,16},{1,9},{9,1},{17,25},{25,17},{2,10},{10... | collective-permute-start | bytes 196616 | tf_op jit(solution)/shard_map/ppermute | solution.py:641
  7.0 7.5 %collective-permute-start.4 = (f32[128,128]{1,0:T(8,128)S(1)}, f32[128,128]{1,0:T(8,128)S(1)}, u32[]{:S(2)}, u32[]{:S(2)}) collective-permute-start(f32[128,128]{1,0:T(8,128)S(1)} %get-tuple-element.41), channel_id=1, source_target_pairs={{0,16},{8,24},{16,0},{24,8},{1,17},{9,25},{17,1},{25,9},{2,18},{10... | collective-permute-start | bytes 196616 | tf_op jit(solution)/shard_map/ppermute | solution.py:641
  9.6 6.2 %collective-permute-start.5 = (f32[128,128]{1,0:T(8,128)S(1)}, f32[128,128]{1,0:T(8,128)S(1)}, u32[]{:S(2)}, u32[]{:S(2)}) collective-permute-start(f32[128,128]{1,0:T(8,128)S(1)} %get-tuple-element.42), channel_id=1, source_target_pairs={{0,24},{8,16},{16,8},{24,0},{1,25},{9,17},{17,9},{25,1},{2,26},{10... | collective-permute-start | bytes 196616 | tf_op jit(solution)/shard_map/ppermute | solution.py:641
  9.9 8.9 %collective-permute-start.1 = (f32[120,128]{1,0:T(8,128)S(1)}, f32[120,128]{1,0:T(8,128)S(1)}, u32[]{:S(2)}, u32[]{:S(2)}) collective-permute-start(f32[120,128]{1,0:T(8,128)S(1)} %get-tuple-element.38), channel_id=1, source_target_pairs={{0,2},{2,4},{4,6},{6,0},{1,3},{3,5},{5,7},{7,1},{8,10},{10,12},{12... | collective-permute-start | bytes 184328 | tf_op jit(solution)/shard_map/ppermute | solution.py:648
  11.7 7.2 %collective-permute-start.2 = (f32[120,128]{1,0:T(8,128)S(1)}, f32[120,128]{1,0:T(8,128)S(1)}, u32[]{:S(2)}, u32[]{:S(2)}) collective-permute-start(f32[120,128]{1,0:T(8,128)S(1)} %get-tuple-element.39), channel_id=1, source_target_pairs={{2,0},{4,2},{6,4},{0,6},{3,1},{5,3},{7,5},{1,7},{10,8},{12,10},{14... | collective-permute-start | bytes 184328 | tf_op jit(solution)/shard_map/ppermute | solution.py:649
  15.9 8.4 %collective-permute-start.9 = (f32[232,128]{1,0:T(8,128)S(1)}, f32[232,128]{1,0:T(8,128)S(1)}, u32[]{:S(2)}, u32[]{:S(2)}) collective-permute-start(f32[232,128]{1,0:T(8,128)S(1)} %get-tuple-element.52), channel_id=1, source_target_pairs={{0,2},{2,4},{4,6},{6,0},{1,3},{3,5},{5,7},{7,1},{8,10},{10,12},{12... | collective-permute-start | bytes 356360 | tf_op jit(solution)/shard_map/ppermute | solution.py:648
  17.4 6.9 %collective-permute-start.10 = (f32[232,128]{1,0:T(8,128)S(1)}, f32[232,128]{1,0:T(8,128)S(1)}, u32[]{:S(2)}, u32[]{:S(2)}) collective-permute-start(f32[232,128]{1,0:T(8,128)S(1)} %get-tuple-element.53), channel_id=1, source_target_pairs={{2,0},{4,2},{6,4},{0,6},{3,1},{5,3},{7,5},{1,7},{10,8},{12,10},{14... | collective-permute-start | bytes 356360 | tf_op jit(solution)/shard_map/ppermute | solution.py:649
  19.5 9.6 %collective-permute-start.6 = (f32[144,128]{1,0:T(8,128)S(1)}, f32[144,128]{1,0:T(8,128)S(1)}, u32[]{:S(2)}, u32[]{:S(2)}) collective-permute-start(f32[144,128]{1,0:T(8,128)S(1)} %get-tuple-element.46), channel_id=1, source_target_pairs={{0,8},{8,0},{16,24},{24,16},{1,9},{9,1},{17,25},{25,17},{2,10},{10... | collective-permute-start | bytes 221192 | tf_op jit(solution)/shard_map/ppermute | solution.py:641
  20.4 8.7 %collective-permute-start.7 = (f32[144,128]{1,0:T(8,128)S(1)}, f32[144,128]{1,0:T(8,128)S(1)}, u32[]{:S(2)}, u32[]{:S(2)}) collective-permute-start(f32[144,128]{1,0:T(8,128)S(1)} %get-tuple-element.47), channel_id=1, source_target_pairs={{0,16},{8,24},{16,0},{24,8},{1,17},{9,25},{17,1},{25,9},{2,18},{10... | collective-permute-start | bytes 221192 | tf_op jit(solution)/shard_map/ppermute | solution.py:641
  22.1 7.0 %collective-permute-start.8 = (f32[144,128]{1,0:T(8,128)S(1)}, f32[144,128]{1,0:T(8,128)S(1)}, u32[]{:S(2)}, u32[]{:S(2)}) collective-permute-start(f32[144,128]{1,0:T(8,128)S(1)} %get-tuple-element.48), channel_id=1, source_target_pairs={{0,24},{8,16},{16,8},{24,0},{1,25},{9,17},{17,9},{25,1},{2,26},{10... | collective-permute-start | bytes 221192 | tf_op jit(solution)/shard_map/ppermute | solution.py:641
  33.8 6.2 %collective-permute-start.11 = (f32[160,128]{1,0:T(8,128)S(1)}, f32[160,128]{1,0:T(8,128)S(1)}, u32[]{:S(2)}, u32[]{:S(2)}) collective-permute-start(f32[160,128]{1,0:T(8,128)S(1)} %get-tuple-element.61), channel_id=1, source_target_pairs={{0,8},{8,0},{16,24},{24,16},{1,9},{9,1},{17,25},{25,17},{2,10},{10... | collective-permute-start | bytes 245768 | tf_op jit(solution)/shard_map/ppermute | solution.py:641
  33.9 6.2 %collective-permute-start.12 = (f32[160,128]{1,0:T(8,128)S(1)}, f32[160,128]{1,0:T(8,128)S(1)}, u32[]{:S(2)}, u32[]{:S(2)}) collective-permute-start(f32[160,128]{1,0:T(8,128)S(1)} %get-tuple-element.62), channel_id=1, source_target_pairs={{0,16},{8,24},{16,0},{24,8},{1,17},{9,25},{17,1},{25,9},{2,18},{10... | collective-permute-start | bytes 245768 | tf_op jit(solution)/shard_map/ppermute | solution.py:641
  36.4 6.2 %collective-permute-start.13 = (f32[160,128]{1,0:T(8,128)S(1)}, f32[160,128]{1,0:T(8,128)S(1)}, u32[]{:S(2)}, u32[]{:S(2)}) collective-permute-start(f32[160,128]{1,0:T(8,128)S(1)} %get-tuple-element.63), channel_id=1, source_target_pairs={{0,24},{8,16},{16,8},{24,0},{1,25},{9,17},{17,9},{25,1},{2,26},{10... | collective-permute-start | bytes 245768 | tf_op jit(solution)/shard_map/ppermute | solution.py:641

commit v5 on v4

--- a/solution.py
+++ b/solution.py
@@ -19,12 +19,14 @@
 HALO_W = 2 * STEPS
 SIDE = 32
 BLOCK = 8
+PARTS = (0, STEPS // 2)
+TURNS = STEPS // (2 * len(PARTS))
 
 VMEM_SPEC = pl.BlockSpec(memory_space=pltpu.VMEM)
 HBM_SPEC = pl.BlockSpec(memory_space=pltpu.HBM)
 
 
-def call(body, outs, scratch=(), limit=32 << 20, inputs=None):
+def call(body, outs, scratch=(), limit=32 << 20, inputs=None, aliases=None):
     def run(*args):
         return pl.pallas_call(
             body,
@@ -32,6 +34,7 @@
             in_specs=inputs or [VMEM_SPEC] * len(args),
             out_specs=[VMEM_SPEC] * len(outs),
             scratch_shapes=list(scratch),
+            input_output_aliases=aliases or {},
             compiler_params=pltpu.CompilerParams(vmem_limit_bytes=limit),
         )(*args)
 
@@ -106,6 +109,36 @@
     return pltpu.roll(ext[lo:hi, pl.ds(base, 2 * LANES)], turn, 1)[:, :LANES]
 
 
+PACKED = 3 * LANES // 4
+
+
+def packed(value):
+    n = value.shape[0] // 4
+    cut = (LANES - PACKED) // 2
+    lane = lax.broadcasted_iota(jnp.int32, (n, LANES), 1)
+    last = value[3 * n :]
+    parts = []
+    for i in range(3):
+        main = pltpu.roll(value[i * n : (i + 1) * n], LANES - cut, 1)
+        rest = pltpu.roll(last, (PACKED - cut - i * (LANES - PACKED)) % LANES, 1)
+        parts.append(jnp.where(lane < PACKED, main, rest))
+    return jnp.concatenate(parts, axis=0)
+
+
+def unpacked(value):
+    n = value.shape[0] // 3
+    cut = (LANES - PACKED) // 2
+    side = LANES - PACKED
+    lane = lax.broadcasted_iota(jnp.int32, (n, LANES), 1)
+    parts, last = [], None
+    for i in range(3):
+        part = value[i * n : (i + 1) * n]
+        parts.append(pltpu.roll(part, cut, 1))
+        rest = pltpu.roll(part, (cut + i * side - PACKED) % LANES, 1)
+        last = rest if i == 0 else jnp.where(lane >= cut + i * side, rest, last)
+    return jnp.concatenate([*parts, last], axis=0)
+
+
 def window_body(count, rows, tile_ref, strip_ref, *refs):
     outs, ext = refs[:count], refs[count]
     me = lax.axis_index("tm")
@@ -115,12 +148,18 @@
         outs[d][...] = window(ext, 0, 2 * rows, wide * (me ^ d))
 
 
-def edge_body(count, rows, tile_ref, strip_ref, after, coef_ref, down_ref, up_ref, ext):
+def edge_body(count, rows, tile_ref, strip_ref, after, *refs):
     del after
+    outs, (coef_ref, down_ref, up_ref, ext) = refs[:count], refs[count:]
     me = lax.axis_index("tm")
     cols = tile_ref.shape[1]
-    extend(ext, 0, 7 * rows, tile_ref[4 * rows :, :], strip_ref[4 * rows :, :])
-    coef_ref[...] = window(ext, 0, 7 * rows, cols // count * me)
+    wide = cols // count
+    extend(ext, 0, 9 * rows, tile_ref[2 * rows :, :], strip_ref[2 * rows :, :])
+    coef_ref[...] = window(ext, 2 * rows, 9 * rows, wide * me)
+    for d in range(count):
+        outs[d][: 2 * rows * PACKED // LANES, :] = packed(
+            window(ext, 0, 2 * rows, wide * (me ^ d))
+        )
     at = edge_rows((down_ref, up_ref), coef_ref, 0, EARLY, 0)
     lane = lax.broadcasted_iota(jnp.int32, (SUB, LANES), 1)
     for ref, low in ((down_ref, rows - HALO_W), (up_ref, 0)):
@@ -144,59 +183,19 @@
         ref[put : put + SUB, :] = sides
 
 
-PACKED = 3 * LANES // 4
-
-
-def packed(value):
-    n = value.shape[0] // 4
-    cut = (LANES - PACKED) // 2
-    lane = lax.broadcasted_iota(jnp.int32, (n, LANES), 1)
-    last = value[3 * n :]
-    parts = []
-    for i in range(3):
-        main = pltpu.roll(value[i * n : (i + 1) * n], LANES - cut, 1)
-        rest = pltpu.roll(last, (PACKED - cut - i * (LANES - PACKED)) % LANES, 1)
-        parts.append(jnp.where(lane < PACKED, main, rest))
-    return jnp.concatenate(parts, axis=0)
-
-
-def unpacked(value):
-    n = value.shape[0] // 3
-    cut = (LANES - PACKED) // 2
-    side = LANES - PACKED
-    lane = lax.broadcasted_iota(jnp.int32, (n, LANES), 1)
-    parts, last = [], None
-    for i in range(3):
-        part = value[i * n : (i + 1) * n]
-        parts.append(pltpu.roll(part, cut, 1))
-        rest = pltpu.roll(part, (cut + i * side - PACKED) % LANES, 1)
-        last = rest if i == 0 else jnp.where(lane >= cut + i * side, rest, last)
-    return jnp.concatenate([*parts, last], axis=0)
-
-
-def adjoint_window_body(count, rows, tile_ref, strip_ref, top_ref, bot_ref, after, *refs):
+def adjoint_window_body(count, rows, cols, top_ref, bot_ref, after, *refs):
     del after
-    outs, ext = refs[:count], refs[count]
+    outs, ext = refs[count : 2 * count], refs[2 * count]
     me = lax.axis_index("tm")
     s_at = lax.axis_index("sx")
-    cols = tile_ref.shape[1]
     wide = cols // count
-    tall = rows + 2 * HALO_W
     for sp in range(2):
-        lo = (2 + sp) * rows
-        base = sp * tall
+        base = sp * 2 * HALO_W
         at = sum(EARLY) + sp * (cols // LANES) * HALO_W
         side_at = sum(EARLY) + 2 * (cols // LANES) * HALO_W
-        extend(
-            ext,
-            base + HALO_W,
-            base + HALO_W + rows,
-            tile_ref[lo : lo + rows, :],
-            strip_ref[lo : lo + rows, :],
-        )
         for ref, start, flag in (
             (top_ref, base, s_at > 0),
-            (bot_ref, base + HALO_W + rows, s_at < lax.axis_size("sx") - 1),
+            (bot_ref, base + HALO_W, s_at < lax.axis_size("sx") - 1),
         ):
             parts = [
                 masked(flag, ref[at + i * HALO_W : at + (i + 1) * HALO_W, :])
@@ -221,7 +220,9 @@
                 jnp.concatenate(strips, axis=0),
             )
     for d in range(count):
-        outs[d][...] = packed(window(ext, 0, 2 * tall, wide * (me ^ d)))
+        outs[d][2 * rows * PACKED // LANES :, :] = packed(
+            window(ext, 0, 4 * HALO_W, wide * (me ^ d))
+        )
 
 
 def interleave_body(count, *refs):
@@ -230,7 +231,7 @@
     rows = cens[0].shape[0] // 2
     me = lax.axis_index("tm")
     for d in range(count):
-        slab = me ^ d
+        slab = me ^ (-d % count)
         g, j = slab // PER_GROUP, slab % PER_GROUP
         for sp in range(2):
             mid[g, pl.ds(sp * PER_GROUP + j, rows, stride=SUB), :] = cens[d][
@@ -300,15 +301,17 @@
 
 
 def sweep(groups, one, two, lo, hi, coefs):
-    def turn(t, carry):
-        def run(g):
-            step(one.at[g], two.at[g], lo, hi, coefs)
-            step(two.at[g], one.at[g], lo, hi, coefs)
-
-        each_group(groups, run)
-        return carry
-
-    lax.fori_loop(0, STEPS // 2, turn, 0)
+    for cut in PARTS:
+
+        def turn(t, carry, a=lo + cut, b=hi - cut):
+            def run(g):
+                step(one.at[g], two.at[g], a, b, coefs)
+                step(two.at[g], one.at[g], a, b, coefs)
+
+            each_group(groups, run)
+            return carry
+
+        lax.fori_loop(0, TURNS, turn, 0)
 
 
 def coarse(gd, cx, value, a, b):
@@ -416,23 +419,26 @@
 
         through_groups(groups, chain, jnp.zeros(((b - a) * SUB, LANES), jnp.float32))
 
-    def forward(turn, carry):
-        def run(g):
-            for k, (src, dst) in enumerate(((two, one), (one, two))):
-                t = 2 * turn + k
-
-                def seen(a, b, before, here, east, new, t=t):
-                    hist[t, g, (a - lo) * SUB : (b - lo) * SUB, :] = here
-                    if HALO <= a < HALO + tile_rows:
-                        at = slice((a - HALO) * SUB, (b - HALO) * SUB)
-                        slope[t, g, at, :] = east - here
-
-                step(src.at[g], dst.at[g], lo, hi, coefs, seen)
-
-        each_group(groups, run)
-        return carry
-
-    lax.fori_loop(0, STEPS // 2, forward, 0)
+    for i, cut in enumerate(PARTS):
+
+        def forward(turn, carry, base=2 * TURNS * i, cut=cut):
+            def run(g):
+                for k, (src, dst) in enumerate(((two, one), (one, two))):
+                    t = base + 2 * turn + k
+
+                    def seen(a, b, before, here, east, new, t=t):
+                        hist[t, g, (a - lo) * SUB : (b - lo) * SUB, :] = here
+                        p, q = max(a, HALO), min(b, HALO + tile_rows)
+                        if p < q:
+                            rise = (east - here)[(p - a) * SUB : (q - a) * SUB]
+                            slope[t, g, (p - HALO) * SUB : (q - HALO) * SUB, :] = rise
+
+                    step(src.at[g], dst.at[g], lo + cut, hi - cut, coefs, seen)
+
+            each_group(groups, run)
+            return carry
+
+        lax.fori_loop(0, TURNS, forward, 0)
     w_lo, w_hi = 2 * STEPS, total - 2 * STEPS
     last_ref[...] = at_rows(two.at[groups - 1], w_lo, w_hi) - at_rows(tg, w_lo, w_hi)
 
@@ -441,17 +447,22 @@
     cens, (cv, ce, cd, cx, gd, lag, guess, one, two) = refs[:count], refs[count:]
     groups = count // PER_GROUP
     total = tile_rows + 2 * HALO
-    tall = tile_rows + 2 * HALO_W
     me = lax.axis_index("tm")
     for d in range(count):
         slab = me ^ d
         g, j = slab // PER_GROUP, slab % PER_GROUP
-        both = unpacked(cens[d][...])
+        split = 2 * tile_rows * PACKED // LANES
+        inner, outer = unpacked(cens[d][:split, :]), unpacked(cens[d][split:, :])
         for sp in range(2):
-            start = (HALO - HALO_W) * SUB + sp * PER_GROUP + j
-            value = both[sp * tall : (sp + 1) * tall, :]
-            guess[g, pl.ds(start, tall, stride=SUB), :] = value
-            one[g, pl.ds(start, tall, stride=SUB), :] = value
+            edge = 2 * HALO_W * sp
+            for start, value in (
+                (HALO, inner[sp * tile_rows : (sp + 1) * tile_rows]),
+                (HALO - HALO_W, outer[edge : edge + HALO_W]),
+                (HALO + tile_rows, outer[edge + HALO_W : edge + 2 * HALO_W]),
+            ):
+                at = pl.ds(start * SUB + sp * PER_GROUP + j, value.shape[0], stride=SUB)
+                guess[g, at, :] = value
+                one[g, at, :] = value
     sweep(groups, one, two, STEPS + 1, total - STEPS - 1, (cv, ce, cd, cx))
     w_lo, w_hi = 2 * STEPS, total - 2 * STEPS
 
@@ -528,20 +539,24 @@
     fh[...] = jnp.zeros_like(fh)
 
     def products(t, g, a, b, before, here, east):
-        if a < HALO or a > end:
-            return
-        at = slice((a - HALO) * SUB, (b - HALO) * SUB)
-        u = hist[t, g, (a - lo - 1) * SUB : (b - lo) * SUB, :]
-        fv[at, :] += (u[SUB:] - u[:-SUB]) * (here - before)
-        if b <= end:
-            fh[at, :] += slope[t, g, at, :] * (east - here)
-
-    def back_step(src, dst, t, g):
+        for ref, stop in ((fv, end + 1), (fh, end)):
+            p, q = max(a, HALO), min(b, stop)
+            if p >= q:
+                continue
+            at = slice((p - HALO) * SUB, (q - HALO) * SUB)
+            part = slice((p - a) * SUB, (q - a) * SUB)
+            if ref is fv:
+                u = hist[t, g, (p - lo - 1) * SUB : (q - lo) * SUB, :]
+                ref[at, :] += (u[SUB:] - u[:-SUB]) * (here[part] - before[part])
+            else:
+                ref[at, :] += slope[t, g, at, :] * (east[part] - here[part])
+
+    def back_step(src, dst, t, g, cut):
         step(
             src.at[g],
             dst.at[g],
-            w_lo,
-            w_hi,
+            w_lo + cut,
+            w_hi - cut,
             coefs,
             lambda a, b, before, here, east, new: products(t, g, a, b, before, here, east),
         )
@@ -550,21 +565,23 @@
         t = STEPS - 1 - 2 * turn
 
         def run(g):
-            back_step(two, one, t, g)
-            back_step(one, two, t - 1, g)
+            back_step(two, one, t, g, 0)
+            back_step(one, two, t - 1, g, 0)
 
         each_group(groups, run)
         return carry
 
-    lax.fori_loop(0, STEPS // 2 - 1, back, 0)
+    lax.fori_loop(0, TURNS, back, 0)
 
     def finish(g):
-        back_step(two, one, 1, g)
-        for a, b in blocks(HALO, end + BLOCK):
+        cut = 2 * TURNS
+        for t in range(STEPS - 1 - cut, 0, -1):
+            src, dst = (two, one) if t % 2 else (one, two)
+            back_step(src, dst, t, g, cut)
+        for a, b in blocks(HALO, end + 1):
             rows = at_rows(one.at[g], a - 1, b)
             here = rows[SUB:]
-            east = pltpu.roll(here, LANES - 1, 1) if b <= end else None
-            products(0, g, a, b, rows[:-SUB], here, east)
+            products(0, g, a, b, rows[:-SUB], here, pltpu.roll(here, LANES - 1, 1))
 
     each_group(groups, finish)
 
@@ -592,7 +609,7 @@
     s_ref, w_ref, g_ref, held = refs[count:]
     me = lax.axis_index("tm")
     for d in range(count):
-        held[me ^ d] = parts[d][...]
+        held[me ^ (-d % count)] = parts[d][...]
     rows = g_ref.shape[0]
     middle = rows // 2
     per = LANES // wide
@@ -636,10 +653,10 @@
         target.reshape(2 * rows, cols),
     )
 
-    def exchanged(parts):
+    def exchanged(parts, far_first=True):
+        order = range(count - 1, 0, -1) if far_first else range(1, count)
         return [parts[0]] + [
-            lax.ppermute(parts[d], "tm", [(i, i ^ d) for i in range(count)])
-            for d in range(1, count)
+            lax.ppermute(parts[d], "tm", [(i, i ^ d) for i in range(count)]) for d in order
         ]
 
     def turned(down, up):
@@ -663,10 +680,11 @@
         [pltpu.VMEM((2 * rows, cols + 2 * LANES), jnp.float32)],
     )(tile, strip)
     states = exchanged(windows)
-    coef, down, up = call(
+    size = 2 * (rows + 2 * HALO_W) * PACKED // LANES
+    *inner, coef, down, up = call(
         functools.partial(edge_body, count, rows),
-        [(7 * rows, LANES), edge, edge],
-        [pltpu.VMEM((7 * rows, cols + 2 * LANES), jnp.float32)],
+        [(size, LANES)] * count + [(7 * rows, LANES), edge, edge],
+        [pltpu.VMEM((9 * rows, cols + 2 * LANES), jnp.float32)],
     )(tile, strip, windows[0])
     edges = turned(down, up)
     mid, down, up = call(
@@ -674,13 +692,13 @@
         [(groups, rows * SUB, LANES)] + [((count - 1) * 2 * HALO + sum(LATE), LANES)] * 2,
     )(*states, coef)
     state_edges = turned(down, up)
-    tall = rows + 2 * HALO_W
     windows = call(
-        functools.partial(adjoint_window_body, count, rows),
-        [(2 * tall * 3 // 4, LANES)] * count,
-        [pltpu.VMEM((2 * tall, cols + 2 * LANES), jnp.float32)],
-    )(tile, strip, *edges, mid)
-    adjoints = exchanged(windows)
+        functools.partial(adjoint_window_body, count, rows, cols),
+        [(size, LANES)] * count,
+        [pltpu.VMEM((4 * HALO_W, cols + 2 * LANES), jnp.float32)],
+        aliases={3 + d: d for d in range(count)},
+    )(*edges, mid, *inner)
+    adjoints = exchanged(windows, far_first=False)
     plain = (total * SUB, LANES)
     work = pltpu.VMEM((groups, total * SUB, LANES), jnp.float32)
     limit = 60 << 20 if groups > 1 else 32 << 20
@@ -715,7 +733,7 @@
         [(2 * rows + rows // 2, LANES)] * count,
         [
             *([work] * 2),
-            pltpu.VMEM(((rows + BLOCK) * SUB, LANES), jnp.float32),
+            pltpu.VMEM(((rows + 1) * SUB, LANES), jnp.float32),
             pltpu.VMEM((rows * SUB, LANES), jnp.float32),
         ],
         limit,

time: 43.7 us -> 43 us (0.984)
  waiting for transfers between devices: 8.61 us -> 8.05 us
    ppermute x9, waiting for transfers between devices: 7.29 us -> 6.41 us  [exchanged(): lax.ppermute(parts[d], 'tm', [(i, i ^ d) for i in range(count)])]
where the time goes in v5:
time: 43 us; the launch traced here: 42.9 us
  starting transfers between devices  21 us (49%)
  Pallas kernels  13.1 us (30%)
  waiting for transfers between devices  8.05 us (19%)
  between operations  0.73 us (2%)
    ppermute x9, starting transfers between devices, exchanged(): lax.ppermute(parts[d], 'tm', [(i, i ^ d) for i in range(count)])  14.6 us
    pallas_call x10, Pallas kernels, run(): pl.pallas_call(body, out_shape=[jax.ShapeDtypeStruct(s, jnp.float32) for...  13.1 us
    ppermute x9, waiting for transfers between devices, exchanged(): lax.ppermute(parts[d], 'tm', [(i, i ^ d) for i in range(count)])  6.41 us
    ppermute x2, starting transfers between devices, turned(): lax.ppermute(down, 'sx', [(i, (i + 1) % n) for i in range(n)])  3.23 us
    ppermute x2, starting transfers between devices, turned(): lax.ppermute(up, 'sx', [((i + 1) % n, i) for i in range(n)])  2.72 us
    ppermute x1, waiting for transfers between devices, local(): strip = lax.ppermute(strip, 'sy', [(0, 1), (1, 0)])  1.3 us
  transfers between devices with their start and end apart: 14, of which 5 were waited for; matrix products, arithmetic and copies ran while one was open for 0% of the time, Pallas kernels for 14%

profile of v5, /device:TPU:0, one launch (start us, length us, event | category | flops | bytes accessed | tf_op | source)
XLA Modules:
  0.0 42.9 jit_solution(2190121919023372500)
XLA Ops:
  0.6 1.3 %shard_map.94 = (f32[704,256]{1,0:T(8,128)S(1)}, f32[704,128]{1,0:T(8,128)S(1)}) custom-call(f32[128,256]{1,0:T(8,128)} %bitcast.6, f32[128,256]{1,0:T(8,128)} %bitcast.7, f32[64,256]{1,0:T(8,128)} %refs_2_.1, f32[64,256]{1,0:T(8,128)} %refs_3_.1, f32[64,256]{1,0:T(8,128)} %refs_4_.1, f32[128,256]{1,0:T(8,128)} %bitcast.8, f32[128,256]{1,0:T(8,128)} %bitcast.9), custom_call_target="tpu_custom_call" | custom-call | tf_op jit(solution)/shard_map/pallas_call | solution.py:31
  1.9 0.5 %collective-permute-start = (f32[704,128]{1,0:T(8,128)S(1)}, f32[704,128]{1,0:T(8,128)S(1)}, u32[]{:S(2)}, u32[]{:S(2)}) collective-permute-start(f32[704,128]{1,0:T(8,128)S(1)} %get-tuple-element.40), channel_id=1, source_target_pairs={{0,1},{1,0},{2,3},{3,2},{4,5},{5,4},{6,7},{7,6},{8,9},{9,8},{10,11... | collective-permute-start | bytes 1081352 | tf_op jit(solution)/shard_map/ppermute | solution.py:675
  2.5 1.3 %collective-permute-done.strip_ref = f32[704,128]{1,0:T(8,128)S(1)} collective-permute-done((f32[704,128]{1,0:T(8,128)S(1)}, f32[704,128]{1,0:T(8,128)S(1)}, u32[]{:S(2)}, u32[]{:S(2)}) %collective-permute-start) | collective-permute-done | bytes 360480 | tf_op jit(solution)/shard_map/ppermute | solution.py:675
  3.8 0.2 shard_map.95
  4.0 5.0 %collective-permute-start.3 = (f32[128,128]{1,0:T(8,128)S(1)}, f32[128,128]{1,0:T(8,128)S(1)}, u32[]{:S(2)}, u32[]{:S(2)}) collective-permute-start(f32[128,128]{1,0:T(8,128)S(1)} %get-tuple-element.44), channel_id=1, source_target_pairs={{0,24},{8,16},{16,8},{24,0},{1,25},{9,17},{17,9},{25,1},{2,26},{10... | collective-permute-start | bytes 196616 | tf_op jit(solution)/shard_map/ppermute | solution.py:659
  9.0 0.0 collective-permute-start.4
  9.0 0.6 %collective-permute-start.5 = (f32[128,128]{1,0:T(8,128)S(1)}, f32[128,128]{1,0:T(8,128)S(1)}, u32[]{:S(2)}, u32[]{:S(2)}) collective-permute-start(f32[128,128]{1,0:T(8,128)S(1)} %get-tuple-element.46), channel_id=1, source_target_pairs={{0,8},{8,0},{16,24},{24,16},{1,9},{9,1},{17,25},{25,17},{2,10},{10... | collective-permute-start | bytes 196616 | tf_op jit(solution)/shard_map/ppermute | solution.py:659
  9.7 0.8 %shard_map.96 = (f32[144,128]{1,0:T(8,128)S(1)}, f32[144,128]{1,0:T(8,128)S(1)}, f32[144,128]{1,0:T(8,128)S(1)}, f32[144,128]{1,0:T(8,128)S(1)}, f32[448,128]{1,...) custom-call(f32[704,256]{1,0:T(8,128)S(1)} %get-tuple-element.39.tile_ref, ...), custom_call_target="tpu_custom_call" | custom-call | tf_op jit(solution)/shard_map/pallas_call | solution.py:31
  10.5 1.7 %collective-permute-start.1 = (f32[120,128]{1,0:T(8,128)S(1)}, f32[120,128]{1,0:T(8,128)S(1)}, u32[]{:S(2)}, u32[]{:S(2)}) collective-permute-start(f32[120,128]{1,0:T(8,128)S(1)} %get-tuple-element.42), channel_id=1, source_target_pairs={{0,2},{2,4},{4,6},{6,0},{1,3},{3,5},{5,7},{7,1},{8,10},{10,12},{12... | collective-permute-start | bytes 184328 | tf_op jit(solution)/shard_map/ppermute | solution.py:665
  12.2 1.3 %collective-permute-start.2 = (f32[120,128]{1,0:T(8,128)S(1)}, f32[120,128]{1,0:T(8,128)S(1)}, u32[]{:S(2)}, u32[]{:S(2)}) collective-permute-start(f32[120,128]{1,0:T(8,128)S(1)} %get-tuple-element.43), channel_id=1, source_target_pairs={{2,0},{4,2},{6,4},{0,6},{3,1},{5,3},{7,5},{1,7},{10,8},{12,10},{14... | collective-permute-start | bytes 184328 | tf_op jit(solution)/shard_map/ppermute | solution.py:666
  13.4 0.0 collective-permute-done.3.refs_1_
  13.4 1.5 %collective-permute-done.4.refs_2_ = f32[128,128]{1,0:T(8,128)S(1)} collective-permute-done((f32[128,128]{1,0:T(8,128)S(1)}, f32[128,128]{1,0:T(8,128)S(1)}, u32[]{:S(2)}, u32[]{:S(2)}) %collective-permute-start.4) | collective-permute-done | bytes 65568 | tf_op jit(solution)/shard_map/ppermute | solution.py:659
  14.9 0.0 collective-permute-done.5.refs_3_
  14.9 0.1 shard_map.97
  15.0 1.5 %collective-permute-start.9 = (f32[232,128]{1,0:T(8,128)S(1)}, f32[232,128]{1,0:T(8,128)S(1)}, u32[]{:S(2)}, u32[]{:S(2)}) collective-permute-start(f32[232,128]{1,0:T(8,128)S(1)} %get-tuple-element.60), channel_id=1, source_target_pairs={{0,2},{2,4},{4,6},{6,0},{1,3},{3,5},{5,7},{7,1},{8,10},{10,12},{12... | collective-permute-start | bytes 356360 | tf_op jit(solution)/shard_map/ppermute | solution.py:665
  16.6 1.4 %collective-permute-start.10 = (f32[232,128]{1,0:T(8,128)S(1)}, f32[232,128]{1,0:T(8,128)S(1)}, u32[]{:S(2)}, u32[]{:S(2)}) collective-permute-start(f32[232,128]{1,0:T(8,128)S(1)} %get-tuple-element.61), channel_id=1, source_target_pairs={{2,0},{4,2},{6,4},{0,6},{3,1},{5,3},{7,5},{1,7},{10,8},{12,10},{14... | collective-permute-start | bytes 356360 | tf_op jit(solution)/shard_map/ppermute | solution.py:666
  18.0 0.0 collective-permute-done.1.top_ref
  18.0 0.0 collective-permute-done.2.bot_ref
  18.0 0.3 shard_map.98
  18.3 1.2 %collective-permute-start.6 = (f32[144,128]{1,0:T(8,128)S(1)}, f32[144,128]{1,0:T(8,128)S(1)}, u32[]{:S(2)}, u32[]{:S(2)}) collective-permute-start(f32[144,128]{1,0:T(8,128)S(1)} %get-tuple-element.54), channel_id=1, source_target_pairs={{0,8},{8,0},{16,24},{24,16},{1,9},{9,1},{17,25},{25,17},{2,10},{10... | collective-permute-start | bytes 221192 | tf_op jit(solution)/shard_map/ppermute | solution.py:659
  19.4 1.9 %collective-permute-start.7 = (f32[144,128]{1,0:T(8,128)S(1)}, f32[144,128]{1,0:T(8,128)S(1)}, u32[]{:S(2)}, u32[]{:S(2)}) collective-permute-start(f32[144,128]{1,0:T(8,128)S(1)} %get-tuple-element.55), channel_id=1, source_target_pairs={{0,16},{8,24},{16,0},{24,8},{1,17},{9,25},{17,1},{25,9},{2,18},{10... | collective-permute-start | bytes 221192 | tf_op jit(solution)/shard_map/ppermute | solution.py:659
  21.4 1.3 %collective-permute-start.8 = (f32[144,128]{1,0:T(8,128)S(1)}, f32[144,128]{1,0:T(8,128)S(1)}, u32[]{:S(2)}, u32[]{:S(2)}) collective-permute-start(f32[144,128]{1,0:T(8,128)S(1)} %get-tuple-element.56), channel_id=1, source_target_pairs={{0,24},{8,16},{16,8},{24,0},{1,25},{9,17},{17,9},{25,1},{2,26},{10... | collective-permute-start | bytes 221192 | tf_op jit(solution)/shard_map/ppermute | solution.py:659
  22.7 0.3 shard_map.99
  23.0 0.0 collective-permute-done.9.top_ref
  23.0 0.3 collective-permute-done.10.bot_ref
  23.4 4.6 %shard_map.100 = (f32[8,1,768,128]{3,2,1,0:T(8,128)S(1)}, f32[8,1,512,128]{3,2,1,0:T(8,128)S(1)}, f32[640,128]{1,0:T(8,128)S(1)}, f32[896,128]{1,0:T(8,128)S(1)}) custom-call(f32[1,512,128]{2,1,0:T(8,128)S(1)} %get-tuple-element.48.after.mid, f32[232,128]{1,0:T(8,128)S(1)} %collective-permute-done.9.top_ref, f32[232,128]{1,0:T(8,128)S(1)} %collective-permute-done.10.bot_ref, ...), custom_call_target="tpu_custom_call" | custom-call | tf_op jit(solution)/shard_map/pallas_call | solution.py:31
  28.0 0.0 collective-permute-done.6.refs_1_
  28.0 0.0 collective-permute-done.7.refs_2_
  28.0 0.0 collective-permute-done.8.refs_3_
  28.1 2.1 %shard_map.101.lag = f32[1,640,128]{2,1,0:T(8,128)S(1)} custom-call(f32[144,128]{1,0:T(8,128)S(1)} %get-tuple-element.53.refs_0_, f32[144,128]{1,0:T(8,128)S(1)} %collective-permute-done.6.refs_1_, f32[144,128]{1,0:T(8,128)S(1)} %collective-permute-done.7.refs_2_, f32[144,128]{1,0:T(8,128)S(1)} %collective-permute-done.8.refs_3_, ...), custom_call_target="tpu_custom_call" | custom-call | tf_op jit(solution)/shard_map/pallas_call | solution.py:31
  30.2 2.4 %shard_map.102 = (f32[160,128]{1,0:T(8,128)S(1)}, f32[160,128]{1,0:T(8,128)S(1)}, f32[160,128]{1,0:T(8,128)S(1)}, f32[160,128]{1,0:T(8,128)S(1)}) custom-call(f32[1,640,128]{2,1,0:T(8,128)S(1)} %shard_map.101.lag, f32[8,1,768,128]{3,2,1,0:T(8,128)S(1)} %get-tuple-element.65.hist, f32[8,1,512,128]{3,2,1,0:T(8,128)S(1)} %get-tuple-element.66.slope, ...), custom_call_target="tpu_custom_call" | custom-call | tf_op jit(solution)/shard_map/pallas_call | solution.py:31
  32.6 2.2 %collective-permute-start.11 = (f32[160,128]{1,0:T(8,128)S(1)}, f32[160,128]{1,0:T(8,128)S(1)}, u32[]{:S(2)}, u32[]{:S(2)}) collective-permute-start(f32[160,128]{1,0:T(8,128)S(1)} %get-tuple-element.69), channel_id=1, source_target_pairs={{0,24},{8,16},{16,8},{24,0},{1,25},{9,17},{17,9},{25,1},{2,26},{10... | collective-permute-start | bytes 245768 | tf_op jit(solution)/shard_map/ppermute | solution.py:659
  34.9 0.0 collective-permute-start.12
  34.9 2.2 %collective-permute-start.13 = (f32[160,128]{1,0:T(8,128)S(1)}, f32[160,128]{1,0:T(8,128)S(1)}, u32[]{:S(2)}, u32[]{:S(2)}) collective-permute-start(f32[160,128]{1,0:T(8,128)S(1)} %get-tuple-element.71), channel_id=1, source_target_pairs={{0,8},{8,0},{16,24},{24,16},{1,9},{9,1},{17,25},{25,17},{2,10},{10... | collective-permute-start | bytes 245768 | tf_op jit(solution)/shard_map/ppermute | solution.py:659
  37.1 2.4 %collective-permute-done.11.refs_1_ = f32[160,128]{1,0:T(8,128)S(1)} collective-permute-done((f32[160,128]{1,0:T(8,128)S(1)}, f32[160,128]{1,0:T(8,128)S(1)}, u32[]{:S(2)}, u32[]{:S(2)}) %collective-permute-start.11) | collective-permute-done | bytes 81952 | tf_op jit(solution)/shard_map/ppermute | solution.py:659
  39.5 2.6 %collective-permute-done.12.refs_2_ = f32[160,128]{1,0:T(8,128)S(1)} collective-permute-done((f32[160,128]{1,0:T(8,128)S(1)}, f32[160,128]{1,0:T(8,128)S(1)}, u32[]{:S(2)}, u32[]{:S(2)}) %collective-permute-start.12) | collective-permute-done | bytes 81952 | tf_op jit(solution)/shard_map/ppermute | solution.py:659
  42.0 0.0 collective-permute-done.13.refs_3_
  42.0 0.9 %shard_map.103 = (f32[128,256]{1,0:T(8,128)}, f32[128,256]{1,0:T(8,128)}, f32[64,256]{1,0:T(8,128)}) custom-call(f32[160,128]{1,0:T(8,128)S(1)} %get-tuple-element.68.refs_0_, f32[160,128]{1,0:T(8,128)S(1)} %collective-permute-done.11.refs_1_, f32[160,128]{1,0:T(8,128)S(1)} %collective-permute-done.12.refs_2_, f32[160,128]{1,0:T(8,128)S(1)} %collective-permute-done.13.refs_3_), custom_call_target="tpu_custom_call" | custom-call | tf_op jit(solution)/shard_map/pallas_call | solution.py:31
Async XLA Ops:
  1.9 1.8 %collective-permute-start = (f32[704,128]{1,0:T(8,128)S(1)}, f32[704,128]{1,0:T(8,128)S(1)}, u32[]{:S(2)}, u32[]{:S(2)}) collective-permute-start(f32[704,128]{1,0:T(8,128)S(1)} %get-tuple-element.40), channel_id=1, source_target_pairs={{0,1},{1,0},{2,3},{3,2},{4,5},{5,4},{6,7},{7,6},{8,9},{9,8},{10,11... | collective-permute-start | bytes 1081352 | tf_op jit(solution)/shard_map/ppermute | solution.py:675
  4.0 9.5 %collective-permute-start.3 = (f32[128,128]{1,0:T(8,128)S(1)}, f32[128,128]{1,0:T(8,128)S(1)}, u32[]{:S(2)}, u32[]{:S(2)}) collective-permute-start(f32[128,128]{1,0:T(8,128)S(1)} %get-tuple-element.44), channel_id=1, source_target_pairs={{0,24},{8,16},{16,8},{24,0},{1,25},{9,17},{17,9},{25,1},{2,26},{10... | collective-permute-start | bytes 196616 | tf_op jit(solution)/shard_map/ppermute | solution.py:659
  9.0 5.9 %collective-permute-start.4 = (f32[128,128]{1,0:T(8,128)S(1)}, f32[128,128]{1,0:T(8,128)S(1)}, u32[]{:S(2)}, u32[]{:S(2)}) collective-permute-start(f32[128,128]{1,0:T(8,128)S(1)} %get-tuple-element.45), channel_id=1, source_target_pairs={{0,16},{8,24},{16,0},{24,8},{1,17},{9,25},{17,1},{25,9},{2,18},{10... | collective-permute-start | bytes 196616 | tf_op jit(solution)/shard_map/ppermute | solution.py:659
  9.0 5.9 %collective-permute-start.5 = (f32[128,128]{1,0:T(8,128)S(1)}, f32[128,128]{1,0:T(8,128)S(1)}, u32[]{:S(2)}, u32[]{:S(2)}) collective-permute-start(f32[128,128]{1,0:T(8,128)S(1)} %get-tuple-element.46), channel_id=1, source_target_pairs={{0,8},{8,0},{16,24},{24,16},{1,9},{9,1},{17,25},{25,17},{2,10},{10... | collective-permute-start | bytes 196616 | tf_op jit(solution)/shard_map/ppermute | solution.py:659
  10.5 7.5 %collective-permute-start.1 = (f32[120,128]{1,0:T(8,128)S(1)}, f32[120,128]{1,0:T(8,128)S(1)}, u32[]{:S(2)}, u32[]{:S(2)}) collective-permute-start(f32[120,128]{1,0:T(8,128)S(1)} %get-tuple-element.42), channel_id=1, source_target_pairs={{0,2},{2,4},{4,6},{6,0},{1,3},{3,5},{5,7},{7,1},{8,10},{10,12},{12... | collective-permute-start | bytes 184328 | tf_op jit(solution)/shard_map/ppermute | solution.py:665
  12.2 5.8 %collective-permute-start.2 = (f32[120,128]{1,0:T(8,128)S(1)}, f32[120,128]{1,0:T(8,128)S(1)}, u32[]{:S(2)}, u32[]{:S(2)}) collective-permute-start(f32[120,128]{1,0:T(8,128)S(1)} %get-tuple-element.43), channel_id=1, source_target_pairs={{2,0},{4,2},{6,4},{0,6},{3,1},{5,3},{7,5},{1,7},{10,8},{12,10},{14... | collective-permute-start | bytes 184328 | tf_op jit(solution)/shard_map/ppermute | solution.py:666
  15.0 8.0 %collective-permute-start.9 = (f32[232,128]{1,0:T(8,128)S(1)}, f32[232,128]{1,0:T(8,128)S(1)}, u32[]{:S(2)}, u32[]{:S(2)}) collective-permute-start(f32[232,128]{1,0:T(8,128)S(1)} %get-tuple-element.60), channel_id=1, source_target_pairs={{0,2},{2,4},{4,6},{6,0},{1,3},{3,5},{5,7},{7,1},{8,10},{10,12},{12... | collective-permute-start | bytes 356360 | tf_op jit(solution)/shard_map/ppermute | solution.py:665
  16.6 6.8 %collective-permute-start.10 = (f32[232,128]{1,0:T(8,128)S(1)}, f32[232,128]{1,0:T(8,128)S(1)}, u32[]{:S(2)}, u32[]{:S(2)}) collective-permute-start(f32[232,128]{1,0:T(8,128)S(1)} %get-tuple-element.61), channel_id=1, source_target_pairs={{2,0},{4,2},{6,4},{0,6},{3,1},{5,3},{7,5},{1,7},{10,8},{12,10},{14... | collective-permute-start | bytes 356360 | tf_op jit(solution)/shard_map/ppermute | solution.py:666
  18.3 9.7 %collective-permute-start.6 = (f32[144,128]{1,0:T(8,128)S(1)}, f32[144,128]{1,0:T(8,128)S(1)}, u32[]{:S(2)}, u32[]{:S(2)}) collective-permute-start(f32[144,128]{1,0:T(8,128)S(1)} %get-tuple-element.54), channel_id=1, source_target_pairs={{0,8},{8,0},{16,24},{24,16},{1,9},{9,1},{17,25},{25,17},{2,10},{10... | collective-permute-start | bytes 221192 | tf_op jit(solution)/shard_map/ppermute | solution.py:659
  19.4 8.6 %collective-permute-start.7 = (f32[144,128]{1,0:T(8,128)S(1)}, f32[144,128]{1,0:T(8,128)S(1)}, u32[]{:S(2)}, u32[]{:S(2)}) collective-permute-start(f32[144,128]{1,0:T(8,128)S(1)} %get-tuple-element.55), channel_id=1, source_target_pairs={{0,16},{8,24},{16,0},{24,8},{1,17},{9,25},{17,1},{25,9},{2,18},{10... | collective-permute-start | bytes 221192 | tf_op jit(solution)/shard_map/ppermute | solution.py:659
  21.4 6.7 %collective-permute-start.8 = (f32[144,128]{1,0:T(8,128)S(1)}, f32[144,128]{1,0:T(8,128)S(1)}, u32[]{:S(2)}, u32[]{:S(2)}) collective-permute-start(f32[144,128]{1,0:T(8,128)S(1)} %get-tuple-element.56), channel_id=1, source_target_pairs={{0,24},{8,16},{16,8},{24,0},{1,25},{9,17},{17,9},{25,1},{2,26},{10... | collective-permute-start | bytes 221192 | tf_op jit(solution)/shard_map/ppermute | solution.py:659
  32.6 6.8 %collective-permute-start.11 = (f32[160,128]{1,0:T(8,128)S(1)}, f32[160,128]{1,0:T(8,128)S(1)}, u32[]{:S(2)}, u32[]{:S(2)}) collective-permute-start(f32[160,128]{1,0:T(8,128)S(1)} %get-tuple-element.69), channel_id=1, source_target_pairs={{0,24},{8,16},{16,8},{24,0},{1,25},{9,17},{17,9},{25,1},{2,26},{10... | collective-permute-start | bytes 245768 | tf_op jit(solution)/shard_map/ppermute | solution.py:659
  34.9 7.2 %collective-permute-start.12 = (f32[160,128]{1,0:T(8,128)S(1)}, f32[160,128]{1,0:T(8,128)S(1)}, u32[]{:S(2)}, u32[]{:S(2)}) collective-permute-start(f32[160,128]{1,0:T(8,128)S(1)} %get-tuple-element.70), channel_id=1, source_target_pairs={{0,16},{8,24},{16,0},{24,8},{1,17},{9,25},{17,1},{25,9},{2,18},{10... | collective-permute-start | bytes 245768 | tf_op jit(solution)/shard_map/ppermute | solution.py:659
  34.9 7.2 %collective-permute-start.13 = (f32[160,128]{1,0:T(8,128)S(1)}, f32[160,128]{1,0:T(8,128)S(1)}, u32[]{:S(2)}, u32[]{:S(2)}) collective-permute-start(f32[160,128]{1,0:T(8,128)S(1)} %get-tuple-element.71), channel_id=1, source_target_pairs={{0,8},{8,0},{16,24},{24,16},{1,9},{9,1},{17,25},{25,17},{2,10},{10... | collective-permute-start | bytes 245768 | tf_op jit(solution)/shard_map/ppermute | solution.py:659

commit v6 on v5

--- a/solution.py
+++ b/solution.py
@@ -41,9 +41,35 @@
     return run
 
 
-def fetch_body(*refs):
-    fields, (tile_ref, strip_ref, sems) = refs[:7], refs[7:]
-    cols = tile_ref.shape[1]
+def copied(copies):
+    for copy in copies:
+        copy.start()
+    for copy in copies:
+        copy.wait()
+
+
+def strip_body(*refs):
+    fields, (strip_ref, sems) = refs[:7], refs[7:]
+    cols = fields[0].shape[1]
+    start = pl.multiple_of(
+        jnp.where(lax.axis_index("sy") == 0, cols - LANES, 0).astype(jnp.int32), LANES
+    )
+    copies = []
+    at = 0
+    for i, ref in enumerate(fields):
+        rows = ref.shape[0]
+        copies.append(
+            pltpu.make_async_copy(
+                ref.at[:, pl.ds(start, LANES)], strip_ref.at[at : at + rows, :], sems.at[i]
+            )
+        )
+        at += rows
+    copied(copies)
+
+
+def tile_body(*refs):
+    fields, (after, tile_ref, sems) = refs[:7], refs[7:]
+    del after
     copies = []
     at = 0
     for i, ref in enumerate(fields):
@@ -52,42 +78,53 @@
             pltpu.make_async_copy(ref, tile_ref.at[at : at + rows, :], sems.at[i])
         )
         at += rows
-    for copy in copies:
-        copy.start()
-    for copy in copies:
-        copy.wait()
-    strip_ref[...] = jnp.where(
-        lax.axis_index("sy") == 0, tile_ref[:, cols - LANES :], tile_ref[:, :LANES]
-    )
+    copied(copies)
 
 
 EARLY = (HALO,) * 2
 LATE = (HALO,) * 3 + (SUB,) * 2
 
 
+def even_row():
+    return lax.axis_index("sx") % 2 == 0
+
+
+def send_rows(refs, at, down, up):
+    refs[0][at, :] = jnp.where(even_row(), down, up)
+    refs[1][at, :] = jnp.where(even_row(), up, down)
+
+
+def received(refs, lo, hi):
+    s_at = lax.axis_index("sx")
+    first, second = refs[0][lo:hi, :], refs[1][lo:hi, :]
+    top = jnp.where(even_row(), second, first)
+    bot = jnp.where(even_row(), first, second)
+    return masked(s_at > 0, top), masked(s_at < lax.axis_size("sx") - 1, bot)
+
+
 def edge_rows(refs, coef_ref, first, sizes, at):
-    down_ref, up_ref = refs
     rows = coef_ref.shape[0] // 7
     for f, size in enumerate(sizes, first):
-        down_ref[at : at + size, :] = coef_ref[(f + 1) * rows - size : (f + 1) * rows, :]
-        up_ref[at : at + size, :] = coef_ref[f * rows : f * rows + size, :]
+        send_rows(
+            refs,
+            slice(at, at + size),
+            coef_ref[(f + 1) * rows - size : (f + 1) * rows, :],
+            coef_ref[f * rows : f * rows + size, :],
+        )
         at += size
     return at
 
 
 def joined_rows(flat, coef_ref, refs, first, sizes, at):
-    s_at = lax.axis_index("sx")
-    has_top = s_at > 0
-    has_bot = s_at < lax.axis_size("sx") - 1
-    top_ref, bot_ref = refs
     rows = coef_ref.shape[0] // 7
     end = HALO + rows
     fields = []
     for i, size in enumerate(sizes):
         f = first + i
-        flat[i, HALO - size : HALO, :] = masked(has_top, top_ref[at : at + size, :])
+        top, bot = received(refs, at, at + size)
+        flat[i, HALO - size : HALO, :] = top
         flat[i, HALO:end, :] = coef_ref[f * rows : (f + 1) * rows, :]
-        flat[i, end : end + size, :] = masked(has_bot, bot_ref[at : at + size, :])
+        flat[i, end : end + size, :] = bot
         fields.append(flat[i])
         at += size
     return fields
@@ -162,46 +199,49 @@
         )
     at = edge_rows((down_ref, up_ref), coef_ref, 0, EARLY, 0)
     lane = lax.broadcasted_iota(jnp.int32, (SUB, LANES), 1)
-    for ref, low in ((down_ref, rows - HALO_W), (up_ref, 0)):
-        put, sides = at, None
-        for sp in range(2):
-            here = (2 + sp) * rows + low
-            for i in range(cols // LANES):
-                ref[put : put + HALO_W, :] = tile_ref[
-                    here : here + HALO_W, i * LANES : (i + 1) * LANES
-                ]
-                put += HALO_W
-            for i in range(HALO_W // SUB):
-                strip = strip_ref[here + i * SUB : here + (i + 1) * SUB, :]
-                n = sp * (HALO_W // SUB) + i
+    sides = [None, None]
+    for sp in range(2):
+        lo = (2 + sp) * rows
+        starts = (lo + rows - HALO_W, lo)
+        for i in range(cols // LANES):
+            send_rows(
+                (down_ref, up_ref),
+                slice(at, at + HALO_W),
+                *[tile_ref[p : p + HALO_W, i * LANES : (i + 1) * LANES] for p in starts],
+            )
+            at += HALO_W
+        for i in range(HALO_W // SUB):
+            n = sp * (HALO_W // SUB) + i
+            for side, p in enumerate(starts):
+                strip = strip_ref[p + i * SUB : p + (i + 1) * SUB, :]
                 strip = jnp.where(
                     lax.axis_index("sy") == 0,
                     pltpu.roll(strip, n * SIDE, 1),
                     pltpu.roll(strip, (n + 1) * SIDE % LANES, 1),
                 )
-                sides = strip if n == 0 else jnp.where(lane >= n * SIDE, strip, sides)
-        ref[put : put + SUB, :] = sides
+                sides[side] = (
+                    strip if n == 0 else jnp.where(lane >= n * SIDE, strip, sides[side])
+                )
+    send_rows((down_ref, up_ref), slice(at, at + SUB), *sides)
 
 
 def adjoint_window_body(count, rows, cols, top_ref, bot_ref, after, *refs):
     del after
     outs, ext = refs[count : 2 * count], refs[2 * count]
     me = lax.axis_index("tm")
-    s_at = lax.axis_index("sx")
     wide = cols // count
     for sp in range(2):
         base = sp * 2 * HALO_W
         at = sum(EARLY) + sp * (cols // LANES) * HALO_W
         side_at = sum(EARLY) + 2 * (cols // LANES) * HALO_W
-        for ref, start, flag in (
-            (top_ref, base, s_at > 0),
-            (bot_ref, base + HALO_W, s_at < lax.axis_size("sx") - 1),
-        ):
-            parts = [
-                masked(flag, ref[at + i * HALO_W : at + (i + 1) * HALO_W, :])
-                for i in range(cols // LANES)
-            ]
-            sides = masked(flag, ref[side_at : side_at + SUB, :])
+        pieces = [
+            received((top_ref, bot_ref), at + i * HALO_W, at + (i + 1) * HALO_W)
+            for i in range(cols // LANES)
+        ]
+        both = received((top_ref, bot_ref), side_at, side_at + SUB)
+        for side, start in enumerate((base, base + HALO_W)):
+            parts = [piece[side] for piece in pieces]
+            sides = both[side]
             strips = []
             for i in range(HALO_W // SUB):
                 n = sp * (HALO_W // SUB) + i
@@ -242,8 +282,12 @@
         def _(d=d, slab=slab):
             for sp in range(2):
                 at = pl.multiple_of((slab * 2 + sp) * HALO, SUB)
-                down_ref[pl.ds(at, HALO), :] = cens[d][(sp + 1) * rows - HALO : (sp + 1) * rows, :]
-                up_ref[pl.ds(at, HALO), :] = cens[d][sp * rows : sp * rows + HALO, :]
+                send_rows(
+                    (down_ref, up_ref),
+                    pl.ds(at, HALO),
+                    cens[d][(sp + 1) * rows - HALO : (sp + 1) * rows, :],
+                    cens[d][sp * rows : sp * rows + HALO, :],
+                )
 
 
 def blocks(lo, hi):
@@ -319,9 +363,6 @@
 
 
 def load(groups, refs, tile_rows, mid, top_ref, bot_ref):
-    s_at = lax.axis_index("sx")
-    has_top = s_at > 0
-    has_bot = s_at < lax.axis_size("sx") - 1
     end = HALO + tile_rows
     for g in range(groups):
         for ref in refs:
@@ -330,8 +371,8 @@
             for sp in range(2):
                 slab = min(g * PER_GROUP + j, groups * PER_GROUP - 2)
                 at = (slab * 2 + sp) * HALO
-                for halo, start, flag in ((top_ref, 0, has_top), (bot_ref, end, has_bot)):
-                    value = masked(flag, halo[at : at + HALO, :])
+                values = received((top_ref, bot_ref), at, at + HALO)
+                for value, start in zip(values, (0, end)):
                     for ref in refs:
                         first = start * SUB + sp * PER_GROUP + j
                         ref[g, pl.ds(first, HALO, stride=SUB), :] = value
@@ -659,19 +700,19 @@
             lax.ppermute(parts[d], "tm", [(i, i ^ d) for i in range(count)]) for d in order
         ]
 
-    def turned(down, up):
+    def turned(first, second):
         n = lax.axis_size("sx")
         return (
-            lax.ppermute(down, "sx", [(i, (i + 1) % n) for i in range(n)]),
-            lax.ppermute(up, "sx", [((i + 1) % n, i) for i in range(n)]),
+            lax.ppermute(first, "sx", [(i, i ^ 1) for i in range(n)]),
+            lax.ppermute(second, "sx", [(i, (i + (1 if i % 2 else n - 1)) % n) for i in range(n)]),
         )
 
-    tile, strip = call(
-        fetch_body,
-        [(11 * rows, cols), (11 * rows, LANES)],
-        [pltpu.SemaphoreType.DMA((7,))],
-        inputs=[HBM_SPEC] * 7,
-    )(*[pltpu.with_memory_space_constraint(f, pltpu.HBM) for f in fields])
+    fields = [pltpu.with_memory_space_constraint(f, pltpu.HBM) for f in fields]
+    sems = [pltpu.SemaphoreType.DMA((7,))]
+    (strip,) = call(strip_body, [(11 * rows, LANES)], sems, inputs=[HBM_SPEC] * 7)(*fields)
+    (tile,) = call(tile_body, [(11 * rows, cols)], sems, inputs=[HBM_SPEC] * 7 + [VMEM_SPEC])(
+        *fields, strip
+    )
     strip = lax.ppermute(strip, "sy", [(0, 1), (1, 0)])
     edge = (sum(EARLY) + 2 * (cols // LANES) * HALO_W + SUB, LANES)
     windows = call(

time: 43 us -> 42.7 us (level)
  waiting for transfers between devices: 8.05 us -> 6.31 us
  Pallas kernels: 13.1 us -> 14.1 us
    ppermute x1, waiting for transfers between devices: 1.3 us -> 0.04 us  [local(): strip = lax.ppermute(strip, 'sy', [(0, 1), (1, 0)])]
    pallas_call x10 -> x11, Pallas kernels: 13.1 us -> 14.1 us  [run(): pl.pallas_call(body, out_shape=[jax.ShapeDtypeStruct(s, jnp.float32) for...]
  transfers between devices with their start and end apart: 14 -> 14, of which waited for: 5 -> 5; matrix products, arithmetic and copies ran while one was open for 0% -> 0% of each run, Pallas kernels for 14% -> 17%
where the time goes in v6:
time: 42.7 us; the launch traced here: 42.5 us
  starting transfers between devices  21.3 us (50%)
  Pallas kernels  14.1 us (33%)
  waiting for transfers between devices  6.31 us (15%)
  between operations  0.73 us (2%)
    ppermute x9, starting transfers between devices, exchanged(): lax.ppermute(parts[d], 'tm', [(i, i ^ d) for i in range(count)])  14.6 us
    pallas_call x11, Pallas kernels, run(): pl.pallas_call(body, out_shape=[jax.ShapeDtypeStruct(s, jnp.float32) for...  14.1 us
    ppermute x9, waiting for transfers between devices, exchanged(): lax.ppermute(parts[d], 'tm', [(i, i ^ d) for i in range(count)])  5.99 us
    ppermute x2, starting transfers between devices, turned(): lax.ppermute(first, 'sx', [(i, i ^ 1) for i in range(n)])  3.26 us
    ppermute x2, starting transfers between devices, turned(): lax.ppermute(second, 'sx', [(i, (i + (1 if i % 2 else n - 1)) % n) for i...  2.98 us
  transfers between devices with their start and end apart: 14, of which 5 were waited for; matrix products, arithmetic and copies ran while one was open for 0% of the time, Pallas kernels for 17%

profile of v6, /device:TPU:0, one launch (start us, length us, event | category | flops | bytes accessed | tf_op | source)
XLA Modules:
  0.0 42.5 jit_solution(1186622878243769147)
XLA Ops:
  0.6 1.1 %shard_map.94.refs_7_ = f32[704,128]{1,0:T(8,128)S(1)} custom-call(f32[128,256]{1,0:T(8,128)} %bitcast.6, f32[128,256]{1,0:T(8,128)} %bitcast.8, f32[64,256]{1,0:T(8,128)} %refs_2_.3, f32[64,256]{1,0:T(8,128)} %refs_3_.3, f32[64,256]{1,0:T(8,128)} %refs_4_.3, f32[128,256]{1,0:T(8,128)} %bitcast.10, f32[128,256]{1,0:T(8,128)} %bitcast.12), custom_call_target="tpu_custom_call" | custom-call | tf_op jit(solution)/shard_map/pallas_call | solution.py:31
  1.7 0.5 %collective-permute-start = (f32[704,128]{1,0:T(8,128)S(1)}, f32[704,128]{1,0:T(8,128)S(1)}, u32[]{:S(2)}, u32[]{:S(2)}) collective-permute-start(f32[704,128]{1,0:T(8,128)S(1)} %shard_map.94.refs_7_), channel_id=1, source_target_pairs={{0,1},{1,0},{2,3},{3,2},{4,5},{5,4},{6,7},{7,6},{8,9},{9,8},{10,11... | collective-permute-start | bytes 1081352 | tf_op jit(solution)/shard_map/ppermute | solution.py:716
  2.2 1.3 %shard_map.95.tile_ref = f32[704,256]{1,0:T(8,128)S(1)} custom-call(f32[128,256]{1,0:T(8,128)} %bitcast.7, f32[128,256]{1,0:T(8,128)} %bitcast.9, f32[64,256]{1,0:T(8,128)} %refs_2_.3, f32[64,256]{1,0:T(8,128)} %refs_3_.3, f32[64,256]{1,0:T(8,128)} %refs_4_.3, f32[128,256]{1,0:T(8,128)} %bitcast.11, f32[128,256]{1,0:T(8,128)} %bitcast.13, ...), custom_call_target="tpu_custom_call" | custom-call | tf_op jit(solution)/shard_map/pallas_call | solution.py:31
  3.5 0.0 collective-permute-done.strip_ref
  3.5 0.2 shard_map.96
  3.7 5.0 %collective-permute-start.3 = (f32[128,128]{1,0:T(8,128)S(1)}, f32[128,128]{1,0:T(8,128)S(1)}, u32[]{:S(2)}, u32[]{:S(2)}) collective-permute-start(f32[128,128]{1,0:T(8,128)S(1)} %get-tuple-element.40), channel_id=1, source_target_pairs={{0,24},{8,16},{16,8},{24,0},{1,25},{9,17},{17,9},{25,1},{2,26},{10... | collective-permute-start | bytes 196616 | tf_op jit(solution)/shard_map/ppermute | solution.py:700
  8.8 0.0 collective-permute-start.4
  8.8 0.6 %collective-permute-start.5 = (f32[128,128]{1,0:T(8,128)S(1)}, f32[128,128]{1,0:T(8,128)S(1)}, u32[]{:S(2)}, u32[]{:S(2)}) collective-permute-start(f32[128,128]{1,0:T(8,128)S(1)} %get-tuple-element.42), channel_id=1, source_target_pairs={{0,8},{8,0},{16,24},{24,16},{1,9},{9,1},{17,25},{25,17},{2,10},{10... | collective-permute-start | bytes 196616 | tf_op jit(solution)/shard_map/ppermute | solution.py:700
  9.4 0.8 %shard_map.97 = (f32[144,128]{1,0:T(8,128)S(1)}, f32[144,128]{1,0:T(8,128)S(1)}, f32[144,128]{1,0:T(8,128)S(1)}, f32[144,128]{1,0:T(8,128)S(1)}, f32[448,128]{1,...) custom-call(f32[704,256]{1,0:T(8,128)S(1)} %shard_map.95.tile_ref, ...), custom_call_target="tpu_custom_call" | custom-call | tf_op jit(solution)/shard_map/pallas_call | solution.py:31
  10.2 1.7 %collective-permute-start.1 = (f32[120,128]{1,0:T(8,128)S(1)}, f32[120,128]{1,0:T(8,128)S(1)}, u32[]{:S(2)}, u32[]{:S(2)}) collective-permute-start(f32[120,128]{1,0:T(8,128)S(1)} %get-tuple-element.38), channel_id=1, source_target_pairs={{0,2},{2,0},{4,6},{6,4},{1,3},{3,1},{5,7},{7,5},{8,10},{10,8},{12,... | collective-permute-start | bytes 184328 | tf_op jit(solution)/shard_map/ppermute | solution.py:706
  11.9 1.5 %collective-permute-start.2 = (f32[120,128]{1,0:T(8,128)S(1)}, f32[120,128]{1,0:T(8,128)S(1)}, u32[]{:S(2)}, u32[]{:S(2)}) collective-permute-start(f32[120,128]{1,0:T(8,128)S(1)} %get-tuple-element.39), channel_id=1, source_target_pairs={{0,6},{2,4},{4,2},{6,0},{1,7},{3,5},{5,3},{7,1},{8,14},{10,12},{12... | collective-permute-start | bytes 184328 | tf_op jit(solution)/shard_map/ppermute | solution.py:707
  13.4 0.0 collective-permute-done.3.refs_1_
  13.4 1.3 %collective-permute-done.4.refs_2_ = f32[128,128]{1,0:T(8,128)S(1)} collective-permute-done((f32[128,128]{1,0:T(8,128)S(1)}, f32[128,128]{1,0:T(8,128)S(1)}, u32[]{:S(2)}, u32[]{:S(2)}) %collective-permute-start.4) | collective-permute-done | bytes 65568 | tf_op jit(solution)/shard_map/ppermute | solution.py:700
  14.7 0.0 collective-permute-done.5.refs_3_
  14.7 0.1 shard_map.98
  14.8 1.6 %collective-permute-start.9 = (f32[232,128]{1,0:T(8,128)S(1)}, f32[232,128]{1,0:T(8,128)S(1)}, u32[]{:S(2)}, u32[]{:S(2)}) collective-permute-start(f32[232,128]{1,0:T(8,128)S(1)} %get-tuple-element.56), channel_id=1, source_target_pairs={{0,2},{2,0},{4,6},{6,4},{1,3},{3,1},{5,7},{7,5},{8,10},{10,8},{12,... | collective-permute-start | bytes 356360 | tf_op jit(solution)/shard_map/ppermute | solution.py:706
  16.3 1.5 %collective-permute-start.10 = (f32[232,128]{1,0:T(8,128)S(1)}, f32[232,128]{1,0:T(8,128)S(1)}, u32[]{:S(2)}, u32[]{:S(2)}) collective-permute-start(f32[232,128]{1,0:T(8,128)S(1)} %get-tuple-element.57), channel_id=1, source_target_pairs={{0,6},{2,4},{4,2},{6,0},{1,7},{3,5},{5,3},{7,1},{8,14},{10,12},{12... | collective-permute-start | bytes 356360 | tf_op jit(solution)/shard_map/ppermute | solution.py:707
  17.8 0.0 collective-permute-done.1.top_ref
  17.8 0.0 collective-permute-done.2.bot_ref
  17.8 0.3 shard_map.99
  18.1 1.2 %collective-permute-start.6 = (f32[144,128]{1,0:T(8,128)S(1)}, f32[144,128]{1,0:T(8,128)S(1)}, u32[]{:S(2)}, u32[]{:S(2)}) collective-permute-start(f32[144,128]{1,0:T(8,128)S(1)} %get-tuple-element.50), channel_id=1, source_target_pairs={{0,8},{8,0},{16,24},{24,16},{1,9},{9,1},{17,25},{25,17},{2,10},{10... | collective-permute-start | bytes 221192 | tf_op jit(solution)/shard_map/ppermute | solution.py:700
  19.3 2.7 %collective-permute-start.7 = (f32[144,128]{1,0:T(8,128)S(1)}, f32[144,128]{1,0:T(8,128)S(1)}, u32[]{:S(2)}, u32[]{:S(2)}) collective-permute-start(f32[144,128]{1,0:T(8,128)S(1)} %get-tuple-element.51), channel_id=1, source_target_pairs={{0,16},{8,24},{16,0},{24,8},{1,17},{9,25},{17,1},{25,9},{2,18},{10... | collective-permute-start | bytes 221192 | tf_op jit(solution)/shard_map/ppermute | solution.py:700
  22.0 0.6 %collective-permute-start.8 = (f32[144,128]{1,0:T(8,128)S(1)}, f32[144,128]{1,0:T(8,128)S(1)}, u32[]{:S(2)}, u32[]{:S(2)}) collective-permute-start(f32[144,128]{1,0:T(8,128)S(1)} %get-tuple-element.52), channel_id=1, source_target_pairs={{0,24},{8,16},{16,8},{24,0},{1,25},{9,17},{17,9},{25,1},{2,26},{10... | collective-permute-start | bytes 221192 | tf_op jit(solution)/shard_map/ppermute | solution.py:700
  22.6 0.3 shard_map.100
  22.9 0.0 collective-permute-done.9.top_ref
  22.9 0.3 collective-permute-done.10.bot_ref
  23.2 4.6 %shard_map.101 = (f32[8,1,768,128]{3,2,1,0:T(8,128)S(1)}, f32[8,1,512,128]{3,2,1,0:T(8,128)S(1)}, f32[640,128]{1,0:T(8,128)S(1)}, f32[896,128]{1,0:T(8,128)S(1)}) custom-call(f32[1,512,128]{2,1,0:T(8,128)S(1)} %get-tuple-element.44.after.mid, f32[232,128]{1,0:T(8,128)S(1)} %collective-permute-done.9.top_ref, f32[232,128]{1,0:T(8,128)S(1)} %collective-permute-done.10.bot_ref, ...), custom_call_target="tpu_custom_call" | custom-call | tf_op jit(solution)/shard_map/pallas_call | solution.py:31
  27.8 0.0 collective-permute-done.6.refs_1_
  27.8 0.0 collective-permute-done.7.refs_2_
  27.8 0.3 collective-permute-done.8.refs_3_
  28.1 2.1 %shard_map.102.lag = f32[1,640,128]{2,1,0:T(8,128)S(1)} custom-call(f32[144,128]{1,0:T(8,128)S(1)} %get-tuple-element.49.refs_0_, f32[144,128]{1,0:T(8,128)S(1)} %collective-permute-done.6.refs_1_, f32[144,128]{1,0:T(8,128)S(1)} %collective-permute-done.7.refs_2_, f32[144,128]{1,0:T(8,128)S(1)} %collective-permute-done.8.refs_3_, ...), custom_call_target="tpu_custom_call" | custom-call | tf_op jit(solution)/shard_map/pallas_call | solution.py:31
  30.3 2.4 %shard_map.103 = (f32[160,128]{1,0:T(8,128)S(1)}, f32[160,128]{1,0:T(8,128)S(1)}, f32[160,128]{1,0:T(8,128)S(1)}, f32[160,128]{1,0:T(8,128)S(1)}) custom-call(f32[1,640,128]{2,1,0:T(8,128)S(1)} %shard_map.102.lag, f32[8,1,768,128]{3,2,1,0:T(8,128)S(1)} %get-tuple-element.61.hist, f32[8,1,512,128]{3,2,1,0:T(8,128)S(1)} %get-tuple-element.62.slope, ...), custom_call_target="tpu_custom_call" | custom-call | tf_op jit(solution)/shard_map/pallas_call | solution.py:31
  32.7 2.7 %collective-permute-start.11 = (f32[160,128]{1,0:T(8,128)S(1)}, f32[160,128]{1,0:T(8,128)S(1)}, u32[]{:S(2)}, u32[]{:S(2)}) collective-permute-start(f32[160,128]{1,0:T(8,128)S(1)} %get-tuple-element.65), channel_id=1, source_target_pairs={{0,24},{8,16},{16,8},{24,0},{1,25},{9,17},{17,9},{25,1},{2,26},{10... | collective-permute-start | bytes 245768 | tf_op jit(solution)/shard_map/ppermute | solution.py:700
  35.5 0.0 collective-permute-start.12
  35.5 1.7 %collective-permute-start.13 = (f32[160,128]{1,0:T(8,128)S(1)}, f32[160,128]{1,0:T(8,128)S(1)}, u32[]{:S(2)}, u32[]{:S(2)}) collective-permute-start(f32[160,128]{1,0:T(8,128)S(1)} %get-tuple-element.67), channel_id=1, source_target_pairs={{0,8},{8,0},{16,24},{24,16},{1,9},{9,1},{17,25},{25,17},{2,10},{10... | collective-permute-start | bytes 245768 | tf_op jit(solution)/shard_map/ppermute | solution.py:700
  37.2 2.6 %collective-permute-done.11.refs_1_ = f32[160,128]{1,0:T(8,128)S(1)} collective-permute-done((f32[160,128]{1,0:T(8,128)S(1)}, f32[160,128]{1,0:T(8,128)S(1)}, u32[]{:S(2)}, u32[]{:S(2)}) %collective-permute-start.11) | collective-permute-done | bytes 81952 | tf_op jit(solution)/shard_map/ppermute | solution.py:700
  39.7 1.8 %collective-permute-done.12.refs_2_ = f32[160,128]{1,0:T(8,128)S(1)} collective-permute-done((f32[160,128]{1,0:T(8,128)S(1)}, f32[160,128]{1,0:T(8,128)S(1)}, u32[]{:S(2)}, u32[]{:S(2)}) %collective-permute-start.12) | collective-permute-done | bytes 81952 | tf_op jit(solution)/shard_map/ppermute | solution.py:700
  41.6 0.0 collective-permute-done.13.refs_3_
  41.6 0.9 %shard_map.104 = (f32[128,256]{1,0:T(8,128)}, f32[128,256]{1,0:T(8,128)}, f32[64,256]{1,0:T(8,128)}) custom-call(f32[160,128]{1,0:T(8,128)S(1)} %get-tuple-element.64.refs_0_, f32[160,128]{1,0:T(8,128)S(1)} %collective-permute-done.11.refs_1_, f32[160,128]{1,0:T(8,128)S(1)} %collective-permute-done.12.refs_2_, f32[160,128]{1,0:T(8,128)S(1)} %collective-permute-done.13.refs_3_), custom_call_target="tpu_custom_call" | custom-call | tf_op jit(solution)/shard_map/pallas_call | solution.py:31
Async XLA Ops:
  1.7 1.8 %collective-permute-start = (f32[704,128]{1,0:T(8,128)S(1)}, f32[704,128]{1,0:T(8,128)S(1)}, u32[]{:S(2)}, u32[]{:S(2)}) collective-permute-start(f32[704,128]{1,0:T(8,128)S(1)} %shard_map.94.refs_7_), channel_id=1, source_target_pairs={{0,1},{1,0},{2,3},{3,2},{4,5},{5,4},{6,7},{7,6},{8,9},{9,8},{10,11... | collective-permute-start | bytes 1081352 | tf_op jit(solution)/shard_map/ppermute | solution.py:716
  3.7 9.7 %collective-permute-start.3 = (f32[128,128]{1,0:T(8,128)S(1)}, f32[128,128]{1,0:T(8,128)S(1)}, u32[]{:S(2)}, u32[]{:S(2)}) collective-permute-start(f32[128,128]{1,0:T(8,128)S(1)} %get-tuple-element.40), channel_id=1, source_target_pairs={{0,24},{8,16},{16,8},{24,0},{1,25},{9,17},{17,9},{25,1},{2,26},{10... | collective-permute-start | bytes 196616 | tf_op jit(solution)/shard_map/ppermute | solution.py:700
  8.8 5.9 %collective-permute-start.4 = (f32[128,128]{1,0:T(8,128)S(1)}, f32[128,128]{1,0:T(8,128)S(1)}, u32[]{:S(2)}, u32[]{:S(2)}) collective-permute-start(f32[128,128]{1,0:T(8,128)S(1)} %get-tuple-element.41), channel_id=1, source_target_pairs={{0,16},{8,24},{16,0},{24,8},{1,17},{9,25},{17,1},{25,9},{2,18},{10... | collective-permute-start | bytes 196616 | tf_op jit(solution)/shard_map/ppermute | solution.py:700
  8.8 5.9 %collective-permute-start.5 = (f32[128,128]{1,0:T(8,128)S(1)}, f32[128,128]{1,0:T(8,128)S(1)}, u32[]{:S(2)}, u32[]{:S(2)}) collective-permute-start(f32[128,128]{1,0:T(8,128)S(1)} %get-tuple-element.42), channel_id=1, source_target_pairs={{0,8},{8,0},{16,24},{24,16},{1,9},{9,1},{17,25},{25,17},{2,10},{10... | collective-permute-start | bytes 196616 | tf_op jit(solution)/shard_map/ppermute | solution.py:700
  10.2 7.6 %collective-permute-start.1 = (f32[120,128]{1,0:T(8,128)S(1)}, f32[120,128]{1,0:T(8,128)S(1)}, u32[]{:S(2)}, u32[]{:S(2)}) collective-permute-start(f32[120,128]{1,0:T(8,128)S(1)} %get-tuple-element.38), channel_id=1, source_target_pairs={{0,2},{2,0},{4,6},{6,4},{1,3},{3,1},{5,7},{7,5},{8,10},{10,8},{12,... | collective-permute-start | bytes 184328 | tf_op jit(solution)/shard_map/ppermute | solution.py:706
  11.9 5.9 %collective-permute-start.2 = (f32[120,128]{1,0:T(8,128)S(1)}, f32[120,128]{1,0:T(8,128)S(1)}, u32[]{:S(2)}, u32[]{:S(2)}) collective-permute-start(f32[120,128]{1,0:T(8,128)S(1)} %get-tuple-element.39), channel_id=1, source_target_pairs={{0,6},{2,4},{4,2},{6,0},{1,7},{3,5},{5,3},{7,1},{8,14},{10,12},{12... | collective-permute-start | bytes 184328 | tf_op jit(solution)/shard_map/ppermute | solution.py:707
  14.8 8.1 %collective-permute-start.9 = (f32[232,128]{1,0:T(8,128)S(1)}, f32[232,128]{1,0:T(8,128)S(1)}, u32[]{:S(2)}, u32[]{:S(2)}) collective-permute-start(f32[232,128]{1,0:T(8,128)S(1)} %get-tuple-element.56), channel_id=1, source_target_pairs={{0,2},{2,0},{4,6},{6,4},{1,3},{3,1},{5,7},{7,5},{8,10},{10,8},{12,... | collective-permute-start | bytes 356360 | tf_op jit(solution)/shard_map/ppermute | solution.py:706
  16.3 6.8 %collective-permute-start.10 = (f32[232,128]{1,0:T(8,128)S(1)}, f32[232,128]{1,0:T(8,128)S(1)}, u32[]{:S(2)}, u32[]{:S(2)}) collective-permute-start(f32[232,128]{1,0:T(8,128)S(1)} %get-tuple-element.57), channel_id=1, source_target_pairs={{0,6},{2,4},{4,2},{6,0},{1,7},{3,5},{5,3},{7,1},{8,14},{10,12},{12... | collective-permute-start | bytes 356360 | tf_op jit(solution)/shard_map/ppermute | solution.py:707
  18.1 9.7 %collective-permute-start.6 = (f32[144,128]{1,0:T(8,128)S(1)}, f32[144,128]{1,0:T(8,128)S(1)}, u32[]{:S(2)}, u32[]{:S(2)}) collective-permute-start(f32[144,128]{1,0:T(8,128)S(1)} %get-tuple-element.50), channel_id=1, source_target_pairs={{0,8},{8,0},{16,24},{24,16},{1,9},{9,1},{17,25},{25,17},{2,10},{10... | collective-permute-start | bytes 221192 | tf_op jit(solution)/shard_map/ppermute | solution.py:700
  19.3 8.5 %collective-permute-start.7 = (f32[144,128]{1,0:T(8,128)S(1)}, f32[144,128]{1,0:T(8,128)S(1)}, u32[]{:S(2)}, u32[]{:S(2)}) collective-permute-start(f32[144,128]{1,0:T(8,128)S(1)} %get-tuple-element.51), channel_id=1, source_target_pairs={{0,16},{8,24},{16,0},{24,8},{1,17},{9,25},{17,1},{25,9},{2,18},{10... | collective-permute-start | bytes 221192 | tf_op jit(solution)/shard_map/ppermute | solution.py:700
  22.0 6.2 %collective-permute-start.8 = (f32[144,128]{1,0:T(8,128)S(1)}, f32[144,128]{1,0:T(8,128)S(1)}, u32[]{:S(2)}, u32[]{:S(2)}) collective-permute-start(f32[144,128]{1,0:T(8,128)S(1)} %get-tuple-element.52), channel_id=1, source_target_pairs={{0,24},{8,16},{16,8},{24,0},{1,25},{9,17},{17,9},{25,1},{2,26},{10... | collective-permute-start | bytes 221192 | tf_op jit(solution)/shard_map/ppermute | solution.py:700
  32.7 7.0 %collective-permute-start.11 = (f32[160,128]{1,0:T(8,128)S(1)}, f32[160,128]{1,0:T(8,128)S(1)}, u32[]{:S(2)}, u32[]{:S(2)}) collective-permute-start(f32[160,128]{1,0:T(8,128)S(1)} %get-tuple-element.65), channel_id=1, source_target_pairs={{0,24},{8,16},{16,8},{24,0},{1,25},{9,17},{17,9},{25,1},{2,26},{10... | collective-permute-start | bytes 245768 | tf_op jit(solution)/shard_map/ppermute | solution.py:700
  35.5 6.1 %collective-permute-start.12 = (f32[160,128]{1,0:T(8,128)S(1)}, f32[160,128]{1,0:T(8,128)S(1)}, u32[]{:S(2)}, u32[]{:S(2)}) collective-permute-start(f32[160,128]{1,0:T(8,128)S(1)} %get-tuple-element.66), channel_id=1, source_target_pairs={{0,16},{8,24},{16,0},{24,8},{1,17},{9,25},{17,1},{25,9},{2,18},{10... | collective-permute-start | bytes 245768 | tf_op jit(solution)/shard_map/ppermute | solution.py:700
  35.5 6.1 %collective-permute-start.13 = (f32[160,128]{1,0:T(8,128)S(1)}, f32[160,128]{1,0:T(8,128)S(1)}, u32[]{:S(2)}, u32[]{:S(2)}) collective-permute-start(f32[160,128]{1,0:T(8,128)S(1)} %get-tuple-element.67), channel_id=1, source_target_pairs={{0,8},{8,0},{16,24},{24,16},{1,9},{9,1},{17,25},{25,17},{2,10},{10... | collective-permute-start | bytes 245768 | tf_op jit(solution)/shard_map/ppermute | solution.py:700

commit v7 on v6

--- a/solution.py
+++ b/solution.py
@@ -19,8 +19,6 @@
 HALO_W = 2 * STEPS
 SIDE = 32
 BLOCK = 8
-PARTS = (0, STEPS // 2)
-TURNS = STEPS // (2 * len(PARTS))
 
 VMEM_SPEC = pl.BlockSpec(memory_space=pltpu.VMEM)
 HBM_SPEC = pl.BlockSpec(memory_space=pltpu.HBM)
@@ -345,17 +343,14 @@
 
 
 def sweep(groups, one, two, lo, hi, coefs):
-    for cut in PARTS:
-
-        def turn(t, carry, a=lo + cut, b=hi - cut):
-            def run(g):
-                step(one.at[g], two.at[g], a, b, coefs)
-                step(two.at[g], one.at[g], a, b, coefs)
-
-            each_group(groups, run)
-            return carry
-
-        lax.fori_loop(0, TURNS, turn, 0)
+    for n in range(STEPS):
+        src, dst = (two, one) if n % 2 else (one, two)
+        each_group(
+            groups,
+            lambda g, src=src, dst=dst, n=n: step(
+                src.at[g], dst.at[g], lo + n // 2 * 2, hi - n // 2 * 2, coefs
+            ),
+        )
 
 
 def coarse(gd, cx, value, a, b):
@@ -460,26 +455,20 @@
 
         through_groups(groups, chain, jnp.zeros(((b - a) * SUB, LANES), jnp.float32))
 
-    for i, cut in enumerate(PARTS):
-
-        def forward(turn, carry, base=2 * TURNS * i, cut=cut):
-            def run(g):
-                for k, (src, dst) in enumerate(((two, one), (one, two))):
-                    t = base + 2 * turn + k
-
-                    def seen(a, b, before, here, east, new, t=t):
-                        hist[t, g, (a - lo) * SUB : (b - lo) * SUB, :] = here
-                        p, q = max(a, HALO), min(b, HALO + tile_rows)
-                        if p < q:
-                            rise = (east - here)[(p - a) * SUB : (q - a) * SUB]
-                            slope[t, g, (p - HALO) * SUB : (q - HALO) * SUB, :] = rise
-
-                    step(src.at[g], dst.at[g], lo + cut, hi - cut, coefs, seen)
-
-            each_group(groups, run)
-            return carry
-
-        lax.fori_loop(0, TURNS, forward, 0)
+    for t in range(STEPS):
+        src, dst = (one, two) if t % 2 else (two, one)
+
+        def run(g, src=src, dst=dst, t=t):
+            def seen(a, b, before, here, east, new):
+                hist[t, g, (a - lo) * SUB : (b - lo) * SUB, :] = here
+                p, q = max(a, HALO), min(b, HALO + tile_rows)
+                if p < q:
+                    rise = (east - here)[(p - a) * SUB : (q - a) * SUB]
+                    slope[t, g, (p - HALO) * SUB : (q - HALO) * SUB, :] = rise
+
+            step(src.at[g], dst.at[g], lo + t // 2 * 2, hi - t // 2 * 2, coefs, seen)
+
+        each_group(groups, run)
     w_lo, w_hi = 2 * STEPS, total - 2 * STEPS
     last_ref[...] = at_rows(two.at[groups - 1], w_lo, w_hi) - at_rows(tg, w_lo, w_hi)
 
@@ -602,23 +591,15 @@
             lambda a, b, before, here, east, new: products(t, g, a, b, before, here, east),
         )
 
-    def back(turn, carry):
-        t = STEPS - 1 - 2 * turn
-
-        def run(g):
-            back_step(two, one, t, g, 0)
-            back_step(one, two, t - 1, g, 0)
-
-        each_group(groups, run)
-        return carry
-
-    lax.fori_loop(0, TURNS, back, 0)
+    for t in range(STEPS - 1, 0, -1):
+        src, dst = (two, one) if t % 2 else (one, two)
+        cut = (STEPS - 1 - t) // 2 * 2
+        each_group(
+            groups,
+            lambda g, src=src, dst=dst, t=t, cut=cut: back_step(src, dst, t, g, cut),
+        )
 
     def finish(g):
-        cut = 2 * TURNS
-        for t in range(STEPS - 1 - cut, 0, -1):
-            src, dst = (two, one) if t % 2 else (one, two)
-            back_step(src, dst, t, g, cut)
         for a, b in blocks(HALO, end + 1):
             rows = at_rows(one.at[g], a - 1, b)
             here = rows[SUB:]

time: 42.7 us -> 41.5 us (0.972)
  Pallas kernels: 14.1 us -> 12.7 us
    pallas_call x11, Pallas kernels: 14.1 us -> 12.7 us  [run(): pl.pallas_call(body, out_shape=[jax.ShapeDtypeStruct(s, jnp.float32) for...]
  transfers between devices with their start and end apart: 14 -> 14, of which waited for: 5 -> 5; matrix products, arithmetic and copies ran while one was open for 0% -> 0% of each run, Pallas kernels for 17% -> 16%
where the time goes in v7:
time: 41.5 us; the launch traced here: 41.3 us
  starting transfers between devices  21.3 us (51%)
  Pallas kernels  12.7 us (31%)
  waiting for transfers between devices  6.54 us (16%)
  between operations  0.73 us (2%)
    ppermute x9, starting transfers between devices, exchanged(): lax.ppermute(parts[d], 'tm', [(i, i ^ d) for i in range(count)])  14.5 us
    pallas_call x11, Pallas kernels, run(): pl.pallas_call(body, out_shape=[jax.ShapeDtypeStruct(s, jnp.float32) for...  12.7 us
    ppermute x9, waiting for transfers between devices, exchanged(): lax.ppermute(parts[d], 'tm', [(i, i ^ d) for i in range(count)])  6.23 us
    ppermute x2, starting transfers between devices, turned(): lax.ppermute(first, 'sx', [(i, i ^ 1) for i in range(n)])  3.26 us
    ppermute x2, starting transfers between devices, turned(): lax.ppermute(second, 'sx', [(i, (i + (1 if i % 2 else n - 1)) % n) for i...  2.98 us
  transfers between devices with their start and end apart: 14, of which 5 were waited for; matrix products, arithmetic and copies ran while one was open for 0% of the time, Pallas kernels for 16%

profile of v7, /device:TPU:0, one launch (start us, length us, event | category | flops | bytes accessed | tf_op | source)
XLA Modules:
  0.0 41.3 jit_solution(4609814536307360694)
XLA Ops:
  0.6 1.1 %shard_map.94.refs_7_ = f32[704,128]{1,0:T(8,128)S(1)} custom-call(f32[128,256]{1,0:T(8,128)} %bitcast.6, f32[128,256]{1,0:T(8,128)} %bitcast.8, f32[64,256]{1,0:T(8,128)} %refs_2_.3, f32[64,256]{1,0:T(8,128)} %refs_3_.3, f32[64,256]{1,0:T(8,128)} %refs_4_.3, f32[128,256]{1,0:T(8,128)} %bitcast.10, f32[128,256]{1,0:T(8,128)} %bitcast.12), custom_call_target="tpu_custom_call" | custom-call | tf_op jit(solution)/shard_map/pallas_call | solution.py:29
  1.7 0.5 %collective-permute-start = (f32[704,128]{1,0:T(8,128)S(1)}, f32[704,128]{1,0:T(8,128)S(1)}, u32[]{:S(2)}, u32[]{:S(2)}) collective-permute-start(f32[704,128]{1,0:T(8,128)S(1)} %shard_map.94.refs_7_), channel_id=1, source_target_pairs={{0,1},{1,0},{2,3},{3,2},{4,5},{5,4},{6,7},{7,6},{8,9},{9,8},{10,11... | collective-permute-start | bytes 1081352 | tf_op jit(solution)/shard_map/ppermute | solution.py:697
  2.2 1.3 %shard_map.95.tile_ref = f32[704,256]{1,0:T(8,128)S(1)} custom-call(f32[128,256]{1,0:T(8,128)} %bitcast.7, f32[128,256]{1,0:T(8,128)} %bitcast.9, f32[64,256]{1,0:T(8,128)} %refs_2_.3, f32[64,256]{1,0:T(8,128)} %refs_3_.3, f32[64,256]{1,0:T(8,128)} %refs_4_.3, f32[128,256]{1,0:T(8,128)} %bitcast.11, f32[128,256]{1,0:T(8,128)} %bitcast.13, ...), custom_call_target="tpu_custom_call" | custom-call | tf_op jit(solution)/shard_map/pallas_call | solution.py:29
  3.5 0.0 collective-permute-done.strip_ref
  3.5 0.2 shard_map.96
  3.7 5.0 %collective-permute-start.3 = (f32[128,128]{1,0:T(8,128)S(1)}, f32[128,128]{1,0:T(8,128)S(1)}, u32[]{:S(2)}, u32[]{:S(2)}) collective-permute-start(f32[128,128]{1,0:T(8,128)S(1)} %get-tuple-element.40), channel_id=1, source_target_pairs={{0,24},{8,16},{16,8},{24,0},{1,25},{9,17},{17,9},{25,1},{2,26},{10... | collective-permute-start | bytes 196616 | tf_op jit(solution)/shard_map/ppermute | solution.py:681
  8.8 0.0 collective-permute-start.4
  8.8 0.6 %collective-permute-start.5 = (f32[128,128]{1,0:T(8,128)S(1)}, f32[128,128]{1,0:T(8,128)S(1)}, u32[]{:S(2)}, u32[]{:S(2)}) collective-permute-start(f32[128,128]{1,0:T(8,128)S(1)} %get-tuple-element.42), channel_id=1, source_target_pairs={{0,8},{8,0},{16,24},{24,16},{1,9},{9,1},{17,25},{25,17},{2,10},{10... | collective-permute-start | bytes 196616 | tf_op jit(solution)/shard_map/ppermute | solution.py:681
  9.4 0.8 %shard_map.97 = (f32[144,128]{1,0:T(8,128)S(1)}, f32[144,128]{1,0:T(8,128)S(1)}, f32[144,128]{1,0:T(8,128)S(1)}, f32[144,128]{1,0:T(8,128)S(1)}, f32[448,128]{1,...) custom-call(f32[704,256]{1,0:T(8,128)S(1)} %shard_map.95.tile_ref, ...), custom_call_target="tpu_custom_call" | custom-call | tf_op jit(solution)/shard_map/pallas_call | solution.py:29
  10.2 1.7 %collective-permute-start.1 = (f32[120,128]{1,0:T(8,128)S(1)}, f32[120,128]{1,0:T(8,128)S(1)}, u32[]{:S(2)}, u32[]{:S(2)}) collective-permute-start(f32[120,128]{1,0:T(8,128)S(1)} %get-tuple-element.38), channel_id=1, source_target_pairs={{0,2},{2,0},{4,6},{6,4},{1,3},{3,1},{5,7},{7,5},{8,10},{10,8},{12,... | collective-permute-start | bytes 184328 | tf_op jit(solution)/shard_map/ppermute | solution.py:687
  11.9 1.5 %collective-permute-start.2 = (f32[120,128]{1,0:T(8,128)S(1)}, f32[120,128]{1,0:T(8,128)S(1)}, u32[]{:S(2)}, u32[]{:S(2)}) collective-permute-start(f32[120,128]{1,0:T(8,128)S(1)} %get-tuple-element.39), channel_id=1, source_target_pairs={{0,6},{2,4},{4,2},{6,0},{1,7},{3,5},{5,3},{7,1},{8,14},{10,12},{12... | collective-permute-start | bytes 184328 | tf_op jit(solution)/shard_map/ppermute | solution.py:688
  13.4 0.0 collective-permute-done.3.refs_1_
  13.4 1.3 %collective-permute-done.4.refs_2_ = f32[128,128]{1,0:T(8,128)S(1)} collective-permute-done((f32[128,128]{1,0:T(8,128)S(1)}, f32[128,128]{1,0:T(8,128)S(1)}, u32[]{:S(2)}, u32[]{:S(2)}) %collective-permute-start.4) | collective-permute-done | bytes 65568 | tf_op jit(solution)/shard_map/ppermute | solution.py:681
  14.7 0.0 collective-permute-done.5.refs_3_
  14.7 0.1 shard_map.98
  14.8 1.6 %collective-permute-start.9 = (f32[232,128]{1,0:T(8,128)S(1)}, f32[232,128]{1,0:T(8,128)S(1)}, u32[]{:S(2)}, u32[]{:S(2)}) collective-permute-start(f32[232,128]{1,0:T(8,128)S(1)} %get-tuple-element.56), channel_id=1, source_target_pairs={{0,2},{2,0},{4,6},{6,4},{1,3},{3,1},{5,7},{7,5},{8,10},{10,8},{12,... | collective-permute-start | bytes 356360 | tf_op jit(solution)/shard_map/ppermute | solution.py:687
  16.3 1.5 %collective-permute-start.10 = (f32[232,128]{1,0:T(8,128)S(1)}, f32[232,128]{1,0:T(8,128)S(1)}, u32[]{:S(2)}, u32[]{:S(2)}) collective-permute-start(f32[232,128]{1,0:T(8,128)S(1)} %get-tuple-element.57), channel_id=1, source_target_pairs={{0,6},{2,4},{4,2},{6,0},{1,7},{3,5},{5,3},{7,1},{8,14},{10,12},{12... | collective-permute-start | bytes 356360 | tf_op jit(solution)/shard_map/ppermute | solution.py:688
  17.8 0.0 collective-permute-done.1.top_ref
  17.8 0.0 collective-permute-done.2.bot_ref
  17.8 0.3 shard_map.99
  18.1 1.2 %collective-permute-start.6 = (f32[144,128]{1,0:T(8,128)S(1)}, f32[144,128]{1,0:T(8,128)S(1)}, u32[]{:S(2)}, u32[]{:S(2)}) collective-permute-start(f32[144,128]{1,0:T(8,128)S(1)} %get-tuple-element.50), channel_id=1, source_target_pairs={{0,8},{8,0},{16,24},{24,16},{1,9},{9,1},{17,25},{25,17},{2,10},{10... | collective-permute-start | bytes 221192 | tf_op jit(solution)/shard_map/ppermute | solution.py:681
  19.3 2.7 %collective-permute-start.7 = (f32[144,128]{1,0:T(8,128)S(1)}, f32[144,128]{1,0:T(8,128)S(1)}, u32[]{:S(2)}, u32[]{:S(2)}) collective-permute-start(f32[144,128]{1,0:T(8,128)S(1)} %get-tuple-element.51), channel_id=1, source_target_pairs={{0,16},{8,24},{16,0},{24,8},{1,17},{9,25},{17,1},{25,9},{2,18},{10... | collective-permute-start | bytes 221192 | tf_op jit(solution)/shard_map/ppermute | solution.py:681
  22.0 0.6 %collective-permute-start.8 = (f32[144,128]{1,0:T(8,128)S(1)}, f32[144,128]{1,0:T(8,128)S(1)}, u32[]{:S(2)}, u32[]{:S(2)}) collective-permute-start(f32[144,128]{1,0:T(8,128)S(1)} %get-tuple-element.52), channel_id=1, source_target_pairs={{0,24},{8,16},{16,8},{24,0},{1,25},{9,17},{17,9},{25,1},{2,26},{10... | collective-permute-start | bytes 221192 | tf_op jit(solution)/shard_map/ppermute | solution.py:681
  22.6 0.3 shard_map.100
  22.9 0.0 collective-permute-done.9.top_ref
  22.9 0.3 collective-permute-done.10.bot_ref
  23.2 3.8 %shard_map.101 = (f32[8,1,768,128]{3,2,1,0:T(8,128)S(1)}, f32[8,1,512,128]{3,2,1,0:T(8,128)S(1)}, f32[640,128]{1,0:T(8,128)S(1)}, f32[896,128]{1,0:T(8,128)S(1)}) custom-call(f32[1,512,128]{2,1,0:T(8,128)S(1)} %get-tuple-element.44.after.mid, f32[232,128]{1,0:T(8,128)S(1)} %collective-permute-done.9.top_ref, f32[232,128]{1,0:T(8,128)S(1)} %collective-permute-done.10.bot_ref, ...), custom_call_target="tpu_custom_call" | custom-call | tf_op jit(solution)/shard_map/pallas_call | solution.py:29
  26.9 0.0 collective-permute-done.6.refs_1_
  26.9 0.0 collective-permute-done.7.refs_2_
  26.9 1.2 %collective-permute-done.8.refs_3_ = f32[144,128]{1,0:T(8,128)S(1)} collective-permute-done((f32[144,128]{1,0:T(8,128)S(1)}, f32[144,128]{1,0:T(8,128)S(1)}, u32[]{:S(2)}, u32[]{:S(2)}) %collective-permute-start.8) | collective-permute-done | bytes 73760 | tf_op jit(solution)/shard_map/ppermute | solution.py:681
  28.1 1.8 %shard_map.102.lag = f32[1,640,128]{2,1,0:T(8,128)S(1)} custom-call(f32[144,128]{1,0:T(8,128)S(1)} %get-tuple-element.49.refs_0_, f32[144,128]{1,0:T(8,128)S(1)} %collective-permute-done.6.refs_1_, f32[144,128]{1,0:T(8,128)S(1)} %collective-permute-done.7.refs_2_, f32[144,128]{1,0:T(8,128)S(1)} %collective-permute-done.8.refs_3_, ...), custom_call_target="tpu_custom_call" | custom-call | tf_op jit(solution)/shard_map/pallas_call | solution.py:29
  30.0 2.2 %shard_map.103 = (f32[160,128]{1,0:T(8,128)S(1)}, f32[160,128]{1,0:T(8,128)S(1)}, f32[160,128]{1,0:T(8,128)S(1)}, f32[160,128]{1,0:T(8,128)S(1)}) custom-call(f32[1,640,128]{2,1,0:T(8,128)S(1)} %shard_map.102.lag, f32[8,1,768,128]{3,2,1,0:T(8,128)S(1)} %get-tuple-element.61.hist, f32[8,1,512,128]{3,2,1,0:T(8,128)S(1)} %get-tuple-element.62.slope, ...), custom_call_target="tpu_custom_call" | custom-call | tf_op jit(solution)/shard_map/pallas_call | solution.py:29
  32.2 1.8 %collective-permute-start.11 = (f32[160,128]{1,0:T(8,128)S(1)}, f32[160,128]{1,0:T(8,128)S(1)}, u32[]{:S(2)}, u32[]{:S(2)}) collective-permute-start(f32[160,128]{1,0:T(8,128)S(1)} %get-tuple-element.65), channel_id=1, source_target_pairs={{0,24},{8,16},{16,8},{24,0},{1,25},{9,17},{17,9},{25,1},{2,26},{10... | collective-permute-start | bytes 245768 | tf_op jit(solution)/shard_map/ppermute | solution.py:681
  34.0 0.0 collective-permute-start.12
  34.0 2.6 %collective-permute-start.13 = (f32[160,128]{1,0:T(8,128)S(1)}, f32[160,128]{1,0:T(8,128)S(1)}, u32[]{:S(2)}, u32[]{:S(2)}) collective-permute-start(f32[160,128]{1,0:T(8,128)S(1)} %get-tuple-element.67), channel_id=1, source_target_pairs={{0,8},{8,0},{16,24},{24,16},{1,9},{9,1},{17,25},{25,17},{2,10},{10... | collective-permute-start | bytes 245768 | tf_op jit(solution)/shard_map/ppermute | solution.py:681
  36.6 2.1 %collective-permute-done.11.refs_1_ = f32[160,128]{1,0:T(8,128)S(1)} collective-permute-done((f32[160,128]{1,0:T(8,128)S(1)}, f32[160,128]{1,0:T(8,128)S(1)}, u32[]{:S(2)}, u32[]{:S(2)}) %collective-permute-start.11) | collective-permute-done | bytes 81952 | tf_op jit(solution)/shard_map/ppermute | solution.py:681
  38.7 1.7 %collective-permute-done.12.refs_2_ = f32[160,128]{1,0:T(8,128)S(1)} collective-permute-done((f32[160,128]{1,0:T(8,128)S(1)}, f32[160,128]{1,0:T(8,128)S(1)}, u32[]{:S(2)}, u32[]{:S(2)}) %collective-permute-start.12) | collective-permute-done | bytes 81952 | tf_op jit(solution)/shard_map/ppermute | solution.py:681
  40.4 0.0 collective-permute-done.13.refs_3_
  40.4 0.9 %shard_map.104 = (f32[128,256]{1,0:T(8,128)}, f32[128,256]{1,0:T(8,128)}, f32[64,256]{1,0:T(8,128)}) custom-call(f32[160,128]{1,0:T(8,128)S(1)} %get-tuple-element.64.refs_0_, f32[160,128]{1,0:T(8,128)S(1)} %collective-permute-done.11.refs_1_, f32[160,128]{1,0:T(8,128)S(1)} %collective-permute-done.12.refs_2_, f32[160,128]{1,0:T(8,128)S(1)} %collective-permute-done.13.refs_3_), custom_call_target="tpu_custom_call" | custom-call | tf_op jit(solution)/shard_map/pallas_call | solution.py:29
Async XLA Ops:
  1.7 1.8 %collective-permute-start = (f32[704,128]{1,0:T(8,128)S(1)}, f32[704,128]{1,0:T(8,128)S(1)}, u32[]{:S(2)}, u32[]{:S(2)}) collective-permute-start(f32[704,128]{1,0:T(8,128)S(1)} %shard_map.94.refs_7_), channel_id=1, source_target_pairs={{0,1},{1,0},{2,3},{3,2},{4,5},{5,4},{6,7},{7,6},{8,9},{9,8},{10,11... | collective-permute-start | bytes 1081352 | tf_op jit(solution)/shard_map/ppermute | solution.py:697
  3.7 9.7 %collective-permute-start.3 = (f32[128,128]{1,0:T(8,128)S(1)}, f32[128,128]{1,0:T(8,128)S(1)}, u32[]{:S(2)}, u32[]{:S(2)}) collective-permute-start(f32[128,128]{1,0:T(8,128)S(1)} %get-tuple-element.40), channel_id=1, source_target_pairs={{0,24},{8,16},{16,8},{24,0},{1,25},{9,17},{17,9},{25,1},{2,26},{10... | collective-permute-start | bytes 196616 | tf_op jit(solution)/shard_map/ppermute | solution.py:681
  8.8 5.9 %collective-permute-start.4 = (f32[128,128]{1,0:T(8,128)S(1)}, f32[128,128]{1,0:T(8,128)S(1)}, u32[]{:S(2)}, u32[]{:S(2)}) collective-permute-start(f32[128,128]{1,0:T(8,128)S(1)} %get-tuple-element.41), channel_id=1, source_target_pairs={{0,16},{8,24},{16,0},{24,8},{1,17},{9,25},{17,1},{25,9},{2,18},{10... | collective-permute-start | bytes 196616 | tf_op jit(solution)/shard_map/ppermute | solution.py:681
  8.8 5.9 %collective-permute-start.5 = (f32[128,128]{1,0:T(8,128)S(1)}, f32[128,128]{1,0:T(8,128)S(1)}, u32[]{:S(2)}, u32[]{:S(2)}) collective-permute-start(f32[128,128]{1,0:T(8,128)S(1)} %get-tuple-element.42), channel_id=1, source_target_pairs={{0,8},{8,0},{16,24},{24,16},{1,9},{9,1},{17,25},{25,17},{2,10},{10... | collective-permute-start | bytes 196616 | tf_op jit(solution)/shard_map/ppermute | solution.py:681
  10.2 7.6 %collective-permute-start.1 = (f32[120,128]{1,0:T(8,128)S(1)}, f32[120,128]{1,0:T(8,128)S(1)}, u32[]{:S(2)}, u32[]{:S(2)}) collective-permute-start(f32[120,128]{1,0:T(8,128)S(1)} %get-tuple-element.38), channel_id=1, source_target_pairs={{0,2},{2,0},{4,6},{6,4},{1,3},{3,1},{5,7},{7,5},{8,10},{10,8},{12,... | collective-permute-start | bytes 184328 | tf_op jit(solution)/shard_map/ppermute | solution.py:687
  11.9 5.9 %collective-permute-start.2 = (f32[120,128]{1,0:T(8,128)S(1)}, f32[120,128]{1,0:T(8,128)S(1)}, u32[]{:S(2)}, u32[]{:S(2)}) collective-permute-start(f32[120,128]{1,0:T(8,128)S(1)} %get-tuple-element.39), channel_id=1, source_target_pairs={{0,6},{2,4},{4,2},{6,0},{1,7},{3,5},{5,3},{7,1},{8,14},{10,12},{12... | collective-permute-start | bytes 184328 | tf_op jit(solution)/shard_map/ppermute | solution.py:688
  14.8 8.1 %collective-permute-start.9 = (f32[232,128]{1,0:T(8,128)S(1)}, f32[232,128]{1,0:T(8,128)S(1)}, u32[]{:S(2)}, u32[]{:S(2)}) collective-permute-start(f32[232,128]{1,0:T(8,128)S(1)} %get-tuple-element.56), channel_id=1, source_target_pairs={{0,2},{2,0},{4,6},{6,4},{1,3},{3,1},{5,7},{7,5},{8,10},{10,8},{12,... | collective-permute-start | bytes 356360 | tf_op jit(solution)/shard_map/ppermute | solution.py:687
  16.3 6.8 %collective-permute-start.10 = (f32[232,128]{1,0:T(8,128)S(1)}, f32[232,128]{1,0:T(8,128)S(1)}, u32[]{:S(2)}, u32[]{:S(2)}) collective-permute-start(f32[232,128]{1,0:T(8,128)S(1)} %get-tuple-element.57), channel_id=1, source_target_pairs={{0,6},{2,4},{4,2},{6,0},{1,7},{3,5},{5,3},{7,1},{8,14},{10,12},{12... | collective-permute-start | bytes 356360 | tf_op jit(solution)/shard_map/ppermute | solution.py:688
  18.1 8.8 %collective-permute-start.6 = (f32[144,128]{1,0:T(8,128)S(1)}, f32[144,128]{1,0:T(8,128)S(1)}, u32[]{:S(2)}, u32[]{:S(2)}) collective-permute-start(f32[144,128]{1,0:T(8,128)S(1)} %get-tuple-element.50), channel_id=1, source_target_pairs={{0,8},{8,0},{16,24},{24,16},{1,9},{9,1},{17,25},{25,17},{2,10},{10... | collective-permute-start | bytes 221192 | tf_op jit(solution)/shard_map/ppermute | solution.py:681
  19.3 7.6 %collective-permute-start.7 = (f32[144,128]{1,0:T(8,128)S(1)}, f32[144,128]{1,0:T(8,128)S(1)}, u32[]{:S(2)}, u32[]{:S(2)}) collective-permute-start(f32[144,128]{1,0:T(8,128)S(1)} %get-tuple-element.51), channel_id=1, source_target_pairs={{0,16},{8,24},{16,0},{24,8},{1,17},{9,25},{17,1},{25,9},{2,18},{10... | collective-permute-start | bytes 221192 | tf_op jit(solution)/shard_map/ppermute | solution.py:681
  22.0 6.2 %collective-permute-start.8 = (f32[144,128]{1,0:T(8,128)S(1)}, f32[144,128]{1,0:T(8,128)S(1)}, u32[]{:S(2)}, u32[]{:S(2)}) collective-permute-start(f32[144,128]{1,0:T(8,128)S(1)} %get-tuple-element.52), channel_id=1, source_target_pairs={{0,24},{8,16},{16,8},{24,0},{1,25},{9,17},{17,9},{25,1},{2,26},{10... | collective-permute-start | bytes 221192 | tf_op jit(solution)/shard_map/ppermute | solution.py:681
  32.2 6.5 %collective-permute-start.11 = (f32[160,128]{1,0:T(8,128)S(1)}, f32[160,128]{1,0:T(8,128)S(1)}, u32[]{:S(2)}, u32[]{:S(2)}) collective-permute-start(f32[160,128]{1,0:T(8,128)S(1)} %get-tuple-element.65), channel_id=1, source_target_pairs={{0,24},{8,16},{16,8},{24,0},{1,25},{9,17},{17,9},{25,1},{2,26},{10... | collective-permute-start | bytes 245768 | tf_op jit(solution)/shard_map/ppermute | solution.py:681
  34.0 6.4 %collective-permute-start.12 = (f32[160,128]{1,0:T(8,128)S(1)}, f32[160,128]{1,0:T(8,128)S(1)}, u32[]{:S(2)}, u32[]{:S(2)}) collective-permute-start(f32[160,128]{1,0:T(8,128)S(1)} %get-tuple-element.66), channel_id=1, source_target_pairs={{0,16},{8,24},{16,0},{24,8},{1,17},{9,25},{17,1},{25,9},{2,18},{10... | collective-permute-start | bytes 245768 | tf_op jit(solution)/shard_map/ppermute | solution.py:681
  34.0 6.4 %collective-permute-start.13 = (f32[160,128]{1,0:T(8,128)S(1)}, f32[160,128]{1,0:T(8,128)S(1)}, u32[]{:S(2)}, u32[]{:S(2)}) collective-permute-start(f32[160,128]{1,0:T(8,128)S(1)} %get-tuple-element.67), channel_id=1, source_target_pairs={{0,8},{8,0},{16,24},{24,16},{1,9},{9,1},{17,25},{25,17},{2,10},{10... | collective-permute-start | bytes 245768 | tf_op jit(solution)/shard_map/ppermute | solution.py:681
